TPU v7x, 32 devices: a whole 2x2x4 slice. The times are simulated.
32 devices in a mesh: wide: 4 (over z), band: 8 (over y, x, core).
Axes of the slice: x: 2, y: 2, z: 4, core: 2. Of those that a mesh axis runs over, the one named last changes fastest.
Arguments:
- day_field: float32 [64, 128, 512], P('wide', 'band'), may hold values from -6 to 6
- obs_mask: int32 [64, 128, 512], P(None, 'band', 'wide'), may hold values 0 or 1
- ocean_mask: int32 [128, 512], P('band', 'wide'), may hold values 0 or 1
- diffusivity: float32 [128, 512], P('band', 'wide'), may hold values from 0.05 to 0.24
- start_modes: float32 [64, 48], replicated, may hold values from -6 to 6
Outputs:
- filled: float32 [64, 128, 512], P(None, 'band', 'wide')
- mode_basis: float32 [64, 48], replicated
All inputs are finite; a program needn't handle non-finite values. No bound on the sum of `obs_mask` or of `ocean_mask` on one device may be relied on, other than what follows from the above.
Results may differ from a plain program's by a relative error of at most 0.00024.
Values sent between devices are 32-bit elements; how exact they have to be, the bound alone decides.
No kernel may reach another device: no remote copies, remote signals or barrier semaphores. Data moves between devices by JAX's collectives and lax.ppermute only.
A program may use at most 64 MiB of HBM per device.

v0:
```python
import jax
import jax.numpy as jnp
from jax import lax
from jax.sharding import PartitionSpec as P

OUTER = 3
INNER = 3
PASSES = 3


def extended(cells, sides, width, closed):
    for axis, dim in sides:
        count = lax.axis_size(axis)
        ends = count if closed else count - 1
        head = lax.slice_in_dim(cells, 0, width, axis=dim)
        tail = lax.slice_in_dim(cells, cells.shape[dim] - width, cells.shape[dim], axis=dim)
        cells = jnp.concatenate(
            [
                lax.ppermute(tail, axis, [(i, (i + 1) % count) for i in range(ends)]),
                cells,
                lax.ppermute(head, axis, [((i + 1) % count, i) for i in range(ends)]),
            ],
            axis=dim,
        )
    return cells


def orthonormal(coeff):
    gram_matrix = jnp.dot(
        coeff.T, coeff, precision=lax.Precision.HIGHEST, preferred_element_type=jnp.float32
    )
    factor = jnp.linalg.cholesky(gram_matrix)
    return jax.scipy.linalg.solve_triangular(factor, coeff.T, lower=True).T


def contract_pixels(left, right):
    return lax.dot_general(
        left,
        right,
        (((1,), (1,)), ((), ())),
        precision=lax.Precision.HIGHEST,
        preferred_element_type=jnp.float32,
    )


def smooth_each(filled, gap_coef):
    rows_ext = extended(filled, (("band", 1),), 1, False)
    cols_ext = extended(filled, (("wide", 2),), 1, True)
    laplacian = (
        rows_ext[:, 2:] + rows_ext[:, :-2] + cols_ext[:, :, 2:] + cols_ext[:, :, :-2] - 4.0 * filled
    )
    return filled + gap_coef * laplacian


def shards(day_field, obs_mask, ocean_mask, diffusivity, start_modes):
    regrouped = lax.all_to_all(day_field, "wide", split_axis=2, concat_axis=0, tiled=True)
    ocean_wide = ocean_mask[None]
    valid = (obs_mask * ocean_wide).astype(jnp.float32)
    gap_weight = ((1 - obs_mask) * ocean_wide).astype(jnp.float32)
    gap_coef = diffusivity[None] * gap_weight
    observed = regrouped * valid
    mode_basis = orthonormal(start_modes)
    filled = observed
    day_count = observed.shape[0]
    for outer_step in range(OUTER):
        flat_field = filled.reshape(day_count, -1)
        covariance = lax.psum(contract_pixels(flat_field, flat_field), ("wide", "band"))
        for inner_step in range(INNER):
            mode_basis = orthonormal(
                jnp.dot(
                    covariance,
                    mode_basis,
                    precision=lax.Precision.HIGHEST,
                    preferred_element_type=jnp.float32,
                )
            )
        projected = jnp.dot(
            mode_basis.T,
            flat_field,
            precision=lax.Precision.HIGHEST,
            preferred_element_type=jnp.float32,
        )
        recon = jnp.dot(
            mode_basis,
            projected,
            precision=lax.Precision.HIGHEST,
            preferred_element_type=jnp.float32,
        )
        filled = observed + gap_weight * recon.reshape(filled.shape)
        for pass_index in range(PASSES):
            filled = smooth_each(filled, gap_coef)
    return (filled, mode_basis)


def solution(mesh):
    placed = (
        P("wide", "band", None),
        P(None, "band", "wide"),
        P("band", "wide"),
        P("band", "wide"),
        P(),
    )
    return jax.shard_map(
        shards,
        mesh=mesh,
        in_specs=placed,
        out_specs=(P(None, "band", "wide"), P()),
        check_vma=False,
    )
```

profile of v0, /device:TPU:0, one launch (start us, length us, event | category | flops | bytes accessed | tf_op | source)
XLA Modules:
  0.0 543.6 jit_solution(288675973146873652)
XLA Ops:
  0.6 4.5 copy.24
  5.2 4.6 reshape.41
  9.8 6.3 %all-to-all-start = ((f32[4,1,32768]{2,1,0:T(1,128)}), f32[4,1,32768]{2,1,0:T(1,128)S(1)}, u32[]{:S(2)}, u32[]{:S(2)}) async-start(f32[4,1,32768]{2,1,0:T(1,128)} %reshape.41), calls=%async_computation | async-start | bytes 1048576 | tf_op jit(solution)/shard_map/all_to_all | solution.py:56
  16.4 4.4 cholesky.164
  22.1 3.7 custom-call.14
  26.0 4.6 all-to-all-done
  31.1 2.2 reduce.4
  33.3 3.4 reshape.42
  36.7 3.0 copy.25
  40.5 38.4 %psum.21 = f32[64,64]{1,0:T(8,128)S(1)} all-reduce(f32[64,64]{1,0:T(8,128)S(1)} %convolution_bitcast_fusion.5), channel_id=1, replica_groups=mesh['wide'=4,'band'=8] {'wide','band'}, use_global_device_ids=true, to_apply=%region_0.1 | all-reduce | flops 4096 | bytes 32768 | tf_op jit(solution)/shard_map/psum | solution.py:67
  79.4 4.4 cholesky.175
  85.1 3.7 custom-call.15
  89.5 4.4 cholesky.186
  95.2 3.7 custom-call.16
  99.6 4.4 cholesky.197
  105.3 3.7 custom-call.17
  112.1 3.0 collective-permute-start.1
  115.4 2.3 collective-permute-start.2
  118.3 11.5 %collective-permute-done.2 = f32[64,16,1]{2,1,0:T(8,128)S(1)} collective-permute-done((f32[64,16,1]{2,1,0:T(8,128)S(1)}, f32[64,16,1]{2,1,0:T(8,128)S(1)}, u32[]{:S(2)}, u32[]{:S(2)}) %collective-permute-start.2) | collective-permute-done | bytes 4128 | tf_op jit(solution)/shard_map/ppermute | solution.py:21
  129.9 13.1 %collective-permute-done.3 = f32[64,16,1]{2,1,0:T(8,128)S(1)} collective-permute-done((f32[64,16,1]{2,1,0:T(8,128)S(1)}, f32[64,16,1]{2,1,0:T(8,128)S(1)}, u32[]{:S(2)}, u32[]{:S(2)}) %collective-permute-start.3) | collective-permute-done | bytes 4128 | tf_op jit(solution)/shard_map/ppermute | solution.py:19
  144.9 3.3 collective-permute-start.5
  148.4 2.4 collective-permute-start.6
  150.8 11.4 %collective-permute-done.6 = f32[64,16,1]{2,1,0:T(8,128)S(1)} collective-permute-done((f32[64,16,1]{2,1,0:T(8,128)S(1)}, f32[64,16,1]{2,1,0:T(8,128)S(1)}, u32[]{:S(2)}, u32[]{:S(2)}) %collective-permute-start.6) | collective-permute-done | bytes 4128 | tf_op jit(solution)/shard_map/ppermute | solution.py:21
  162.2 12.2 %collective-permute-done.7 = f32[64,16,1]{2,1,0:T(8,128)S(1)} collective-permute-done((f32[64,16,1]{2,1,0:T(8,128)S(1)}, f32[64,16,1]{2,1,0:T(8,128)S(1)}, u32[]{:S(2)}, u32[]{:S(2)}) %collective-permute-start.7) | collective-permute-done | bytes 4128 | tf_op jit(solution)/shard_map/ppermute | solution.py:19
  176.4 3.3 collective-permute-start.9
  179.9 2.1 collective-permute-start.10
  182.0 12.1 %collective-permute-done.10 = f32[64,16,1]{2,1,0:T(8,128)S(1)} collective-permute-done((f32[64,16,1]{2,1,0:T(8,128)S(1)}, f32[64,16,1]{2,1,0:T(8,128)S(1)}, u32[]{:S(2)}, u32[]{:S(2)}) %collective-permute-start.10) | collective-permute-done | bytes 4128 | tf_op jit(solution)/shard_map/ppermute | solution.py:21
  194.1 11.0 %collective-permute-done.11 = f32[64,16,1]{2,1,0:T(8,128)S(1)} collective-permute-done((f32[64,16,1]{2,1,0:T(8,128)S(1)}, f32[64,16,1]{2,1,0:T(8,128)S(1)}, u32[]{:S(2)}, u32[]{:S(2)}) %collective-permute-start.11) | collective-permute-done | bytes 4128 | tf_op jit(solution)/shard_map/ppermute | solution.py:19
  206.5 41.3 %psum.22 = f32[64,64]{1,0:T(8,128)S(1)} all-reduce(f32[64,64]{1,0:T(8,128)S(1)} %convolution_bitcast_fusion.4), channel_id=1, replica_groups=mesh['wide'=4,'band'=8] {'wide','band'}, use_global_device_ids=true, to_apply=%region_3.6 | all-reduce | flops 4096 | bytes 32768 | tf_op jit(solution)/shard_map/psum | solution.py:67
  248.3 4.4 cholesky.208
  254.0 3.7 custom-call.18
  258.4 4.4 cholesky.219
  264.1 3.7 custom-call.19
  268.5 4.4 cholesky.230
  274.2 3.7 custom-call.20
  281.0 3.0 collective-permute-start.13
  284.2 2.3 collective-permute-start.14
  286.6 11.6 %collective-permute-done.14 = f32[64,16,1]{2,1,0:T(8,128)S(1)} collective-permute-done((f32[64,16,1]{2,1,0:T(8,128)S(1)}, f32[64,16,1]{2,1,0:T(8,128)S(1)}, u32[]{:S(2)}, u32[]{:S(2)}) %collective-permute-start.14) | collective-permute-done | bytes 4128 | tf_op jit(solution)/shard_map/ppermute | solution.py:21
  298.2 11.2 %collective-permute-done.15 = f32[64,16,1]{2,1,0:T(8,128)S(1)} collective-permute-done((f32[64,16,1]{2,1,0:T(8,128)S(1)}, f32[64,16,1]{2,1,0:T(8,128)S(1)}, u32[]{:S(2)}, u32[]{:S(2)}) %collective-permute-start.15) | collective-permute-done | bytes 4128 | tf_op jit(solution)/shard_map/ppermute | solution.py:19
  311.4 3.6 collective-permute-start.17
  315.2 2.1 collective-permute-start.18
  317.3 11.4 %collective-permute-done.18 = f32[64,16,1]{2,1,0:T(8,128)S(1)} collective-permute-done((f32[64,16,1]{2,1,0:T(8,128)S(1)}, f32[64,16,1]{2,1,0:T(8,128)S(1)}, u32[]{:S(2)}, u32[]{:S(2)}) %collective-permute-start.18) | collective-permute-done | bytes 4128 | tf_op jit(solution)/shard_map/ppermute | solution.py:21
  328.8 12.3 %collective-permute-done.19 = f32[64,16,1]{2,1,0:T(8,128)S(1)} collective-permute-done((f32[64,16,1]{2,1,0:T(8,128)S(1)}, f32[64,16,1]{2,1,0:T(8,128)S(1)}, u32[]{:S(2)}, u32[]{:S(2)}) %collective-permute-start.19) | collective-permute-done | bytes 4128 | tf_op jit(solution)/shard_map/ppermute | solution.py:19
  343.1 3.6 collective-permute-start.21
  348.9 12.0 %collective-permute-done.22 = f32[64,16,1]{2,1,0:T(8,128)S(1)} collective-permute-done((f32[64,16,1]{2,1,0:T(8,128)S(1)}, f32[64,16,1]{2,1,0:T(8,128)S(1)}, u32[]{:S(2)}, u32[]{:S(2)}) %collective-permute-start.22) | collective-permute-done | bytes 4128 | tf_op jit(solution)/shard_map/ppermute | solution.py:21
  361.0 13.0 %collective-permute-done.23 = f32[64,16,1]{2,1,0:T(8,128)S(1)} collective-permute-done((f32[64,16,1]{2,1,0:T(8,128)S(1)}, f32[64,16,1]{2,1,0:T(8,128)S(1)}, u32[]{:S(2)}, u32[]{:S(2)}) %collective-permute-start.23) | collective-permute-done | bytes 4128 | tf_op jit(solution)/shard_map/ppermute | solution.py:19
  375.3 40.8 %psum.23 = f32[64,64]{1,0:T(8,128)S(1)} all-reduce(f32[64,64]{1,0:T(8,128)S(1)} %convolution_bitcast_fusion.3), channel_id=1, replica_groups=mesh['wide'=4,'band'=8] {'wide','band'}, use_global_device_ids=true, to_apply=%region_4.7 | all-reduce | flops 4096 | bytes 32768 | tf_op jit(solution)/shard_map/psum | solution.py:67
  416.6 4.4 cholesky.241
  422.3 3.7 custom-call.21
  426.7 4.4 cholesky.252
  432.4 3.7 custom-call.22
  436.7 4.4 cholesky.263
  442.5 3.7 custom-call.23
  449.3 3.0 collective-permute-start.25
  454.6 11.9 %collective-permute-done.26 = f32[64,16,1]{2,1,0:T(8,128)S(1)} collective-permute-done((f32[64,16,1]{2,1,0:T(8,128)S(1)}, f32[64,16,1]{2,1,0:T(8,128)S(1)}, u32[]{:S(2)}, u32[]{:S(2)}) %collective-permute-start.26) | collective-permute-done | bytes 4128 | tf_op jit(solution)/shard_map/ppermute | solution.py:21
  466.5 12.6 %collective-permute-done.27 = f32[64,16,1]{2,1,0:T(8,128)S(1)} collective-permute-done((f32[64,16,1]{2,1,0:T(8,128)S(1)}, f32[64,16,1]{2,1,0:T(8,128)S(1)}, u32[]{:S(2)}, u32[]{:S(2)}) %collective-permute-start.27) | collective-permute-done | bytes 4128 | tf_op jit(solution)/shard_map/ppermute | solution.py:19
  481.1 3.3 collective-permute-start.29
  484.6 2.4 collective-permute-start.30
  487.0 11.5 %collective-permute-done.30 = f32[64,16,1]{2,1,0:T(8,128)S(1)} collective-permute-done((f32[64,16,1]{2,1,0:T(8,128)S(1)}, f32[64,16,1]{2,1,0:T(8,128)S(1)}, u32[]{:S(2)}, u32[]{:S(2)}) %collective-permute-start.30) | collective-permute-done | bytes 4128 | tf_op jit(solution)/shard_map/ppermute | solution.py:21
  498.5 12.3 %collective-permute-done.31 = f32[64,16,1]{2,1,0:T(8,128)S(1)} collective-permute-done((f32[64,16,1]{2,1,0:T(8,128)S(1)}, f32[64,16,1]{2,1,0:T(8,128)S(1)}, u32[]{:S(2)}, u32[]{:S(2)}) %collective-permute-start.31) | collective-permute-done | bytes 4128 | tf_op jit(solution)/shard_map/ppermute | solution.py:19
  512.8 3.3 collective-permute-start.33
  516.3 2.1 collective-permute-start.34
  518.4 12.0 %collective-permute-done.34 = f32[64,16,1]{2,1,0:T(8,128)S(1)} collective-permute-done((f32[64,16,1]{2,1,0:T(8,128)S(1)}, f32[64,16,1]{2,1,0:T(8,128)S(1)}, u32[]{:S(2)}, u32[]{:S(2)}) %collective-permute-start.34) | collective-permute-done | bytes 4128 | tf_op jit(solution)/shard_map/ppermute | solution.py:21
  530.4 11.6 %collective-permute-done.35 = f32[64,16,1]{2,1,0:T(8,128)S(1)} collective-permute-done((f32[64,16,1]{2,1,0:T(8,128)S(1)}, f32[64,16,1]{2,1,0:T(8,128)S(1)}, u32[]{:S(2)}, u32[]{:S(2)}) %collective-permute-start.35) | collective-permute-done | bytes 4128 | tf_op jit(solution)/shard_map/ppermute | solution.py:19
  (171 shorter events, 52.0 us)
Async XLA Ops:
  0.6 15.5 %copy-start = (f32[64,48]{0,1:T(8,128)S(1)}, f32[64,48]{0,1:T(8,128)}, u32[]{:S(2)}) copy-start(f32[64,48]{0,1:T(8,128)} %param.12) | copy-start | bytes 36868
  9.8 20.8 %all-to-all-start = ((f32[4,1,32768]{2,1,0:T(1,128)}), f32[4,1,32768]{2,1,0:T(1,128)S(1)}, u32[]{:S(2)}, u32[]{:S(2)}) async-start(f32[4,1,32768]{2,1,0:T(1,128)} %reshape.41), calls=%async_computation | async-start | bytes 1048576 | tf_op jit(solution)/shard_map/all_to_all | solution.py:56
  33.3 6.4 %copy-start.1 = (s32[64,16,128]{2,1,0:T(8,128)S(1)}, s32[64,16,128]{2,1,0:T(8,128)}, u32[]{:S(2)}) copy-start(s32[64,16,128]{2,1,0:T(8,128)} %param.9) | copy-start | bytes 1572868
  33.3 6.4 %copy-start.2 = (s32[16,128]{1,0:T(8,128)S(1)}, s32[16,128]{1,0:T(8,128)}, u32[]{:S(2)}) copy-start(s32[16,128]{1,0:T(8,128)} %param.10) | copy-start | bytes 24580
  79.4 63.5 %copy-start.3 = (f32[16,128]{1,0:T(8,128)S(1)}, f32[16,128]{1,0:T(8,128)}, u32[]{:S(2)}) copy-start(f32[16,128]{1,0:T(8,128)} %param.11) | copy-start | bytes 24580
  110.8 32.1 %collective-permute-start = (f32[64,1,128]{2,1,0:T(1,128)S(1)}, f32[64,1,128]{2,1,0:T(1,128)S(1)}, u32[]{:S(2)}, u32[]{:S(2)}) collective-permute-start(f32[64,1,128]{2,1,0:T(1,128)S(1)} %get-tuple-element.36), channel_id=1, source_target_pairs={{1,0},{2,1},{3,2},{4,3},{5,4},{6,5},{7,6},{9,8},{10,9},{11,10},{12... | collective-permute-start | bytes 98312 | tf_op jit(solution)/shard_map/ppermute | solution.py:21
  112.1 30.8 %collective-permute-start.1 = (f32[64,1,128]{2,1,0:T(1,128)S(1)}, f32[64,1,128]{2,1,0:T(1,128)S(1)}, u32[]{:S(2)}, u32[]{:S(2)}) collective-permute-start(f32[64,1,128]{2,1,0:T(1,128)S(1)} %get-tuple-element.37), channel_id=1, source_target_pairs={{0,1},{1,2},{2,3},{3,4},{4,5},{5,6},{6,7},{8,9},{9,10},{10,11},{11... | collective-permute-start | bytes 98312 | tf_op jit(solution)/shard_map/ppermute | solution.py:19
  115.4 14.5 %collective-permute-start.2 = (f32[64,16,1]{2,1,0:T(8,128)S(1)}, f32[64,16,1]{2,1,0:T(8,128)S(1)}, u32[]{:S(2)}, u32[]{:S(2)}) collective-permute-start(f32[64,16,1]{2,1,0:T(8,128)S(1)} %get-tuple-element.38), channel_id=1, source_target_pairs={{8,0},{16,8},{24,16},{0,24},{9,1},{17,9},{25,17},{1,25},{10,2},{18... | collective-permute-start | bytes 12296 | tf_op jit(solution)/shard_map/ppermute | solution.py:21
  117.7 25.2 %collective-permute-start.3 = (f32[64,16,1]{2,1,0:T(8,128)S(1)}, f32[64,16,1]{2,1,0:T(8,128)S(1)}, u32[]{:S(2)}, u32[]{:S(2)}) collective-permute-start(f32[64,16,1]{2,1,0:T(8,128)S(1)} %get-tuple-element.39), channel_id=1, source_target_pairs={{0,8},{8,16},{16,24},{24,0},{1,9},{9,17},{17,25},{25,1},{2,10},{10... | collective-permute-start | bytes 12296 | tf_op jit(solution)/shard_map/ppermute | solution.py:19
  143.6 30.7 %collective-permute-start.4 = (f32[64,1,128]{2,1,0:T(1,128)S(1)}, f32[64,1,128]{2,1,0:T(1,128)S(1)}, u32[]{:S(2)}, u32[]{:S(2)}) collective-permute-start(f32[64,1,128]{2,1,0:T(1,128)S(1)} %get-tuple-element.32), channel_id=1, source_target_pairs={{1,0},{2,1},{3,2},{4,3},{5,4},{6,5},{7,6},{9,8},{10,9},{11,10},{12... | collective-permute-start | bytes 98312 | tf_op jit(solution)/shard_map/ppermute | solution.py:21
  144.9 29.4 %collective-permute-start.5 = (f32[64,1,128]{2,1,0:T(1,128)S(1)}, f32[64,1,128]{2,1,0:T(1,128)S(1)}, u32[]{:S(2)}, u32[]{:S(2)}) collective-permute-start(f32[64,1,128]{2,1,0:T(1,128)S(1)} %get-tuple-element.33), channel_id=1, source_target_pairs={{0,1},{1,2},{2,3},{3,4},{4,5},{5,6},{6,7},{8,9},{9,10},{10,11},{11... | collective-permute-start | bytes 98312 | tf_op jit(solution)/shard_map/ppermute | solution.py:19
  148.4 13.8 %collective-permute-start.6 = (f32[64,16,1]{2,1,0:T(8,128)S(1)}, f32[64,16,1]{2,1,0:T(8,128)S(1)}, u32[]{:S(2)}, u32[]{:S(2)}) collective-permute-start(f32[64,16,1]{2,1,0:T(8,128)S(1)} %get-tuple-element.34), channel_id=1, source_target_pairs={{8,0},{16,8},{24,16},{0,24},{9,1},{17,9},{25,17},{1,25},{10,2},{18... | collective-permute-start | bytes 12296 | tf_op jit(solution)/shard_map/ppermute | solution.py:21
  150.8 23.6 %collective-permute-start.7 = (f32[64,16,1]{2,1,0:T(8,128)S(1)}, f32[64,16,1]{2,1,0:T(8,128)S(1)}, u32[]{:S(2)}, u32[]{:S(2)}) collective-permute-start(f32[64,16,1]{2,1,0:T(8,128)S(1)} %get-tuple-element.35), channel_id=1, source_target_pairs={{0,8},{8,16},{16,24},{24,0},{1,9},{9,17},{17,25},{25,1},{2,10},{10... | collective-permute-start | bytes 12296 | tf_op jit(solution)/shard_map/ppermute | solution.py:19
  175.1 30.1 %collective-permute-start.8 = (f32[64,1,128]{2,1,0:T(1,128)S(1)}, f32[64,1,128]{2,1,0:T(1,128)S(1)}, u32[]{:S(2)}, u32[]{:S(2)}) collective-permute-start(f32[64,1,128]{2,1,0:T(1,128)S(1)} %get-tuple-element.28), channel_id=1, source_target_pairs={{1,0},{2,1},{3,2},{4,3},{5,4},{6,5},{7,6},{9,8},{10,9},{11,10},{12... | collective-permute-start | bytes 98312 | tf_op jit(solution)/shard_map/ppermute | solution.py:21
  176.4 28.8 %collective-permute-start.9 = (f32[64,1,128]{2,1,0:T(1,128)S(1)}, f32[64,1,128]{2,1,0:T(1,128)S(1)}, u32[]{:S(2)}, u32[]{:S(2)}) collective-permute-start(f32[64,1,128]{2,1,0:T(1,128)S(1)} %get-tuple-element.29), channel_id=1, source_target_pairs={{0,1},{1,2},{2,3},{3,4},{4,5},{5,6},{6,7},{8,9},{9,10},{10,11},{11... | collective-permute-start | bytes 98312 | tf_op jit(solution)/shard_map/ppermute | solution.py:19
  179.9 14.2 %collective-permute-start.10 = (f32[64,16,1]{2,1,0:T(8,128)S(1)}, f32[64,16,1]{2,1,0:T(8,128)S(1)}, u32[]{:S(2)}, u32[]{:S(2)}) collective-permute-start(f32[64,16,1]{2,1,0:T(8,128)S(1)} %get-tuple-element.30), channel_id=1, source_target_pairs={{8,0},{16,8},{24,16},{0,24},{9,1},{17,9},{25,17},{1,25},{10,2},{18... | collective-permute-start | bytes 12296 | tf_op jit(solution)/shard_map/ppermute | solution.py:21
  182.0 23.2 %collective-permute-start.11 = (f32[64,16,1]{2,1,0:T(8,128)S(1)}, f32[64,16,1]{2,1,0:T(8,128)S(1)}, u32[]{:S(2)}, u32[]{:S(2)}) collective-permute-start(f32[64,16,1]{2,1,0:T(8,128)S(1)} %get-tuple-element.31), channel_id=1, source_target_pairs={{0,8},{8,16},{16,24},{24,0},{1,9},{9,17},{17,25},{25,1},{2,10},{10... | collective-permute-start | bytes 12296 | tf_op jit(solution)/shard_map/ppermute | solution.py:19
  279.7 29.7 %collective-permute-start.12 = (f32[64,1,128]{2,1,0:T(1,128)S(1)}, f32[64,1,128]{2,1,0:T(1,128)S(1)}, u32[]{:S(2)}, u32[]{:S(2)}) collective-permute-start(f32[64,1,128]{2,1,0:T(1,128)S(1)} %get-tuple-element.24), channel_id=1, source_target_pairs={{1,0},{2,1},{3,2},{4,3},{5,4},{6,5},{7,6},{9,8},{10,9},{11,10},{12... | collective-permute-start | bytes 98312 | tf_op jit(solution)/shard_map/ppermute | solution.py:21
  281.0 28.4 %collective-permute-start.13 = (f32[64,1,128]{2,1,0:T(1,128)S(1)}, f32[64,1,128]{2,1,0:T(1,128)S(1)}, u32[]{:S(2)}, u32[]{:S(2)}) collective-permute-start(f32[64,1,128]{2,1,0:T(1,128)S(1)} %get-tuple-element.25), channel_id=1, source_target_pairs={{0,1},{1,2},{2,3},{3,4},{4,5},{5,6},{6,7},{8,9},{9,10},{10,11},{11... | collective-permute-start | bytes 98312 | tf_op jit(solution)/shard_map/ppermute | solution.py:19
  284.2 14.0 %collective-permute-start.14 = (f32[64,16,1]{2,1,0:T(8,128)S(1)}, f32[64,16,1]{2,1,0:T(8,128)S(1)}, u32[]{:S(2)}, u32[]{:S(2)}) collective-permute-start(f32[64,16,1]{2,1,0:T(8,128)S(1)} %get-tuple-element.26), channel_id=1, source_target_pairs={{8,0},{16,8},{24,16},{0,24},{9,1},{17,9},{25,17},{1,25},{10,2},{18... | collective-permute-start | bytes 12296 | tf_op jit(solution)/shard_map/ppermute | solution.py:21
  286.6 22.8 %collective-permute-start.15 = (f32[64,16,1]{2,1,0:T(8,128)S(1)}, f32[64,16,1]{2,1,0:T(8,128)S(1)}, u32[]{:S(2)}, u32[]{:S(2)}) collective-permute-start(f32[64,16,1]{2,1,0:T(8,128)S(1)} %get-tuple-element.27), channel_id=1, source_target_pairs={{0,8},{8,16},{16,24},{24,0},{1,9},{9,17},{17,25},{25,1},{2,10},{10... | collective-permute-start | bytes 12296 | tf_op jit(solution)/shard_map/ppermute | solution.py:19
  310.1 31.0 %collective-permute-start.16 = (f32[64,1,128]{2,1,0:T(1,128)S(1)}, f32[64,1,128]{2,1,0:T(1,128)S(1)}, u32[]{:S(2)}, u32[]{:S(2)}) collective-permute-start(f32[64,1,128]{2,1,0:T(1,128)S(1)} %get-tuple-element.20), channel_id=1, source_target_pairs={{1,0},{2,1},{3,2},{4,3},{5,4},{6,5},{7,6},{9,8},{10,9},{11,10},{12... | collective-permute-start | bytes 98312 | tf_op jit(solution)/shard_map/ppermute | solution.py:21
  311.4 29.7 %collective-permute-start.17 = (f32[64,1,128]{2,1,0:T(1,128)S(1)}, f32[64,1,128]{2,1,0:T(1,128)S(1)}, u32[]{:S(2)}, u32[]{:S(2)}) collective-permute-start(f32[64,1,128]{2,1,0:T(1,128)S(1)} %get-tuple-element.21), channel_id=1, source_target_pairs={{0,1},{1,2},{2,3},{3,4},{4,5},{5,6},{6,7},{8,9},{9,10},{10,11},{11... | collective-permute-start | bytes 98312 | tf_op jit(solution)/shard_map/ppermute | solution.py:19
  315.2 13.6 %collective-permute-start.18 = (f32[64,16,1]{2,1,0:T(8,128)S(1)}, f32[64,16,1]{2,1,0:T(8,128)S(1)}, u32[]{:S(2)}, u32[]{:S(2)}) collective-permute-start(f32[64,16,1]{2,1,0:T(8,128)S(1)} %get-tuple-element.22), channel_id=1, source_target_pairs={{8,0},{16,8},{24,16},{0,24},{9,1},{17,9},{25,17},{1,25},{10,2},{18... | collective-permute-start | bytes 12296 | tf_op jit(solution)/shard_map/ppermute | solution.py:21
  317.3 23.8 %collective-permute-start.19 = (f32[64,16,1]{2,1,0:T(8,128)S(1)}, f32[64,16,1]{2,1,0:T(8,128)S(1)}, u32[]{:S(2)}, u32[]{:S(2)}) collective-permute-start(f32[64,16,1]{2,1,0:T(8,128)S(1)} %get-tuple-element.23), channel_id=1, source_target_pairs={{0,8},{8,16},{16,24},{24,0},{1,9},{9,17},{17,25},{25,1},{2,10},{10... | collective-permute-start | bytes 12296 | tf_op jit(solution)/shard_map/ppermute | solution.py:19
  341.8 32.2 %collective-permute-start.20 = (f32[64,1,128]{2,1,0:T(1,128)S(1)}, f32[64,1,128]{2,1,0:T(1,128)S(1)}, u32[]{:S(2)}, u32[]{:S(2)}) collective-permute-start(f32[64,1,128]{2,1,0:T(1,128)S(1)} %get-tuple-element.16), channel_id=1, source_target_pairs={{1,0},{2,1},{3,2},{4,3},{5,4},{6,5},{7,6},{9,8},{10,9},{11,10},{12... | collective-permute-start | bytes 98312 | tf_op jit(solution)/shard_map/ppermute | solution.py:21
  343.1 30.9 %collective-permute-start.21 = (f32[64,1,128]{2,1,0:T(1,128)S(1)}, f32[64,1,128]{2,1,0:T(1,128)S(1)}, u32[]{:S(2)}, u32[]{:S(2)}) collective-permute-start(f32[64,1,128]{2,1,0:T(1,128)S(1)} %get-tuple-element.17), channel_id=1, source_target_pairs={{0,1},{1,2},{2,3},{3,4},{4,5},{5,6},{6,7},{8,9},{9,10},{10,11},{11... | collective-permute-start | bytes 98312 | tf_op jit(solution)/shard_map/ppermute | solution.py:19
  346.9 14.1 %collective-permute-start.22 = (f32[64,16,1]{2,1,0:T(8,128)S(1)}, f32[64,16,1]{2,1,0:T(8,128)S(1)}, u32[]{:S(2)}, u32[]{:S(2)}) collective-permute-start(f32[64,16,1]{2,1,0:T(8,128)S(1)} %get-tuple-element.18), channel_id=1, source_target_pairs={{8,0},{16,8},{24,16},{0,24},{9,1},{17,9},{25,17},{1,25},{10,2},{18... | collective-permute-start | bytes 12296 | tf_op jit(solution)/shard_map/ppermute | solution.py:21
  348.8 25.1 %collective-permute-start.23 = (f32[64,16,1]{2,1,0:T(8,128)S(1)}, f32[64,16,1]{2,1,0:T(8,128)S(1)}, u32[]{:S(2)}, u32[]{:S(2)}) collective-permute-start(f32[64,16,1]{2,1,0:T(8,128)S(1)} %get-tuple-element.19), channel_id=1, source_target_pairs={{0,8},{8,16},{16,24},{24,0},{1,9},{9,17},{17,25},{25,1},{2,10},{10... | collective-permute-start | bytes 12296 | tf_op jit(solution)/shard_map/ppermute | solution.py:19
  446.4 33.3 %copy-start.4 = (f32[48,64]{1,0:T(8,128)}, f32[48,64]{1,0:T(8,128)S(1)}, u32[]{:S(2)}) copy-start(f32[48,64]{1,0:T(8,128)S(1)} %fusion.79) | copy-start | bytes 36868
  448.0 31.1 %collective-permute-start.24 = (f32[64,1,128]{2,1,0:T(1,128)S(1)}, f32[64,1,128]{2,1,0:T(1,128)S(1)}, u32[]{:S(2)}, u32[]{:S(2)}) collective-permute-start(f32[64,1,128]{2,1,0:T(1,128)S(1)} %get-tuple-element.12), channel_id=1, source_target_pairs={{1,0},{2,1},{3,2},{4,3},{5,4},{6,5},{7,6},{9,8},{10,9},{11,10},{12... | collective-permute-start | bytes 98312 | tf_op jit(solution)/shard_map/ppermute | solution.py:21
  449.3 29.8 %collective-permute-start.25 = (f32[64,1,128]{2,1,0:T(1,128)S(1)}, f32[64,1,128]{2,1,0:T(1,128)S(1)}, u32[]{:S(2)}, u32[]{:S(2)}) collective-permute-start(f32[64,1,128]{2,1,0:T(1,128)S(1)} %get-tuple-element.13), channel_id=1, source_target_pairs={{0,1},{1,2},{2,3},{3,4},{4,5},{5,6},{6,7},{8,9},{9,10},{10,11},{11... | collective-permute-start | bytes 98312 | tf_op jit(solution)/shard_map/ppermute | solution.py:19
  452.5 13.9 %collective-permute-start.26 = (f32[64,16,1]{2,1,0:T(8,128)S(1)}, f32[64,16,1]{2,1,0:T(8,128)S(1)}, u32[]{:S(2)}, u32[]{:S(2)}) collective-permute-start(f32[64,16,1]{2,1,0:T(8,128)S(1)} %get-tuple-element.14), channel_id=1, source_target_pairs={{8,0},{16,8},{24,16},{0,24},{9,1},{17,9},{25,17},{1,25},{10,2},{18... | collective-permute-start | bytes 12296 | tf_op jit(solution)/shard_map/ppermute | solution.py:21
  454.4 24.7 %collective-permute-start.27 = (f32[64,16,1]{2,1,0:T(8,128)S(1)}, f32[64,16,1]{2,1,0:T(8,128)S(1)}, u32[]{:S(2)}, u32[]{:S(2)}) collective-permute-start(f32[64,16,1]{2,1,0:T(8,128)S(1)} %get-tuple-element.15), channel_id=1, source_target_pairs={{0,8},{8,16},{16,24},{24,0},{1,9},{9,17},{17,25},{25,1},{2,10},{10... | collective-permute-start | bytes 12296 | tf_op jit(solution)/shard_map/ppermute | solution.py:19
  479.8 31.0 %collective-permute-start.28 = (f32[64,1,128]{2,1,0:T(1,128)S(1)}, f32[64,1,128]{2,1,0:T(1,128)S(1)}, u32[]{:S(2)}, u32[]{:S(2)}) collective-permute-start(f32[64,1,128]{2,1,0:T(1,128)S(1)} %get-tuple-element.8), channel_id=1, source_target_pairs={{1,0},{2,1},{3,2},{4,3},{5,4},{6,5},{7,6},{9,8},{10,9},{11,10},{12... | collective-permute-start | bytes 98312 | tf_op jit(solution)/shard_map/ppermute | solution.py:21
  481.1 29.7 %collective-permute-start.29 = (f32[64,1,128]{2,1,0:T(1,128)S(1)}, f32[64,1,128]{2,1,0:T(1,128)S(1)}, u32[]{:S(2)}, u32[]{:S(2)}) collective-permute-start(f32[64,1,128]{2,1,0:T(1,128)S(1)} %get-tuple-element.9), channel_id=1, source_target_pairs={{0,1},{1,2},{2,3},{3,4},{4,5},{5,6},{6,7},{8,9},{9,10},{10,11},{11... | collective-permute-start | bytes 98312 | tf_op jit(solution)/shard_map/ppermute | solution.py:19
  484.6 13.9 %collective-permute-start.30 = (f32[64,16,1]{2,1,0:T(8,128)S(1)}, f32[64,16,1]{2,1,0:T(8,128)S(1)}, u32[]{:S(2)}, u32[]{:S(2)}) collective-permute-start(f32[64,16,1]{2,1,0:T(8,128)S(1)} %get-tuple-element.10), channel_id=1, source_target_pairs={{8,0},{16,8},{24,16},{0,24},{9,1},{17,9},{25,17},{1,25},{10,2},{18... | collective-permute-start | bytes 12296 | tf_op jit(solution)/shard_map/ppermute | solution.py:21
  487.0 23.8 %collective-permute-start.31 = (f32[64,16,1]{2,1,0:T(8,128)S(1)}, f32[64,16,1]{2,1,0:T(8,128)S(1)}, u32[]{:S(2)}, u32[]{:S(2)}) collective-permute-start(f32[64,16,1]{2,1,0:T(8,128)S(1)} %get-tuple-element.11), channel_id=1, source_target_pairs={{0,8},{8,16},{16,24},{24,0},{1,9},{9,17},{17,25},{25,1},{2,10},{10... | collective-permute-start | bytes 12296 | tf_op jit(solution)/shard_map/ppermute | solution.py:19
  511.5 30.5 %collective-permute-start.32 = (f32[64,1,128]{2,1,0:T(1,128)S(1)}, f32[64,1,128]{2,1,0:T(1,128)S(1)}, u32[]{:S(2)}, u32[]{:S(2)}) collective-permute-start(f32[64,1,128]{2,1,0:T(1,128)S(1)} %get-tuple-element.4), channel_id=1, source_target_pairs={{1,0},{2,1},{3,2},{4,3},{5,4},{6,5},{7,6},{9,8},{10,9},{11,10},{12... | collective-permute-start | bytes 98312 | tf_op jit(solution)/shard_map/ppermute | solution.py:21
  512.8 29.2 %collective-permute-start.33 = (f32[64,1,128]{2,1,0:T(1,128)S(1)}, f32[64,1,128]{2,1,0:T(1,128)S(1)}, u32[]{:S(2)}, u32[]{:S(2)}) collective-permute-start(f32[64,1,128]{2,1,0:T(1,128)S(1)} %get-tuple-element.5), channel_id=1, source_target_pairs={{0,1},{1,2},{2,3},{3,4},{4,5},{5,6},{6,7},{8,9},{9,10},{10,11},{11... | collective-permute-start | bytes 98312 | tf_op jit(solution)/shard_map/ppermute | solution.py:19
  516.3 14.1 %collective-permute-start.34 = (f32[64,16,1]{2,1,0:T(8,128)S(1)}, f32[64,16,1]{2,1,0:T(8,128)S(1)}, u32[]{:S(2)}, u32[]{:S(2)}) collective-permute-start(f32[64,16,1]{2,1,0:T(8,128)S(1)} %get-tuple-element.6), channel_id=1, source_target_pairs={{8,0},{16,8},{24,16},{0,24},{9,1},{17,9},{25,17},{1,25},{10,2},{18... | collective-permute-start | bytes 12296 | tf_op jit(solution)/shard_map/ppermute | solution.py:21
  518.4 23.6 %collective-permute-start.35 = (f32[64,16,1]{2,1,0:T(8,128)S(1)}, f32[64,16,1]{2,1,0:T(8,128)S(1)}, u32[]{:S(2)}, u32[]{:S(2)}) collective-permute-start(f32[64,16,1]{2,1,0:T(8,128)S(1)} %get-tuple-element.7), channel_id=1, source_target_pairs={{0,8},{8,16},{16,24},{24,0},{1,9},{9,17},{17,25},{25,1},{2,10},{10... | collective-permute-start | bytes 12296 | tf_op jit(solution)/shard_map/ppermute | solution.py:19
where the time goes:
time: 551 us; the launch traced here: 544 us
  waiting for transfers between devices  219 us (40%)
  blocking collectives  121 us (22%)
  other arithmetic  103 us (19%)
  starting transfers between devices  68 us (12%)
  local copies, waits for them, and re-layouts  19.3 us (4%)
  matrix products  11.5 us (2%)
    psum x3, blocking collectives, shards(): lax.psum(contract_pixels(flat_field, flat_field), ('wide', 'band'))  121 us
    ppermute x18, waiting for transfers between devices, extended(): lax.ppermute(tail, axis, [(i, (i + 1) % count) for i in range(ends)])  109 us
    ppermute x18, waiting for transfers between devices, extended(): lax.ppermute(head, axis, [((i + 1) % count, i) for i in range(ends)])  105 us
    another operation x30, other arithmetic, orthonormal(): factor = jnp.linalg.cholesky(gram_matrix)  50.5 us
    another operation x20, other arithmetic, orthonormal(): return jax.scipy.linalg.solve_triangular(factor, coeff.T, lower=True).T  43.2 us
    ppermute x18, starting transfers between devices, extended(): lax.ppermute(head, axis, [((i + 1) % count, i) for i in range(ends)])  31.3 us
    ppermute x18, starting transfers between devices, extended(): lax.ppermute(tail, axis, [(i, (i + 1) % count) for i in range(ends)])  30.4 us
    unnamed x16, local copies, waits for them, and re-layouts  12.8 us
  transfers between devices with their start and end apart: 37, of which 19 were waited for; matrix products, arithmetic and copies ran while one was open for 2% of the time, Pallas kernels for 0%

commit v1 on v0

v1 whole, which is shorter than its diff:
```python
import functools
import jax
import jax.numpy as jnp
from jax import lax
from jax.experimental import pallas as pl
from jax.experimental.pallas import tpu as pltpu
from jax.sharding import PartitionSpec as P

OUTER = 3
INNER = 3
PASSES = 3
HALO = OUTER * PASSES
LANES = 128
EXTRA = 8
FLOOR = 0.02

F32 = jnp.float32
BF16 = jnp.bfloat16
VMEM = pl.BlockSpec(memory_space=pltpu.VMEM)
SMEM = pl.BlockSpec(memory_space=pltpu.SMEM)


def highest(left, right, left_dim, right_dim):
    return lax.dot_general(
        left,
        right,
        (((left_dim,), (right_dim,)), ((), ())),
        precision=lax.Precision.HIGHEST,
        preferred_element_type=F32,
    )


def halves(value):
    high = value.astype(BF16)
    return high, (value - high.astype(F32)).astype(BF16)


def thirds(value):
    first = value.astype(BF16)
    rest = value - first.astype(F32)
    second = rest.astype(BF16)
    return first, second, (rest - second.astype(F32)).astype(BF16)


def grid_of(shape, axis):
    return lax.broadcasted_iota(jnp.int32, shape, axis)


def covariance_of(rows_of, count):
    days = None
    total = None
    for start in range(0, count, 2):
        pair = jnp.concatenate([rows_of(start), rows_of(start + 1)], axis=1)
        days = pair.shape[0]
        stack = jnp.concatenate(thirds(pair), axis=0)
        part = lax.dot_general(
            stack, stack, (((1,), (1,)), ((), ())), preferred_element_type=F32
        )
        total = part if total is None else total + part
    block = lambda i, j: total[i * days : (i + 1) * days, j * days : (j + 1) * days]
    small = block(2, 2) + (block(1, 2) + block(2, 1))
    small = small + (block(0, 2) + block(2, 0)) + block(1, 1)
    return block(0, 0) + ((block(0, 1) + block(1, 0)) + small)


def pack_symmetric(packed_ref, cov):
    half = cov.shape[0] // 2
    quarter = half // 2
    upper = grid_of((half, half), 1) >= grid_of((half, half), 0)
    same = grid_of((half, half), 1) == grid_of((half, half), 0)
    low = cov[half:, half:]
    mixed = jnp.where(upper, cov[:half, :half], low)
    cross = cov[:half, half:]
    body = jnp.concatenate(
        [mixed[:quarter], cross[:quarter], mixed[quarter:], cross[quarter:]], axis=1
    )
    diagonal = jnp.sum(jnp.where(same, low, 0.0), axis=0, keepdims=True)
    diagonal = jnp.concatenate([diagonal, jnp.zeros((1, LANES - half), F32)], axis=1)
    each = quarter // 2
    for side in range(2):
        for row in range(each):
            packed_ref[side, :, row * LANES : (row + 1) * LANES] = body[
                side * each + row : side * each + row + 1
            ]
        packed_ref[side, :, each * LANES :] = (
            diagonal if side == 0 else jnp.zeros((1, LANES), F32)
        )


def unpack_symmetric(parts_ref, body_ref, days):
    half = days // 2
    quarter = half // 2
    each = quarter // 2
    sides = []
    for side in range(2):
        values = [parts_ref[j] for j in range(side, parts_ref.shape[0], 2)]
        while len(values) > 1:
            paired = [values[i] + values[i + 1] for i in range(0, len(values) - 1, 2)]
            values = paired + values[len(paired) * 2 :]
        sides.append(values[0])
        for row in range(each):
            body_ref[side * each + row : side * each + row + 1, :] = values[0][
                :, row * LANES : (row + 1) * LANES
            ]
    body = body_ref[...]
    diagonal = sides[0][:, each * LANES : each * LANES + half]
    mixed = jnp.concatenate([body[:, :half], body[:, 2 * half : 3 * half]], axis=0)
    cross = jnp.concatenate([body[:, half : 2 * half], body[:, 3 * half :]], axis=0)
    col, row = grid_of((half, half), 1), grid_of((half, half), 0)
    flipped = mixed.T
    high = jnp.where(col >= row, mixed, flipped)
    low = jnp.where(col < row, mixed, flipped)
    low = jnp.where(col == row, jnp.broadcast_to(diagonal, (half, half)), low)
    top = jnp.concatenate([high, cross], axis=1)
    bottom = jnp.concatenate([cross.T, low], axis=1)
    return jnp.concatenate([top, bottom], axis=0)


def orthonormal_rows(rows):
    count, width = rows.shape
    gram = highest(rows, rows, 1, 1)
    pad = jnp.zeros((count, LANES - count - width), F32)
    table = jnp.concatenate([gram, rows, pad], axis=1)
    groups = [table[8 * i : 8 * i + 8] for i in range(count // 8)]
    sublane = grid_of((8, LANES), 0)
    pivots = []
    spread = lambda row: jnp.broadcast_to(row, (8, LANES))
    for k in range(0, count, 2):
        i, s = k // 8, k % 8
        first = [jnp.broadcast_to(g[:, k : k + 1], (8, LANES)) for g in groups[i:]]
        second = [jnp.broadcast_to(g[:, k + 1 : k + 2], (8, LANES)) for g in groups[i:]]
        row0, row1 = spread(groups[i][s : s + 1]), spread(groups[i][s + 1 : s + 2])
        a = spread(first[0][s : s + 1])
        b = spread(first[0][s + 1 : s + 2])
        c = spread(second[0][s + 1 : s + 2])
        det = a * c - b * b
        scale = 1.0 / det
        h0, h1, h2 = c * scale, b * scale, a * scale
        w0 = h0 * row0 - h1 * row1
        w1 = h2 * row1 - h1 * row0
        ratio = b / a
        pivots.append((a, c - b * ratio))
        for j in range(i, len(groups)):
            c0, c1 = first[j - i], second[j - i]
            updated = groups[j] - (c0 * w0 + c1 * w1)
            if j == i:
                updated = jnp.where(sublane > s + 1, updated, groups[j])
                updated = jnp.where(sublane == s + 1, row1 - ratio * row0, updated)
            groups[j] = updated
    outs, worst = [], None
    for i, g in enumerate(groups):
        d = jnp.zeros((8, LANES), F32)
        for s in range(8):
            d = jnp.where(sublane == s, pivots[(8 * i + s) // 2][s % 2], d)
        own = grid_of((8, LANES), 1) == sublane + 8 * i
        start = jnp.sum(
            jnp.where(own, table[8 * i : 8 * i + 8], 0.0), axis=1, keepdims=True
        )
        kept = d / start
        worst = kept if worst is None else jnp.minimum(worst, kept)
        outs.append(g[:, count : count + width] * lax.rsqrt(d)[:, :width])
    return jnp.concatenate(outs, axis=0), jnp.min(worst)


def start_kernel(modes_ref, rows_ref):
    rows_ref[...], _ = orthonormal_rows(modes_ref[...].T)


def modes_kernel(parts_ref, rows_ref, new_ref, last_ref, body_ref):
    rows = rows_ref[...]
    days = rows.shape[1]
    cov = unpack_symmetric(parts_ref, body_ref, days)
    same = grid_of((days, days), 1) == grid_of((days, days), 0)
    peak = jnp.max(jnp.where(same, cov, 0.0), keepdims=True)
    cov = cov * (1.0 / peak)
    moved = highest(rows, cov, 1, 0)
    twice = highest(cov, cov, 1, 0)
    new, kept = orthonormal_rows(highest(moved, twice, 1, 0))
    new_ref[...] = new

    @pl.when(jnp.logical_not(kept >= FLOOR))
    def _():
        def step(_, held):
            return orthonormal_rows(highest(held, cov, 1, 0))[0]

        new_ref[...] = lax.fori_loop(0, INNER, step, rows)

    final = new_ref[...]
    last_ref[...] = highest(final, final, 0, 0)


def static_kernel(obs_ref, ocean_ref, diff_ref, stat_ref):
    days, rows, cols = obs_ref.shape
    flat = obs_ref.reshape(days * rows, cols)
    for r in range(rows):
        seen = flat[pl.ds(r, days, stride=rows), :]
        ocean = ocean_ref[r : r + 1, :]
        stat_ref[r, :days, :] = ((1 - seen) * ocean).astype(F32)
        rest = jnp.concatenate(
            [
                diff_ref[r : r + 1, :],
                ocean.astype(F32),
                jnp.zeros((EXTRA - 2, cols), F32),
            ],
            axis=0,
        )
        stat_ref[r, days:, :] = rest


def observed_kernel(blocks, offs_ref, *refs):
    piece_refs = refs[:blocks]
    stat_ref, seen_ref, packed_ref = refs[blocks:]
    rows, days, cols = seen_ref.shape
    each = piece_refs[0].shape[0]
    for r in range(rows):
        ocean = stat_ref[r, days + 1 : days + 2, :]
        for b, piece_ref in enumerate(piece_refs):
            flat = piece_ref.reshape(each * rows, cols)
            start = pl.multiple_of(offs_ref[b], each)
            gap = stat_ref[r, pl.ds(start, each), :]
            value = flat[pl.ds(r, each, stride=rows), :]
            seen_ref[r, pl.ds(start, each), :] = value * (ocean - gap)
    pack_symmetric(packed_ref, covariance_of(lambda r: seen_ref[r], rows))


def row_source(refs, rows, e):
    north, main, south = refs
    if e < HALO:
        return north[e]
    if e < HALO + rows:
        return main[e - HALO]
    return south[e - HALO - rows]


def strip_kernel(*refs):
    seen, stat = refs[0:3], refs[3:6]
    east_ref, west_ref = refs[6:]
    rows, days, cols = seen[1].shape
    per = cols // HALO
    lane_seen = grid_of((days, cols), 1)
    lane_stat = grid_of((days + EXTRA, cols), 1)
    total = rows + 2 * HALO
    for tile in range(east_ref.shape[0]):
        for source, at, lane in (
            (seen, slice(0, days), lane_seen),
            (stat, slice(days, None), lane_stat),
        ):
            east = jnp.zeros(lane.shape, F32)
            west = jnp.zeros(lane.shape, F32)
            for j in range(min(per, total - tile * per)):
                value = row_source(source, rows, tile * per + j)
                here = (lane >= j * HALO) & (lane < (j + 1) * HALO)
                to_west = pltpu.roll(value, j * HALO, 1) if j else value
                to_east = pltpu.roll(value, (j + 1) * HALO, 1)
                west = jnp.where(here, to_west, west)
                east = jnp.where(here, to_east, east)
            east_ref[tile, at, :] = east
            west_ref[tile, at, :] = west


def project_rows(last, f_ref, out_ref, seen_ref, gap_ref, low, high):
    p0, p1 = halves(last)
    weights = jnp.concatenate([p0, p0, p1, p1], axis=1)

    def row(e, _):
        f0, f1 = halves(f_ref[e])
        stack = jnp.concatenate([f0, f1, f0, f1], axis=0)
        recon = jnp.dot(weights, stack, preferred_element_type=F32)
        out_ref[e] = seen_ref[e] + gap_ref[e] * recon
        return 0

    lax.fori_loop(low, high, row, 0)


def smooth_rows(f_ref, out_ref, gap_ref, diff_ref, low, high):
    width = f_ref.shape[2]

    def row(e, _):
        value = f_ref[e]
        around = f_ref[e - 1] + f_ref[e + 1]
        around = around + pltpu.roll(value, 1, 1) + pltpu.roll(value, width - 1, 1)
        coef = gap_ref[e] * diff_ref[e]
        out_ref[e] = value + coef * (around - 4.0 * value)
        return 0

    lax.fori_loop(low, high, row, 0)


def sweep_body(sweep, last, f_ref, a_ref, b_ref, seen_ref, gap_ref, diff_ref):
    total = seen_ref.shape[0]
    edge = sweep * PASSES
    project_rows(last, f_ref, a_ref, seen_ref, gap_ref, edge, total - edge)
    now, other = a_ref, b_ref
    for step in range(PASSES):
        edge += 1
        smooth_rows(now, other, gap_ref, diff_ref, edge, total - edge)
        now, other = other, now
    return now


def first_kernel(*refs):
    last_ref = refs[0]
    seen, stat = refs[1:4], refs[4:7]
    east_ref, west_ref = refs[7:9]
    seen_ref, gap_ref, diff_ref, out_ref, packed_ref = refs[9:14]
    a_ref = refs[14]
    rows, days, cols = seen[1].shape
    total = rows + 2 * HALO
    per = cols // HALO
    lane = grid_of((days, cols), 1)
    lane1 = grid_of((1, cols), 1)

    def side(e, at, lane):
        tile, j = e // per, e % per
        east, west = east_ref[tile, at, :], west_ref[tile, at, :]
        shift = (cols - j * HALO) % cols
        east = pltpu.roll(east, shift, 1) if shift else east
        west = pltpu.roll(west, cols - (j + 1) * HALO, 1)
        value = jnp.where(lane >= cols - HALO, west, 0.0)
        return jnp.where(lane < HALO, east, value)

    for e in range(total):
        seen_ref[e, :, :cols] = row_source(seen, rows, e)
        seen_ref[e, :, cols:] = side(e, slice(0, days), lane)
        whole = row_source(stat, rows, e)
        gap_ref[e, :, :cols] = whole[:days]
        gap_ref[e, :, cols:] = side(e, slice(days, 2 * days), lane)
        diff_ref[e, :, :cols] = whole[days : days + 1]
        diff_ref[e, :, cols:] = side(e, slice(2 * days, 2 * days + 1), lane1)
    now = sweep_body(
        0, last_ref[...], seen_ref, a_ref, out_ref, seen_ref, gap_ref, diff_ref
    )
    assert now is out_ref
    cov = covariance_of(lambda r: out_ref[HALO + r, :, :cols], rows)
    pack_symmetric(packed_ref, cov)


def next_kernel(sweep, last_ref, f_ref, seen_ref, gap_ref, diff_ref, out_ref, packed_ref, a_ref):
    now = sweep_body(sweep, last_ref[...], f_ref, a_ref, out_ref, seen_ref, gap_ref, diff_ref)
    assert now is out_ref
    rows = out_ref.shape[0] - 2 * HALO
    cols = out_ref.shape[2] // 2
    cov = covariance_of(lambda r: out_ref[HALO + r, :, :cols], rows)
    pack_symmetric(packed_ref, cov)


def end_kernel(sweep, last_ref, f_ref, seen_ref, gap_ref, diff_ref, rows_ref, out_ref, modes_ref, a_ref, b_ref):
    now = sweep_body(sweep, last_ref[...], f_ref, a_ref, b_ref, seen_ref, gap_ref, diff_ref)
    days, rows, cols = out_ref.shape
    flat = out_ref.reshape(days * rows, cols)
    for r in range(rows):
        flat[pl.ds(r, days, stride=rows), :] = now[HALO + r, :, :cols]
    modes_ref[...] = rows_ref[...].T


def call(kernel, name, ins, outs, scratch=(), scalars=0):
    specs = [SMEM] * scalars + [VMEM] * (len(ins) - scalars)
    return pl.pallas_call(
        kernel,
        name=name,
        out_shape=[jax.ShapeDtypeStruct(s, F32) for s in outs],
        in_specs=specs,
        out_specs=[VMEM] * len(outs),
        scratch_shapes=[pltpu.VMEM(s, F32) for s in scratch],
        compiler_params=pltpu.CompilerParams(vmem_limit_bytes=24 * 2**20),
    )(*ins)


def sum_parts(packed):
    count = lax.axis_size("band")
    width = packed.shape[2]
    parity = lax.rem(lax.axis_index("band"), 2)
    mine = lax.dynamic_slice_in_dim(packed, parity, 1, 0)
    other = lax.dynamic_slice_in_dim(packed, 1 - parity, 1, 0)
    got = lax.ppermute(other, "band", [(i, i ^ 1) for i in range(count)])
    everyone = count * lax.axis_size("wide")
    copies = jnp.broadcast_to(mine + got, (everyone, 1, width))
    return lax.all_to_all(copies, ("wide", "band"), 0, 0, tiled=True)


def edges(cells):
    rows = cells.shape[0]
    count = lax.axis_size("band")
    north = lax.ppermute(cells[rows - HALO :], "band", [(i, i + 1) for i in range(count - 1)])
    south = lax.ppermute(cells[:HALO], "band", [(i + 1, i) for i in range(count - 1)])
    return [north, cells, south]


def shards(day_field, obs_mask, ocean_mask, diffusivity, start_modes):
    days, rows, cols = obs_mask.shape
    modes = start_modes.shape[1]
    count = lax.axis_size("wide")
    me = lax.axis_index("wide")
    pieces, offs = [], []
    for k in range(count):
        to = lambda i: i ^ k
        piece = lax.dynamic_slice_in_dim(day_field, to(me) * cols, cols, 2)
        if k:
            piece = lax.ppermute(piece, "wide", [(i, to(i)) for i in range(count)])
        pieces.append(piece)
        offs.append(to(me) * day_field.shape[0])
    (stat,) = call(
        static_kernel, "static", [obs_mask, ocean_mask, diffusivity], [(rows, days + EXTRA, cols)]
    )
    stats = edges(stat)
    (basis,) = call(start_kernel, "start", [start_modes], [(modes, days)])
    offs = jnp.stack(offs).astype(jnp.int32)
    width = (days // 8 // 2 * 2 // 2 // 2 * 2 + 1) * LANES
    width = (days // 8 + 1) * LANES
    seen, packed = call(
        functools.partial(observed_kernel, count),
        "observed",
        [offs] + pieces + [stat],
        [(rows, days, cols), (2, 1, width)],
        scalars=1,
    )
    seens = edges(seen)
    parts = sum_parts(packed)
    total = rows + 2 * HALO
    tiles = pl.cdiv(total, cols // HALO)
    strip = (tiles, 2 * days + EXTRA, cols)
    east, west = call(strip_kernel, "strips", seens + stats, [strip, strip])
    from_west = lax.ppermute(east, "wide", [(i, (i + 1) % count) for i in range(count)])
    from_east = lax.ppermute(west, "wide", [((i + 1) % count, i) for i in range(count)])
    quarter = (days // 4, LANES)
    orth = lambda parts, basis: call(
        modes_kernel, "modes", [parts, basis], [(modes, days), (days, days)], [quarter]
    )
    wide_map, wide_row = (total, days, 2 * cols), (total, 1, 2 * cols)
    basis, last = orth(parts, basis)
    seen_w, gap_w, diff_w, filled, packed = call(
        first_kernel,
        "sweep0",
        [last] + seens + stats + [from_east, from_west],
        [wide_map, wide_map, wide_row, wide_map, (2, 1, width)],
        [wide_map],
    )
    for sweep in range(1, OUTER):
        basis, last = orth(sum_parts(packed), basis)
        ins = [last, filled, seen_w, gap_w, diff_w]
        if sweep < OUTER - 1:
            filled, packed = call(
                functools.partial(next_kernel, sweep),
                f"sweep{sweep}",
                ins,
                [wide_map, (2, 1, width)],
                [wide_map],
            )
        else:
            out, mode_basis = call(
                functools.partial(end_kernel, sweep),
                f"sweep{sweep}",
                ins + [basis],
                [(days, rows, cols), (days, modes)],
                [wide_map, wide_map],
            )
    return (out, mode_basis)


def solution(mesh):
    placed = (
        P("wide", "band", None),
        P(None, "band", "wide"),
        P("band", "wide"),
        P("band", "wide"),
        P(),
    )
    return jax.shard_map(
        shards,
        mesh=mesh,
        in_specs=placed,
        out_specs=(P(None, "band", "wide"), P()),
        check_vma=False,
    )
```

time: 551 us -> 123 us (0.22); the launches traced: 544 us -> 123 us
  waiting for transfers between devices: 219 us -> 8.83 us
  other arithmetic: 103 us -> 0.15 us
  blocking collectives: 121 us -> 21.9 us
  Pallas kernels: 0 us -> 61.3 us
  starting transfers between devices: 68 us -> 23.7 us
  local copies, waits for them, and re-layouts: 19.3 us -> 6.08 us
  matrix products: 11.5 us -> 0 us
    ppermute x36 -> x12, waiting for transfers between devices: 215 us -> 8.83 us  [the longest x3 3.29 us: shards(): piece = lax.ppermute(piece, 'wide', [(i, to(i)) for i in range(count)])]
    psum x3 -> x0, blocking collectives: 121 us -> none  [shards(): lax.psum(contract_pixels(flat_field, flat_field), ('wide', 'band'))]
    another operation x50 -> x1, other arithmetic: 93.8 us -> 0.08 us  [shards(): offs = jnp.stack(offs).astype(jnp.int32)]
    pallas_call x0 -> x10, Pallas kernels: none -> 61.3 us  [call(): pl.pallas_call(kernel, name=name, out_shape=[jax.ShapeDtypeStruct(s, F32)...]
    ppermute x36 -> x12, starting transfers between devices: 61.6 us -> 19.7 us  [the longest x2 6.1 us: edges(): lax.ppermute(cells[rows - HALO:], 'band', [(i, i + 1) for i in range(coun...]
    all_to_all x0 -> x2, blocking collectives: none -> 21.9 us  [sum_parts(): return lax.all_to_all(copies, ('wide', 'band'), 0, 0, tiled=True)]
    unnamed x16 -> x9, local copies, waits for them, and re-layouts: 12.8 us -> 2.52 us
    dot_general x28 -> x0, matrix products: 9.11 us -> none  [the longest x3 2.13 us: contract_pixels(): lax.dot_general(left, right, (((1,), (1,)), ((), ())), precision=lax.Prec...]
  transfers between devices with their start and end apart: 37 -> 13, of which waited for: 19 -> 5; matrix products, arithmetic and copies ran while one was open for 2% -> 1% of each run, Pallas kernels for 0% -> 9%
where the time goes in v1:
time: 123 us
  Pallas kernels  61.3 us (50%)
  starting transfers between devices  23.7 us (19%)
  blocking collectives  21.9 us (18%)
  waiting for transfers between devices  8.83 us (7%)
  local copies, waits for them, and re-layouts  6.08 us (5%)
    pallas_call x10, Pallas kernels, call(): pl.pallas_call(kernel, name=name, out_shape=[jax.ShapeDtypeStruct(s, F32)...  61.3 us
    all_to_all x2, blocking collectives, sum_parts(): return lax.all_to_all(copies, ('wide', 'band'), 0, 0, tiled=True)  21.9 us
    ppermute x2, starting transfers between devices, edges(): lax.ppermute(cells[rows - HALO:], 'band', [(i, i + 1) for i in range(coun...  6.1 us
    ppermute x3, starting transfers between devices, shards(): piece = lax.ppermute(piece, 'wide', [(i, to(i)) for i in range(count)])  5.78 us
    all_to_all x1, starting transfers between devices, sum_parts(): return lax.all_to_all(copies, ('wide', 'band'), 0, 0, tiled=True)  3.97 us
    ppermute x1, starting transfers between devices, shards(): lax.ppermute(west, 'wide', [((i + 1) % count, i) for i in range(count)])  3.67 us
    ppermute x3, waiting for transfers between devices, shards(): piece = lax.ppermute(piece, 'wide', [(i, to(i)) for i in range(count)])  3.29 us
    ppermute x3, waiting for transfers between devices, sum_parts(): got = lax.ppermute(other, 'band', [(i, i ^ 1) for i in range(count)])  2.88 us
  transfers between devices with their start and end apart: 13, of which 5 were waited for; matrix products, arithmetic and copies ran while one was open for 1% of the time, Pallas kernels for 9%

profile of v1, /device:TPU:0, one launch (start us, length us, event | category | flops | bytes accessed | tf_op | source)
XLA Modules:
  0.0 122.8 jit_solution(2254078100138522138)
XLA Ops:
  0.7 1.1 constant_dynamic-slice_fusion.3
  1.8 5.1 %collective-permute-start.2 = (f32[16,16,128]{2,1,0:T(8,128)S(1)}, f32[16,16,128]{2,1,0:T(8,128)S(1)}, u32[]{:S(2)}, u32[]{:S(2)}) collective-permute-start(f32[16,16,128]{2,1,0:T(8,128)S(1)} %get-tuple-element.42), channel_id=1, source_target_pairs={{0,24},{8,16},{16,8},{24,0},{1,25},{9,17},{17,9},{25,1},{2,26},{10... | collective-permute-start | bytes 393224 | tf_op jit(solution)/shard_map/ppermute | solution.py:399
  6.9 0.0 collective-permute-start
  6.9 0.6 collective-permute-start.1
  7.6 0.0 copy-start
  7.6 1.0 copy-done
  8.6 0.0 copy-start.1
  8.6 0.7 copy-done.1
  9.3 0.0 copy-start.2
  9.3 0.7 copy-done.2
  10.0 0.2 static.1.refs_4_.refs_5_
  10.3 1.3 %collective-permute-start.7 = (f32[9,72,128]{2,1,0:T(8,128)S(1)}, f32[9,72,128]{2,1,0:T(8,128)S(1)}, u32[]{:S(2)}, u32[]{:S(2)}) collective-permute-start(f32[9,72,128]{2,1,0:T(8,128)S(1)} %get-tuple-element.38), channel_id=1, source_target_pairs={{1,0},{2,1},{3,2},{4,3},{5,4},{6,5},{7,6},{9,8},{10,9},{11,10},{12... | collective-permute-start | bytes 995336 | tf_op jit(solution)/shard_map/ppermute | solution.py:385
  11.6 3.1 %collective-permute-start.6 = (f32[9,72,128]{2,1,0:T(8,128)S(1)}, f32[9,72,128]{2,1,0:T(8,128)S(1)}, u32[]{:S(2)}, u32[]{:S(2)}) collective-permute-start(f32[9,72,128]{2,1,0:T(8,128)S(1)} %get-tuple-element.39), channel_id=1, source_target_pairs={{0,1},{1,2},{2,3},{3,4},{4,5},{5,6},{6,7},{8,9},{9,10},{10,11},{11... | collective-permute-start | bytes 995336 | tf_op jit(solution)/shard_map/ppermute | solution.py:384
  14.7 0.1 pad_add_fusion.offs_ref
  14.7 0.0 collective-permute-done.2.refs_3_
  14.7 0.0 collective-permute-done.refs_1_
  14.7 3.3 %collective-permute-done.1.refs_2_ = f32[16,16,128]{2,1,0:T(8,128)S(1)} collective-permute-done((f32[16,16,128]{2,1,0:T(8,128)S(1)}, f32[16,16,128]{2,1,0:T(8,128)S(1)}, u32[]{:S(2)}, u32[]{:S(2)}) %collective-permute-start.1) | collective-permute-done | bytes 131104 | tf_op jit(solution)/shard_map/ppermute | solution.py:399
  18.0 1.5 %observed.1 = (f32[16,64,128]{2,1,0:T(8,128)S(1)}, f32[2,1,1152]{2,1,0:T(1,128)S(1)}) custom-call(s32[4]{0:T(128)S(1)} %pad_add_fusion.offs_ref, f32[16,16,128]{2,1,0:T(8,128)S(1)} %get-tuple-element.44.refs_0_, f32[16,16,128]{2,1,0:T(8,128)S(1)} %collective-permute-done.refs_1_, f32[16,16,128]{2,1,0:T(8,128)S(1)} %collective-permute-done.1.refs_2_, ...), custom_call_target="tpu_custom_call" | custom-call | tf_op jit(solution)/shard_map/observed/pallas_call | solution.py:358
  19.5 0.0 copy-start.3
  19.5 0.8 fusion.1
  20.3 1.3 %collective-permute-start.5 = (f32[9,64,128]{2,1,0:T(8,128)}, f32[9,64,128]{2,1,0:T(8,128)S(1)}, u32[]{:S(2)}, u32[]{:S(2)}) collective-permute-start(f32[9,64,128]{2,1,0:T(8,128)} %get-tuple-element.40), channel_id=1, source_target_pairs={{1,0},{2,1},{3,2},{4,3},{5,4},{6,5},{7,6},{9,8},{10,9},{11,10},{12... | collective-permute-start | bytes 884744 | tf_op jit(solution)/shard_map/ppermute | solution.py:385
  21.6 3.0 %collective-permute-start.4 = (f32[9,64,128]{2,1,0:T(8,128)S(1)}, f32[9,64,128]{2,1,0:T(8,128)S(1)}, u32[]{:S(2)}, u32[]{:S(2)}) collective-permute-start(f32[9,64,128]{2,1,0:T(8,128)S(1)} %get-tuple-element.41), channel_id=1, source_target_pairs={{0,1},{1,2},{2,3},{3,4},{4,5},{5,6},{6,7},{8,9},{9,10},{10,11},{11... | collective-permute-start | bytes 884744 | tf_op jit(solution)/shard_map/ppermute | solution.py:384
  24.7 1.2 collective-permute-start.3
  25.8 0.8 collective-permute-done.3
  26.7 0.7 broadcast_in_dim.22
  27.4 4.0 %all-to-all-start = ((f32[32,1,1152]{2,1,0:T(1,128)}), f32[32,1,1152]{2,1,0:T(1,128)S(1)}, u32[]{:S(2)}, u32[]{:S(2)}) async-start(f32[32,1,1152]{2,1,0:T(1,128)} %broadcast_in_dim.22), calls=%async_computation | async-start | bytes 294912 | tf_op jit(solution)/shard_map/all_to_all | solution.py:378
  31.4 0.0 collective-permute-done.7.refs_5_.refs_6_
  31.4 0.0 collective-permute-done.6.refs_3_.refs_4_
  31.4 0.0 collective-permute-done.5.refs_2_.refs_3_
  31.4 0.0 collective-permute-done.4.refs_0_.refs_1_
  31.4 1.3 %strips.1 = (f32[3,136,128]{2,1,0:T(8,128)S(1)}, f32[3,136,128]{2,1,0:T(8,128)S(1)}) custom-call(f32[9,64,128]{2,1,0:T(8,128)S(1)} %collective-permute-done.4.refs_0_.refs_1_, f32[16,64,128]{2,1,0:T(8,128)S(1)} %get-tuple-element.21.refs_1_.refs_2_, f32[9,64,128]{2,1,0:T(8,128)S(1)} %collective-permute-done.5.refs_2_.refs_3_, ...), custom_call_target="tpu_custom_call" | custom-call | tf_op jit(solution)/shard_map/strips/pallas_call | solution.py:358
  32.7 3.7 %collective-permute-start.8 = (f32[3,136,128]{2,1,0:T(8,128)S(1)}, f32[3,136,128]{2,1,0:T(8,128)S(1)}, u32[]{:S(2)}, u32[]{:S(2)}) collective-permute-start(f32[3,136,128]{2,1,0:T(8,128)S(1)} %get-tuple-element.22), channel_id=1, source_target_pairs={{8,0},{16,8},{24,16},{0,24},{9,1},{17,9},{25,17},{1,25},{10,2},{18... | collective-permute-start | bytes 626696 | tf_op jit(solution)/shard_map/ppermute | solution.py:424
  36.3 0.0 collective-permute-start.9
  36.3 0.0 copy-done.3
  36.4 0.1 copy.7.modes_ref
  36.4 3.7 %start.1.rows_ref = f32[48,64]{1,0:T(8,128)S(1)} custom-call(f32[64,48]{1,0:T(8,128)S(1)} %copy.7.modes_ref), custom_call_target="tpu_custom_call" | custom-call | tf_op jit(solution)/shard_map/start/pallas_call | solution.py:358
  40.1 0.0 all-to-all-done.parts_ref
  40.1 4.6 %modes.3 = (f32[48,64]{1,0:T(8,128)S(1)}, f32[64,64]{1,0:T(8,128)S(1)}) custom-call(f32[32,1,1152]{2,1,0:T(1,128)S(1)} %all-to-all-done.parts_ref, f32[48,64]{1,0:T(8,128)S(1)} %start.1.rows_ref), custom_call_target="tpu_custom_call" | custom-call | tf_op jit(solution)/shard_map/modes/pallas_call | solution.py:358
  44.7 0.0 collective-permute-done.8.refs_7_
  44.7 2.7 %collective-permute-done.9.refs_8_ = f32[3,136,128]{2,1,0:T(8,128)S(1)} collective-permute-done((f32[3,136,128]{2,1,0:T(8,128)S(1)}, f32[3,136,128]{2,1,0:T(8,128)S(1)}, u32[]{:S(2)}, u32[]{:S(2)}) %collective-permute-start.9) | collective-permute-done | bytes 208928 | tf_op jit(solution)/shard_map/ppermute | solution.py:423
  47.4 17.3 %sweep0.1 = (f32[34,64,256]{2,1,0:T(8,128)S(1)}, f32[34,64,256]{2,1,0:T(8,128)S(1)}, f32[34,1,256]{2,1,0:T(1,128)S(1)}, f32[34,64,256]{2,1,0:T(8,128)S(1)}, f32[2,1,1152]{2,1,0:T(1,128)S(1)}) custom-call(f32[64,64]{1,0:T(8,128)S(1)} %get-tuple-element.20.refs_0_, f32[9,64,128]{2,1,0:T(8,128)S(1)} %collective-permute-done.4.refs_0_.refs_1_, ...), custom_call_target="tpu_custom_call" | custom-call | tf_op jit(solution)/shard_map/sweep0/pallas_call | solution.py:358
  64.7 0.1 collective-permute-start.10
  64.8 1.2 collective-permute-done.10
  66.0 0.1 broadcast_in_dim.24
  66.0 11.6 %all_to_all.15.parts_ref = f32[32,1,1152]{2,1,0:T(1,128)S(1)} all-to-all(f32[32,1,1152]{2,1,0:T(1,128)S(1)} %broadcast_in_dim.24), channel_id=1, replica_groups=mesh['wide'=4,'band'=8] {'wide','band'}, dimensions={0} | all-to-all | bytes 294912 | tf_op jit(solution)/shard_map/all_to_all | solution.py:378
  77.7 4.6 %modes.4 = (f32[48,64]{1,0:T(8,128)S(1)}, f32[64,64]{1,0:T(8,128)S(1)}) custom-call(f32[32,1,1152]{2,1,0:T(1,128)S(1)} %all_to_all.15.parts_ref, f32[48,64]{1,0:T(8,128)S(1)} %get-tuple-element.25.rows_ref), custom_call_target="tpu_custom_call" | custom-call | tf_op jit(solution)/shard_map/modes/pallas_call | solution.py:358
  82.2 13.1 %sweep1.1 = (f32[34,64,256]{2,1,0:T(8,128)S(1)}, f32[2,1,1152]{2,1,0:T(1,128)S(1)}) custom-call(f32[64,64]{1,0:T(8,128)S(1)} %get-tuple-element.26.last_ref, f32[34,64,256]{2,1,0:T(8,128)S(1)} %get-tuple-element.27.f_ref, f32[34,64,256]{2,1,0:T(8,128)S(1)} %get-tuple-element.28.seen_ref, f32[34,64,256]{2,1,0:T(8,128)S(1)} %get-tuple-element.29.gap_ref, ...), custom_call_target="tpu_custom_call" | custom-call | tf_op jit(solution)/shard_map/sweep1/pallas_call | solution.py:358
  95.4 0.3 collective-permute-start.11
  95.7 0.9 collective-permute-done.11
  96.6 0.1 broadcast_in_dim.26
  96.7 10.3 %all_to_all.16.parts_ref = f32[32,1,1152]{2,1,0:T(1,128)S(1)} all-to-all(f32[32,1,1152]{2,1,0:T(1,128)S(1)} %broadcast_in_dim.26), channel_id=1, replica_groups=mesh['wide'=4,'band'=8] {'wide','band'}, dimensions={0} | all-to-all | bytes 294912 | tf_op jit(solution)/shard_map/all_to_all | solution.py:378
  107.0 4.6 %modes.5 = (f32[48,64]{1,0:T(8,128)S(1)}, f32[64,64]{1,0:T(8,128)S(1)}) custom-call(f32[32,1,1152]{2,1,0:T(1,128)S(1)} %all_to_all.16.parts_ref, f32[48,64]{1,0:T(8,128)S(1)} %get-tuple-element.32.rows_ref), custom_call_target="tpu_custom_call" | custom-call | tf_op jit(solution)/shard_map/modes/pallas_call | solution.py:358
  111.6 10.5 %sweep2.1 = (f32[64,16,128]{2,1,0:T(8,128)}, f32[64,48]{1,0:T(8,128)S(1)}) custom-call(f32[64,64]{1,0:T(8,128)S(1)} %get-tuple-element.33.last_ref, f32[34,64,256]{2,1,0:T(8,128)S(1)} %get-tuple-element.34.f_ref, f32[34,64,256]{2,1,0:T(8,128)S(1)} %get-tuple-element.28.seen_ref, f32[34,64,256]{2,1,0:T(8,128)S(1)} %get-tuple-element.29.gap_ref, ...), custom_call_target="tpu_custom_call" | custom-call | tf_op jit(solution)/shard_map/sweep2/pallas_call | solution.py:358
  122.1 0.7 copy.8
  (7 shorter events, 0.2 us)
Async XLA Ops:
  1.8 12.9 %collective-permute-start.2 = (f32[16,16,128]{2,1,0:T(8,128)S(1)}, f32[16,16,128]{2,1,0:T(8,128)S(1)}, u32[]{:S(2)}, u32[]{:S(2)}) collective-permute-start(f32[16,16,128]{2,1,0:T(8,128)S(1)} %get-tuple-element.42), channel_id=1, source_target_pairs={{0,24},{8,16},{16,8},{24,0},{1,25},{9,17},{17,9},{25,1},{2,26},{10... | collective-permute-start | bytes 393224 | tf_op jit(solution)/shard_map/ppermute | solution.py:399
  6.9 7.8 %collective-permute-start = (f32[16,16,128]{2,1,0:T(8,128)S(1)}, f32[16,16,128]{2,1,0:T(8,128)S(1)}, u32[]{:S(2)}, u32[]{:S(2)}) collective-permute-start(f32[16,16,128]{2,1,0:T(8,128)S(1)} %get-tuple-element.43), channel_id=1, source_target_pairs={{0,8},{8,0},{16,24},{24,16},{1,9},{9,1},{17,25},{25,17},{2,10},{10... | collective-permute-start | bytes 393224 | tf_op jit(solution)/shard_map/ppermute | solution.py:399
  6.9 11.1 %collective-permute-start.1 = (f32[16,16,128]{2,1,0:T(8,128)S(1)}, f32[16,16,128]{2,1,0:T(8,128)S(1)}, u32[]{:S(2)}, u32[]{:S(2)}) collective-permute-start(f32[16,16,128]{2,1,0:T(8,128)S(1)} %get-tuple-element.45), channel_id=1, source_target_pairs={{0,16},{8,24},{16,0},{24,8},{1,17},{9,25},{17,1},{25,9},{2,18},{10... | collective-permute-start | bytes 393224 | tf_op jit(solution)/shard_map/ppermute | solution.py:399
  7.6 1.0 copy-start
  8.6 0.7 copy-start.1
  9.3 0.7 copy-start.2
  10.3 21.1 %collective-permute-start.7 = (f32[9,72,128]{2,1,0:T(8,128)S(1)}, f32[9,72,128]{2,1,0:T(8,128)S(1)}, u32[]{:S(2)}, u32[]{:S(2)}) collective-permute-start(f32[9,72,128]{2,1,0:T(8,128)S(1)} %get-tuple-element.38), channel_id=1, source_target_pairs={{1,0},{2,1},{3,2},{4,3},{5,4},{6,5},{7,6},{9,8},{10,9},{11,10},{12... | collective-permute-start | bytes 995336 | tf_op jit(solution)/shard_map/ppermute | solution.py:385
  11.6 19.8 %collective-permute-start.6 = (f32[9,72,128]{2,1,0:T(8,128)S(1)}, f32[9,72,128]{2,1,0:T(8,128)S(1)}, u32[]{:S(2)}, u32[]{:S(2)}) collective-permute-start(f32[9,72,128]{2,1,0:T(8,128)S(1)} %get-tuple-element.39), channel_id=1, source_target_pairs={{0,1},{1,2},{2,3},{3,4},{4,5},{5,6},{6,7},{8,9},{9,10},{10,11},{11... | collective-permute-start | bytes 995336 | tf_op jit(solution)/shard_map/ppermute | solution.py:384
  19.5 16.8 %copy-start.3 = (f32[64,48]{0,1:T(8,128)S(1)}, f32[64,48]{0,1:T(8,128)}, u32[]{:S(2)}) copy-start(f32[64,48]{0,1:T(8,128)} %param.9) | copy-start | bytes 36868
  20.3 11.1 %collective-permute-start.5 = (f32[9,64,128]{2,1,0:T(8,128)}, f32[9,64,128]{2,1,0:T(8,128)S(1)}, u32[]{:S(2)}, u32[]{:S(2)}) collective-permute-start(f32[9,64,128]{2,1,0:T(8,128)} %get-tuple-element.40), channel_id=1, source_target_pairs={{1,0},{2,1},{3,2},{4,3},{5,4},{6,5},{7,6},{9,8},{10,9},{11,10},{12... | collective-permute-start | bytes 884744 | tf_op jit(solution)/shard_map/ppermute | solution.py:385
  21.6 9.8 %collective-permute-start.4 = (f32[9,64,128]{2,1,0:T(8,128)S(1)}, f32[9,64,128]{2,1,0:T(8,128)S(1)}, u32[]{:S(2)}, u32[]{:S(2)}) collective-permute-start(f32[9,64,128]{2,1,0:T(8,128)S(1)} %get-tuple-element.41), channel_id=1, source_target_pairs={{0,1},{1,2},{2,3},{3,4},{4,5},{5,6},{6,7},{8,9},{9,10},{10,11},{11... | collective-permute-start | bytes 884744 | tf_op jit(solution)/shard_map/ppermute | solution.py:384
  24.7 2.0 %collective-permute-start.3 = (f32[1,1,1152]{2,1,0:T(1,128)S(1)}, f32[1,1,1152]{2,1,0:T(1,128)S(1)}, u32[]{:S(2)}, u32[]{:S(2)}) collective-permute-start(f32[1,1,1152]{2,1,0:T(1,128)S(1)} %constant_dynamic-slice_fusion.2), channel_id=1, source_target_pairs={{0,1},{1,0},{2,3},{3,2},{4,5},{5,4},{6,7},{7,6},{8,9},{9,8},{10,11... | collective-permute-start | bytes 13832 | tf_op jit(solution)/shard_map/ppermute | solution.py:375
  27.4 12.7 %all-to-all-start = ((f32[32,1,1152]{2,1,0:T(1,128)}), f32[32,1,1152]{2,1,0:T(1,128)S(1)}, u32[]{:S(2)}, u32[]{:S(2)}) async-start(f32[32,1,1152]{2,1,0:T(1,128)} %broadcast_in_dim.22), calls=%async_computation | async-start | bytes 294912 | tf_op jit(solution)/shard_map/all_to_all | solution.py:378
  32.7 12.0 %collective-permute-start.8 = (f32[3,136,128]{2,1,0:T(8,128)S(1)}, f32[3,136,128]{2,1,0:T(8,128)S(1)}, u32[]{:S(2)}, u32[]{:S(2)}) collective-permute-start(f32[3,136,128]{2,1,0:T(8,128)S(1)} %get-tuple-element.22), channel_id=1, source_target_pairs={{8,0},{16,8},{24,16},{0,24},{9,1},{17,9},{25,17},{1,25},{10,2},{18... | collective-permute-start | bytes 626696 | tf_op jit(solution)/shard_map/ppermute | solution.py:424
  36.3 11.0 %collective-permute-start.9 = (f32[3,136,128]{2,1,0:T(8,128)S(1)}, f32[3,136,128]{2,1,0:T(8,128)S(1)}, u32[]{:S(2)}, u32[]{:S(2)}) collective-permute-start(f32[3,136,128]{2,1,0:T(8,128)S(1)} %get-tuple-element.23), channel_id=1, source_target_pairs={{0,8},{8,16},{16,24},{24,0},{1,9},{9,17},{17,25},{25,1},{2,10},{10... | collective-permute-start | bytes 626696 | tf_op jit(solution)/shard_map/ppermute | solution.py:423
  64.7 1.2 %collective-permute-start.10 = (f32[1,1,1152]{2,1,0:T(1,128)S(1)}, f32[1,1,1152]{2,1,0:T(1,128)S(1)}, u32[]{:S(2)}, u32[]{:S(2)}) collective-permute-start(f32[1,1,1152]{2,1,0:T(1,128)S(1)} %constant_dynamic-slice_fusion.1), channel_id=1, source_target_pairs={{0,1},{1,0},{2,3},{3,2},{4,5},{5,4},{6,7},{7,6},{8,9},{9,8},{10,11... | collective-permute-start | bytes 13832 | tf_op jit(solution)/shard_map/ppermute | solution.py:375
  95.4 1.2 %collective-permute-start.11 = (f32[1,1,1152]{2,1,0:T(1,128)S(1)}, f32[1,1,1152]{2,1,0:T(1,128)S(1)}, u32[]{:S(2)}, u32[]{:S(2)}) collective-permute-start(f32[1,1,1152]{2,1,0:T(1,128)S(1)} %constant_dynamic-slice_fusion), channel_id=1, source_target_pairs={{0,1},{1,0},{2,3},{3,2},{4,5},{5,4},{6,7},{7,6},{8,9},{9,8},{10,11... | collective-permute-start | bytes 13832 | tf_op jit(solution)/shard_map/ppermute | solution.py:375

commit v2 on v1

--- a/solution.py
+++ b/solution.py
@@ -12,6 +12,8 @@
 HALO = OUTER * PASSES
 LANES = 128
 EXTRA = 8
+CHUNK = 8
+BATCH = 2
 FLOOR = 0.02
 
 F32 = jnp.float32
@@ -269,31 +271,51 @@
         out_ref[e] = seen_ref[e] + gap_ref[e] * recon
         return 0
 
-    lax.fori_loop(low, high, row, 0)
-
-
-def smooth_rows(f_ref, out_ref, gap_ref, diff_ref, low, high):
-    width = f_ref.shape[2]
-
-    def row(e, _):
-        value = f_ref[e]
-        around = f_ref[e - 1] + f_ref[e + 1]
-        around = around + pltpu.roll(value, 1, 1) + pltpu.roll(value, width - 1, 1)
-        coef = gap_ref[e] * diff_ref[e]
-        out_ref[e] = value + coef * (around - 4.0 * value)
+    lax.fori_loop(low, high, row, 0, unroll=True)
+
+
+def beside_matrix(width):
+    row, col = grid_of((width, width), 0), grid_of((width, width), 1)
+    apart = jnp.abs(row - col)
+    near = jnp.where((apart == 1) | (apart == width - 1), 1.0, 0.0)
+    return jnp.where(apart == 0, -4.0, near).astype(BF16)
+
+
+def smooth_rows(near, f_ref, out_ref, gap_ref, diff_ref, low, high):
+    total, days, width = f_ref.shape
+    low = max(1, low - (low - high) % BATCH)
+    steps = (high - low) // BATCH
+
+    def batch(i, _):
+        e = low + i * BATCH
+        value = f_ref[pl.ds(e, BATCH)].reshape(BATCH * days, width)
+        f0, f1 = halves(value)
+        lap = jnp.dot(f0, near, preferred_element_type=F32) + jnp.dot(
+            f1, near, preferred_element_type=F32
+        )
+        for k in range(BATCH):
+            coef = jnp.broadcast_to(diff_ref[e + k], (CHUNK, width))
+            for at in range(0, days, CHUNK):
+                part = slice(at, at + CHUNK)
+                around = f_ref[e + k - 1, part, :] + f_ref[e + k + 1, part, :]
+                around = around + lap[k * days + at : k * days + at + CHUNK]
+                out_ref[e + k, part, :] = (
+                    f_ref[e + k, part, :] + (gap_ref[e + k, part, :] * coef) * around
+                )
         return 0
 
-    lax.fori_loop(low, high, row, 0)
+    lax.fori_loop(0, steps, batch, 0, unroll=True)
 
 
 def sweep_body(sweep, last, f_ref, a_ref, b_ref, seen_ref, gap_ref, diff_ref):
     total = seen_ref.shape[0]
     edge = sweep * PASSES
     project_rows(last, f_ref, a_ref, seen_ref, gap_ref, edge, total - edge)
+    near = beside_matrix(seen_ref.shape[2])
     now, other = a_ref, b_ref
     for step in range(PASSES):
         edge += 1
-        smooth_rows(now, other, gap_ref, diff_ref, edge, total - edge)
+        smooth_rows(near, now, other, gap_ref, diff_ref, edge, total - edge)
         now, other = other, now
     return now
 

time: 123 us -> 93.1 us (0.76)
  Pallas kernels: 61.3 us -> 31.1 us
    pallas_call x10, Pallas kernels: 61.3 us -> 31.1 us  [call(): pl.pallas_call(kernel, name=name, out_shape=[jax.ShapeDtypeStruct(s, F32)...]
  transfers between devices with their start and end apart: 13 -> 13, of which waited for: 5 -> 5; matrix products, arithmetic and copies ran while one was open for 1% -> 2% of each run, Pallas kernels for 9% -> 12%
where the time goes in v2:
time: 93.1 us; the launch traced here: 92.6 us
  Pallas kernels  31.1 us (33%)
  starting transfers between devices  23.7 us (25%)
  blocking collectives  21.9 us (24%)
  waiting for transfers between devices  8.84 us (9%)
  local copies, waits for them, and re-layouts  6.08 us (7%)
    pallas_call x10, Pallas kernels, call(): pl.pallas_call(kernel, name=name, out_shape=[jax.ShapeDtypeStruct(s, F32)...  31.1 us
    all_to_all x2, blocking collectives, sum_parts(): return lax.all_to_all(copies, ('wide', 'band'), 0, 0, tiled=True)  21.9 us
    ppermute x2, starting transfers between devices, edges(): lax.ppermute(cells[rows - HALO:], 'band', [(i, i + 1) for i in range(coun...  6.1 us
    ppermute x3, starting transfers between devices, shards(): piece = lax.ppermute(piece, 'wide', [(i, to(i)) for i in range(count)])  5.78 us
    all_to_all x1, starting transfers between devices, sum_parts(): return lax.all_to_all(copies, ('wide', 'band'), 0, 0, tiled=True)  3.97 us
    ppermute x1, starting transfers between devices, shards(): lax.ppermute(west, 'wide', [((i + 1) % count, i) for i in range(count)])  3.67 us
    ppermute x3, waiting for transfers between devices, shards(): piece = lax.ppermute(piece, 'wide', [(i, to(i)) for i in range(count)])  3.29 us
    ppermute x3, waiting for transfers between devices, sum_parts(): got = lax.ppermute(other, 'band', [(i, i ^ 1) for i in range(count)])  2.88 us
  transfers between devices with their start and end apart: 13, of which 5 were waited for; matrix products, arithmetic and copies ran while one was open for 2% of the time, Pallas kernels for 12%

profile of v2, /device:TPU:0, one launch (start us, length us, event | category | flops | bytes accessed | tf_op | source)
XLA Modules:
  0.0 92.6 jit_solution(712176906695812551)
XLA Ops:
  0.7 1.1 %constant_dynamic-slice_fusion.3 = (f32[16,16,128]{2,1,0:T(8,128)S(1)}, f32[16,16,128]{2,1,0:T(8,128)S(1)}, f32[16,16,128]{2,1,0:T(8,128)S(1)}, f32[16,16,128]{2,1,0:T(8,128)S(1)}) fusion(f32[16,16,512]{2,1,0:T(8,128)} %param.5, s32[]{:T(128)S(6)} %select_n.25, s32[]{:T(128)S(6)} %select_n.23, s32[]{:T(128)S(6)} %select_n.22, s32[]{:T(128)S(6)} %select_n.24), kind=kLoop, calls=%fused_computation.6 | loop fusion | bytes 1048592 | tf_op jit(solution)/shard_map/dynamic_slice | solution.py:419
  1.8 5.1 %collective-permute-start.2 = (f32[16,16,128]{2,1,0:T(8,128)S(1)}, f32[16,16,128]{2,1,0:T(8,128)S(1)}, u32[]{:S(2)}, u32[]{:S(2)}) collective-permute-start(f32[16,16,128]{2,1,0:T(8,128)S(1)} %get-tuple-element.42), channel_id=1, source_target_pairs={{0,24},{8,16},{16,8},{24,0},{1,25},{9,17},{17,9},{25,1},{2,26},{10... | collective-permute-start | bytes 393224 | tf_op jit(solution)/shard_map/ppermute | solution.py:421
  6.9 0.0 collective-permute-start
  6.9 0.6 collective-permute-start.1
  7.6 0.0 copy-start
  7.6 1.0 %copy-done = s32[64,16,128]{2,1,0:T(8,128)S(1)} copy-done((s32[64,16,128]{2,1,0:T(8,128)S(1)}, s32[64,16,128]{2,1,0:T(8,128)}, u32[]{:S(2)}) %copy-start) | copy-done | bytes 524312
  8.6 0.0 copy-start.1
  8.6 0.7 copy-done.1
  9.3 0.0 copy-start.2
  9.3 0.7 copy-done.2
  10.0 0.2 static.1.refs_4_.refs_5_
  10.3 1.3 %collective-permute-start.7 = (f32[9,72,128]{2,1,0:T(8,128)S(1)}, f32[9,72,128]{2,1,0:T(8,128)S(1)}, u32[]{:S(2)}, u32[]{:S(2)}) collective-permute-start(f32[9,72,128]{2,1,0:T(8,128)S(1)} %get-tuple-element.38), channel_id=1, source_target_pairs={{1,0},{2,1},{3,2},{4,3},{5,4},{6,5},{7,6},{9,8},{10,9},{11,10},{12... | collective-permute-start | bytes 995336 | tf_op jit(solution)/shard_map/ppermute | solution.py:407
  11.6 3.1 %collective-permute-start.6 = (f32[9,72,128]{2,1,0:T(8,128)S(1)}, f32[9,72,128]{2,1,0:T(8,128)S(1)}, u32[]{:S(2)}, u32[]{:S(2)}) collective-permute-start(f32[9,72,128]{2,1,0:T(8,128)S(1)} %get-tuple-element.39), channel_id=1, source_target_pairs={{0,1},{1,2},{2,3},{3,4},{4,5},{5,6},{6,7},{8,9},{9,10},{10,11},{11... | collective-permute-start | bytes 995336 | tf_op jit(solution)/shard_map/ppermute | solution.py:406
  14.7 0.1 pad_add_fusion.offs_ref
  14.7 0.0 collective-permute-done.2.refs_3_
  14.7 0.0 collective-permute-done.refs_1_
  14.7 3.3 %collective-permute-done.1.refs_2_ = f32[16,16,128]{2,1,0:T(8,128)S(1)} collective-permute-done((f32[16,16,128]{2,1,0:T(8,128)S(1)}, f32[16,16,128]{2,1,0:T(8,128)S(1)}, u32[]{:S(2)}, u32[]{:S(2)}) %collective-permute-start.1) | collective-permute-done | bytes 131104 | tf_op jit(solution)/shard_map/ppermute | solution.py:421
  18.0 1.5 %observed.1 = (f32[16,64,128]{2,1,0:T(8,128)S(1)}, f32[2,1,1152]{2,1,0:T(1,128)S(1)}) custom-call(s32[4]{0:T(128)S(1)} %pad_add_fusion.offs_ref, f32[16,16,128]{2,1,0:T(8,128)S(1)} %get-tuple-element.44.refs_0_, f32[16,16,128]{2,1,0:T(8,128)S(1)} %collective-permute-done.refs_1_, f32[16,16,128]{2,1,0:T(8,128)S(1)} %collective-permute-done.1.refs_2_, ...), custom_call_target="tpu_custom_call" | custom-call | tf_op jit(solution)/shard_map/observed/pallas_call | solution.py:380
  19.5 0.0 copy-start.3
  19.5 0.8 fusion.1
  20.3 1.3 %collective-permute-start.5 = (f32[9,64,128]{2,1,0:T(8,128)}, f32[9,64,128]{2,1,0:T(8,128)S(1)}, u32[]{:S(2)}, u32[]{:S(2)}) collective-permute-start(f32[9,64,128]{2,1,0:T(8,128)} %get-tuple-element.40), channel_id=1, source_target_pairs={{1,0},{2,1},{3,2},{4,3},{5,4},{6,5},{7,6},{9,8},{10,9},{11,10},{12... | collective-permute-start | bytes 884744 | tf_op jit(solution)/shard_map/ppermute | solution.py:407
  21.6 3.0 %collective-permute-start.4 = (f32[9,64,128]{2,1,0:T(8,128)S(1)}, f32[9,64,128]{2,1,0:T(8,128)S(1)}, u32[]{:S(2)}, u32[]{:S(2)}) collective-permute-start(f32[9,64,128]{2,1,0:T(8,128)S(1)} %get-tuple-element.41), channel_id=1, source_target_pairs={{0,1},{1,2},{2,3},{3,4},{4,5},{5,6},{6,7},{8,9},{9,10},{10,11},{11... | collective-permute-start | bytes 884744 | tf_op jit(solution)/shard_map/ppermute | solution.py:406
  24.7 1.2 %collective-permute-start.3 = (f32[1,1,1152]{2,1,0:T(1,128)S(1)}, f32[1,1,1152]{2,1,0:T(1,128)S(1)}, u32[]{:S(2)}, u32[]{:S(2)}) collective-permute-start(f32[1,1,1152]{2,1,0:T(1,128)S(1)} %constant_dynamic-slice_fusion.2), channel_id=1, source_target_pairs={{0,1},{1,0},{2,3},{3,2},{4,5},{5,4},{6,7},{7,6},{8,9},{9,8},{10,11... | collective-permute-start | bytes 13832 | tf_op jit(solution)/shard_map/ppermute | solution.py:397
  25.8 0.8 collective-permute-done.3
  26.7 0.7 broadcast_in_dim.22
  27.4 4.0 %all-to-all-start = ((f32[32,1,1152]{2,1,0:T(1,128)}), f32[32,1,1152]{2,1,0:T(1,128)S(1)}, u32[]{:S(2)}, u32[]{:S(2)}) async-start(f32[32,1,1152]{2,1,0:T(1,128)} %broadcast_in_dim.22), calls=%async_computation | async-start | bytes 294912 | tf_op jit(solution)/shard_map/all_to_all | solution.py:400
  31.4 0.0 collective-permute-done.7.refs_5_.refs_6_
  31.4 0.0 collective-permute-done.6.refs_3_.refs_4_
  31.4 0.0 collective-permute-done.5.refs_2_.refs_3_
  31.4 0.0 collective-permute-done.4.refs_0_.refs_1_
  31.4 1.3 %strips.1 = (f32[3,136,128]{2,1,0:T(8,128)S(1)}, f32[3,136,128]{2,1,0:T(8,128)S(1)}) custom-call(f32[9,64,128]{2,1,0:T(8,128)S(1)} %collective-permute-done.4.refs_0_.refs_1_, f32[16,64,128]{2,1,0:T(8,128)S(1)} %get-tuple-element.21.refs_1_.refs_2_, f32[9,64,128]{2,1,0:T(8,128)S(1)} %collective-permute-done.5.refs_2_.refs_3_, ...), custom_call_target="tpu_custom_call" | custom-call | tf_op jit(solution)/shard_map/strips/pallas_call | solution.py:380
  32.7 3.7 %collective-permute-start.8 = (f32[3,136,128]{2,1,0:T(8,128)S(1)}, f32[3,136,128]{2,1,0:T(8,128)S(1)}, u32[]{:S(2)}, u32[]{:S(2)}) collective-permute-start(f32[3,136,128]{2,1,0:T(8,128)S(1)} %get-tuple-element.22), channel_id=1, source_target_pairs={{8,0},{16,8},{24,16},{0,24},{9,1},{17,9},{25,17},{1,25},{10,2},{18... | collective-permute-start | bytes 626696 | tf_op jit(solution)/shard_map/ppermute | solution.py:446
  36.3 0.0 collective-permute-start.9
  36.3 0.0 copy-done.3
  36.4 0.1 copy.7.modes_ref
  36.4 3.7 %start.1.rows_ref = f32[48,64]{1,0:T(8,128)S(1)} custom-call(f32[64,48]{1,0:T(8,128)S(1)} %copy.7.modes_ref), custom_call_target="tpu_custom_call" | custom-call | tf_op jit(solution)/shard_map/start/pallas_call | solution.py:380
  40.1 0.0 all-to-all-done.parts_ref
  40.1 4.6 %modes.3 = (f32[48,64]{1,0:T(8,128)S(1)}, f32[64,64]{1,0:T(8,128)S(1)}) custom-call(f32[32,1,1152]{2,1,0:T(1,128)S(1)} %all-to-all-done.parts_ref, f32[48,64]{1,0:T(8,128)S(1)} %start.1.rows_ref), custom_call_target="tpu_custom_call" | custom-call | tf_op jit(solution)/shard_map/modes/pallas_call | solution.py:380
  44.7 0.0 collective-permute-done.8.refs_7_
  44.7 2.7 %collective-permute-done.9.refs_8_ = f32[3,136,128]{2,1,0:T(8,128)S(1)} collective-permute-done((f32[3,136,128]{2,1,0:T(8,128)S(1)}, f32[3,136,128]{2,1,0:T(8,128)S(1)}, u32[]{:S(2)}, u32[]{:S(2)}) %collective-permute-start.9) | collective-permute-done | bytes 208928 | tf_op jit(solution)/shard_map/ppermute | solution.py:445
  47.4 4.2 %sweep0.1 = (f32[34,64,256]{2,1,0:T(8,128)S(1)}, f32[34,64,256]{2,1,0:T(8,128)S(1)}, f32[34,1,256]{2,1,0:T(1,128)S(1)}, f32[34,64,256]{2,1,0:T(8,128)S(1)}, f32[2,1,1152]{2,1,0:T(1,128)S(1)}) custom-call(f32[64,64]{1,0:T(8,128)S(1)} %get-tuple-element.20.refs_0_, f32[9,64,128]{2,1,0:T(8,128)S(1)} %collective-permute-done.4.refs_0_.refs_1_, ...), custom_call_target="tpu_custom_call" | custom-call | tf_op jit(solution)/shard_map/sweep0/pallas_call | solution.py:380
  51.6 0.1 collective-permute-start.10
  51.7 1.2 %collective-permute-done.10 = f32[1,1,1152]{2,1,0:T(1,128)S(1)} collective-permute-done((f32[1,1,1152]{2,1,0:T(1,128)S(1)}, f32[1,1,1152]{2,1,0:T(1,128)S(1)}, u32[]{:S(2)}, u32[]{:S(2)}) %collective-permute-start.10) | collective-permute-done | bytes 4640 | tf_op jit(solution)/shard_map/ppermute | solution.py:397
  52.8 0.1 broadcast_in_dim.24
  52.9 11.6 %all_to_all.15.parts_ref = f32[32,1,1152]{2,1,0:T(1,128)S(1)} all-to-all(f32[32,1,1152]{2,1,0:T(1,128)S(1)} %broadcast_in_dim.24), channel_id=1, replica_groups=mesh['wide'=4,'band'=8] {'wide','band'}, dimensions={0} | all-to-all | bytes 294912 | tf_op jit(solution)/shard_map/all_to_all | solution.py:400
  64.6 4.7 %modes.4 = (f32[48,64]{1,0:T(8,128)S(1)}, f32[64,64]{1,0:T(8,128)S(1)}) custom-call(f32[32,1,1152]{2,1,0:T(1,128)S(1)} %all_to_all.15.parts_ref, f32[48,64]{1,0:T(8,128)S(1)} %get-tuple-element.25.rows_ref), custom_call_target="tpu_custom_call" | custom-call | tf_op jit(solution)/shard_map/modes/pallas_call | solution.py:380
  69.3 3.5 %sweep1.1 = (f32[34,64,256]{2,1,0:T(8,128)S(1)}, f32[2,1,1152]{2,1,0:T(1,128)S(1)}) custom-call(f32[64,64]{1,0:T(8,128)S(1)} %get-tuple-element.26.last_ref, f32[34,64,256]{2,1,0:T(8,128)S(1)} %get-tuple-element.27.f_ref, f32[34,64,256]{2,1,0:T(8,128)S(1)} %get-tuple-element.28.seen_ref, f32[34,64,256]{2,1,0:T(8,128)S(1)} %get-tuple-element.29.gap_ref, ...), custom_call_target="tpu_custom_call" | custom-call | tf_op jit(solution)/shard_map/sweep1/pallas_call | solution.py:380
  72.8 0.3 collective-permute-start.11
  73.1 0.9 collective-permute-done.11
  74.0 0.1 broadcast_in_dim.26
  74.1 10.3 %all_to_all.16.parts_ref = f32[32,1,1152]{2,1,0:T(1,128)S(1)} all-to-all(f32[32,1,1152]{2,1,0:T(1,128)S(1)} %broadcast_in_dim.26), channel_id=1, replica_groups=mesh['wide'=4,'band'=8] {'wide','band'}, dimensions={0} | all-to-all | bytes 294912 | tf_op jit(solution)/shard_map/all_to_all | solution.py:400
  84.4 4.6 %modes.5 = (f32[48,64]{1,0:T(8,128)S(1)}, f32[64,64]{1,0:T(8,128)S(1)}) custom-call(f32[32,1,1152]{2,1,0:T(1,128)S(1)} %all_to_all.16.parts_ref, f32[48,64]{1,0:T(8,128)S(1)} %get-tuple-element.32.rows_ref), custom_call_target="tpu_custom_call" | custom-call | tf_op jit(solution)/shard_map/modes/pallas_call | solution.py:380
  89.0 2.9 %sweep2.1 = (f32[64,16,128]{2,1,0:T(8,128)}, f32[64,48]{1,0:T(8,128)S(1)}) custom-call(f32[64,64]{1,0:T(8,128)S(1)} %get-tuple-element.33.last_ref, f32[34,64,256]{2,1,0:T(8,128)S(1)} %get-tuple-element.34.f_ref, f32[34,64,256]{2,1,0:T(8,128)S(1)} %get-tuple-element.28.seen_ref, f32[34,64,256]{2,1,0:T(8,128)S(1)} %get-tuple-element.29.gap_ref, ...), custom_call_target="tpu_custom_call" | custom-call | tf_op jit(solution)/shard_map/sweep2/pallas_call | solution.py:380
  91.9 0.7 copy.8
  (7 shorter events, 0.2 us)
Async XLA Ops:
  1.8 12.9 %collective-permute-start.2 = (f32[16,16,128]{2,1,0:T(8,128)S(1)}, f32[16,16,128]{2,1,0:T(8,128)S(1)}, u32[]{:S(2)}, u32[]{:S(2)}) collective-permute-start(f32[16,16,128]{2,1,0:T(8,128)S(1)} %get-tuple-element.42), channel_id=1, source_target_pairs={{0,24},{8,16},{16,8},{24,0},{1,25},{9,17},{17,9},{25,1},{2,26},{10... | collective-permute-start | bytes 393224 | tf_op jit(solution)/shard_map/ppermute | solution.py:421
  6.9 7.8 %collective-permute-start = (f32[16,16,128]{2,1,0:T(8,128)S(1)}, f32[16,16,128]{2,1,0:T(8,128)S(1)}, u32[]{:S(2)}, u32[]{:S(2)}) collective-permute-start(f32[16,16,128]{2,1,0:T(8,128)S(1)} %get-tuple-element.43), channel_id=1, source_target_pairs={{0,8},{8,0},{16,24},{24,16},{1,9},{9,1},{17,25},{25,17},{2,10},{10... | collective-permute-start | bytes 393224 | tf_op jit(solution)/shard_map/ppermute | solution.py:421
  6.9 11.1 %collective-permute-start.1 = (f32[16,16,128]{2,1,0:T(8,128)S(1)}, f32[16,16,128]{2,1,0:T(8,128)S(1)}, u32[]{:S(2)}, u32[]{:S(2)}) collective-permute-start(f32[16,16,128]{2,1,0:T(8,128)S(1)} %get-tuple-element.45), channel_id=1, source_target_pairs={{0,16},{8,24},{16,0},{24,8},{1,17},{9,25},{17,1},{25,9},{2,18},{10... | collective-permute-start | bytes 393224 | tf_op jit(solution)/shard_map/ppermute | solution.py:421
  7.6 1.0 %copy-start = (s32[64,16,128]{2,1,0:T(8,128)S(1)}, s32[64,16,128]{2,1,0:T(8,128)}, u32[]{:S(2)}) copy-start(s32[64,16,128]{2,1,0:T(8,128)} %obs_ref.1) | copy-start | bytes 1572868
  8.6 0.7 copy-start.1
  9.3 0.7 copy-start.2
  10.3 21.1 %collective-permute-start.7 = (f32[9,72,128]{2,1,0:T(8,128)S(1)}, f32[9,72,128]{2,1,0:T(8,128)S(1)}, u32[]{:S(2)}, u32[]{:S(2)}) collective-permute-start(f32[9,72,128]{2,1,0:T(8,128)S(1)} %get-tuple-element.38), channel_id=1, source_target_pairs={{1,0},{2,1},{3,2},{4,3},{5,4},{6,5},{7,6},{9,8},{10,9},{11,10},{12... | collective-permute-start | bytes 995336 | tf_op jit(solution)/shard_map/ppermute | solution.py:407
  11.6 19.8 %collective-permute-start.6 = (f32[9,72,128]{2,1,0:T(8,128)S(1)}, f32[9,72,128]{2,1,0:T(8,128)S(1)}, u32[]{:S(2)}, u32[]{:S(2)}) collective-permute-start(f32[9,72,128]{2,1,0:T(8,128)S(1)} %get-tuple-element.39), channel_id=1, source_target_pairs={{0,1},{1,2},{2,3},{3,4},{4,5},{5,6},{6,7},{8,9},{9,10},{10,11},{11... | collective-permute-start | bytes 995336 | tf_op jit(solution)/shard_map/ppermute | solution.py:406
  19.5 16.8 %copy-start.3 = (f32[64,48]{0,1:T(8,128)S(1)}, f32[64,48]{0,1:T(8,128)}, u32[]{:S(2)}) copy-start(f32[64,48]{0,1:T(8,128)} %param.9) | copy-start | bytes 36868
  20.3 11.1 %collective-permute-start.5 = (f32[9,64,128]{2,1,0:T(8,128)}, f32[9,64,128]{2,1,0:T(8,128)S(1)}, u32[]{:S(2)}, u32[]{:S(2)}) collective-permute-start(f32[9,64,128]{2,1,0:T(8,128)} %get-tuple-element.40), channel_id=1, source_target_pairs={{1,0},{2,1},{3,2},{4,3},{5,4},{6,5},{7,6},{9,8},{10,9},{11,10},{12... | collective-permute-start | bytes 884744 | tf_op jit(solution)/shard_map/ppermute | solution.py:407
  21.6 9.8 %collective-permute-start.4 = (f32[9,64,128]{2,1,0:T(8,128)S(1)}, f32[9,64,128]{2,1,0:T(8,128)S(1)}, u32[]{:S(2)}, u32[]{:S(2)}) collective-permute-start(f32[9,64,128]{2,1,0:T(8,128)S(1)} %get-tuple-element.41), channel_id=1, source_target_pairs={{0,1},{1,2},{2,3},{3,4},{4,5},{5,6},{6,7},{8,9},{9,10},{10,11},{11... | collective-permute-start | bytes 884744 | tf_op jit(solution)/shard_map/ppermute | solution.py:406
  24.7 2.0 %collective-permute-start.3 = (f32[1,1,1152]{2,1,0:T(1,128)S(1)}, f32[1,1,1152]{2,1,0:T(1,128)S(1)}, u32[]{:S(2)}, u32[]{:S(2)}) collective-permute-start(f32[1,1,1152]{2,1,0:T(1,128)S(1)} %constant_dynamic-slice_fusion.2), channel_id=1, source_target_pairs={{0,1},{1,0},{2,3},{3,2},{4,5},{5,4},{6,7},{7,6},{8,9},{9,8},{10,11... | collective-permute-start | bytes 13832 | tf_op jit(solution)/shard_map/ppermute | solution.py:397
  27.4 12.7 %all-to-all-start = ((f32[32,1,1152]{2,1,0:T(1,128)}), f32[32,1,1152]{2,1,0:T(1,128)S(1)}, u32[]{:S(2)}, u32[]{:S(2)}) async-start(f32[32,1,1152]{2,1,0:T(1,128)} %broadcast_in_dim.22), calls=%async_computation | async-start | bytes 294912 | tf_op jit(solution)/shard_map/all_to_all | solution.py:400
  32.7 12.0 %collective-permute-start.8 = (f32[3,136,128]{2,1,0:T(8,128)S(1)}, f32[3,136,128]{2,1,0:T(8,128)S(1)}, u32[]{:S(2)}, u32[]{:S(2)}) collective-permute-start(f32[3,136,128]{2,1,0:T(8,128)S(1)} %get-tuple-element.22), channel_id=1, source_target_pairs={{8,0},{16,8},{24,16},{0,24},{9,1},{17,9},{25,17},{1,25},{10,2},{18... | collective-permute-start | bytes 626696 | tf_op jit(solution)/shard_map/ppermute | solution.py:446
  36.3 11.0 %collective-permute-start.9 = (f32[3,136,128]{2,1,0:T(8,128)S(1)}, f32[3,136,128]{2,1,0:T(8,128)S(1)}, u32[]{:S(2)}, u32[]{:S(2)}) collective-permute-start(f32[3,136,128]{2,1,0:T(8,128)S(1)} %get-tuple-element.23), channel_id=1, source_target_pairs={{0,8},{8,16},{16,24},{24,0},{1,9},{9,17},{17,25},{25,1},{2,10},{10... | collective-permute-start | bytes 626696 | tf_op jit(solution)/shard_map/ppermute | solution.py:445
  51.6 1.2 %collective-permute-start.10 = (f32[1,1,1152]{2,1,0:T(1,128)S(1)}, f32[1,1,1152]{2,1,0:T(1,128)S(1)}, u32[]{:S(2)}, u32[]{:S(2)}) collective-permute-start(f32[1,1,1152]{2,1,0:T(1,128)S(1)} %constant_dynamic-slice_fusion.1), channel_id=1, source_target_pairs={{0,1},{1,0},{2,3},{3,2},{4,5},{5,4},{6,7},{7,6},{8,9},{9,8},{10,11... | collective-permute-start | bytes 13832 | tf_op jit(solution)/shard_map/ppermute | solution.py:397
  72.8 1.2 %collective-permute-start.11 = (f32[1,1,1152]{2,1,0:T(1,128)S(1)}, f32[1,1,1152]{2,1,0:T(1,128)S(1)}, u32[]{:S(2)}, u32[]{:S(2)}) collective-permute-start(f32[1,1,1152]{2,1,0:T(1,128)S(1)} %constant_dynamic-slice_fusion), channel_id=1, source_target_pairs={{0,1},{1,0},{2,3},{3,2},{4,5},{5,4},{6,7},{7,6},{8,9},{9,8},{10,11... | collective-permute-start | bytes 13832 | tf_op jit(solution)/shard_map/ppermute | solution.py:397

commit v3 on v2

v3 whole, which is shorter than its diff:
```python
import functools
import jax
import jax.numpy as jnp
from jax import lax
from jax.experimental import pallas as pl
from jax.experimental.pallas import tpu as pltpu
from jax.sharding import PartitionSpec as P

OUTER = 3
INNER = 3
PASSES = 3
HALO = OUTER * PASSES
LANES = 128
EXTRA = 8
CHUNK = 8
BATCH = 2
FLOOR = 0.1

F32 = jnp.float32
BF16 = jnp.bfloat16
VMEM = pl.BlockSpec(memory_space=pltpu.VMEM)
SMEM = pl.BlockSpec(memory_space=pltpu.SMEM)


def highest(left, right, left_dim, right_dim):
    return lax.dot_general(
        left,
        right,
        (((left_dim,), (right_dim,)), ((), ())),
        precision=lax.Precision.HIGHEST,
        preferred_element_type=F32,
    )


def halves(value):
    high = value.astype(BF16)
    return high, (value - high.astype(F32)).astype(BF16)


def thirds(value):
    first = value.astype(BF16)
    rest = value - first.astype(F32)
    second = rest.astype(BF16)
    return first, second, (rest - second.astype(F32)).astype(BF16)


def grid_of(shape, axis):
    return lax.broadcasted_iota(jnp.int32, shape, axis)


def covariance_of(rows_of, count):
    days = None
    total = None
    for start in range(0, count, 2):
        pair = jnp.concatenate([rows_of(start), rows_of(start + 1)], axis=1)
        days = pair.shape[0]
        stack = jnp.concatenate(thirds(pair), axis=0)
        part = lax.dot_general(
            stack, stack, (((1,), (1,)), ((), ())), preferred_element_type=F32
        )
        total = part if total is None else total + part
    block = lambda i, j: total[i * days : (i + 1) * days, j * days : (j + 1) * days]
    small = block(2, 2) + (block(1, 2) + block(2, 1))
    small = small + (block(0, 2) + block(2, 0)) + block(1, 1)
    return block(0, 0) + ((block(0, 1) + block(1, 0)) + small)


def pack_symmetric(packed_ref, cov):
    half = cov.shape[0] // 2
    quarter = half // 2
    upper = grid_of((half, half), 1) >= grid_of((half, half), 0)
    same = grid_of((half, half), 1) == grid_of((half, half), 0)
    low = cov[half:, half:]
    mixed = jnp.where(upper, cov[:half, :half], low)
    cross = cov[:half, half:]
    body = jnp.concatenate(
        [mixed[:quarter], cross[:quarter], mixed[quarter:], cross[quarter:]], axis=1
    )
    diagonal = jnp.sum(jnp.where(same, low, 0.0), axis=0, keepdims=True)
    diagonal = jnp.concatenate([diagonal, jnp.zeros((1, LANES - half), F32)], axis=1)
    each = quarter // 2
    for side in range(2):
        for row in range(each):
            packed_ref[side, :, row * LANES : (row + 1) * LANES] = body[
                side * each + row : side * each + row + 1
            ]
        packed_ref[side, :, each * LANES :] = (
            diagonal if side == 0 else jnp.zeros((1, LANES), F32)
        )


def unpack_symmetric(parts_ref, body_ref, days):
    half = days // 2
    quarter = half // 2
    each = quarter // 2
    sides = []
    for side in range(2):
        values = [parts_ref[j] for j in range(side, parts_ref.shape[0], 2)]
        while len(values) > 1:
            paired = [values[i] + values[i + 1] for i in range(0, len(values) - 1, 2)]
            values = paired + values[len(paired) * 2 :]
        sides.append(values[0])
        for row in range(each):
            body_ref[side * each + row : side * each + row + 1, :] = values[0][
                :, row * LANES : (row + 1) * LANES
            ]
    body = body_ref[...]
    diagonal = sides[0][:, each * LANES : each * LANES + half]
    mixed = jnp.concatenate([body[:, :half], body[:, 2 * half : 3 * half]], axis=0)
    cross = jnp.concatenate([body[:, half : 2 * half], body[:, 3 * half :]], axis=0)
    col, row = grid_of((half, half), 1), grid_of((half, half), 0)
    flipped = mixed.T
    high = jnp.where(col >= row, mixed, flipped)
    low = jnp.where(col < row, mixed, flipped)
    low = jnp.where(col == row, jnp.broadcast_to(diagonal, (half, half)), low)
    top = jnp.concatenate([high, cross], axis=1)
    bottom = jnp.concatenate([cross.T, low], axis=1)
    return jnp.concatenate([top, bottom], axis=0)


def spread(value, at):
    return jnp.broadcast_to(value[at : at + 1], value.shape)


def column_spread(value, at, zero):
    return jnp.broadcast_to(value[:, at : at + 1], value.shape) + zero


def block_pivots(lead, own, zero):
    sublane = grid_of(lead.shape, 0)
    below, solved = lead, lead
    columns = [column_spread(lead, own + m, zero) for m in range(8)]
    pivots = jnp.ones(lead.shape, F32)
    for k in range(0, 8, 2):
        left, right = columns[k], columns[k + 1]
        a, b, c = spread(left, k), spread(left, k + 1), spread(right, k + 1)
        scale = 1.0 / (a * c - b * b)
        ratio = b * (1.0 / a)
        first, second = sublane == k, sublane == k + 1
        g0 = (left * c - right * b) * scale
        g1 = (right * a - left * b) * scale
        h0 = jnp.where(first, 1.0 - c * scale, jnp.where(second, b * scale, g0))
        h1 = jnp.where(first, b * scale, jnp.where(second, 1.0 - a * scale, g1))
        for m in range(k + 2, 8):
            top, low = spread(columns[m], k), spread(columns[m], k + 1)
            columns[m] = columns[m] - (h0 * top + h1 * low)
        solved = solved - (h0 * spread(solved, k) + h1 * spread(solved, k + 1))
        f0 = jnp.where(sublane > k + 1, g0, jnp.where(second, ratio, 0.0))
        f1 = jnp.where(sublane > k + 1, g1, 0.0)
        below = below - (f0 * spread(below, k) + f1 * spread(below, k + 1))
        pivots = jnp.where(first, a, jnp.where(second, c - b * ratio, pivots))
    return below, solved, pivots


def orthonormal_rows(rows):
    count, width = rows.shape
    gram = highest(rows, rows, 1, 1)
    pad = jnp.zeros((count, LANES - count - width), F32)
    table = jnp.concatenate([gram, rows, pad], axis=1)
    groups = [table[8 * i : 8 * i + 8] for i in range(count // 8)]
    lane, sublane = grid_of((8, LANES), 1), grid_of((8, LANES), 0)
    zero = jnp.where(lane < 0, 1.0, 0.0)
    outs, worst = [], None
    for i, lead in enumerate(groups):
        below, solved, pivots = block_pivots(lead, 8 * i, zero)
        factors = [spread(solved, m) for m in range(8)]
        for j in range(i + 1, len(groups)):
            terms = [
                column_spread(groups[j], 8 * i + m, zero) * factors[m] for m in range(8)
            ]
            while len(terms) > 1:
                terms = [terms[n] + terms[n + 1] for n in range(0, len(terms), 2)]
            groups[j] = groups[j] - terms[0]
        start = jnp.where(lane == sublane + 8 * i, table[8 * i : 8 * i + 8], 0.0)
        kept = pivots / jnp.sum(start, axis=1, keepdims=True)
        worst = kept if worst is None else jnp.minimum(worst, kept)
        outs.append(below[:, count : count + width] * lax.rsqrt(pivots)[:, :width])
    return jnp.concatenate(outs, axis=0), jnp.min(worst)


def careful_rows(rows):
    count, width = rows.shape
    gram = highest(rows, rows, 1, 1)
    pad = jnp.zeros((count, LANES - count - width), F32)
    table = jnp.concatenate([gram, rows, pad], axis=1)
    groups = [table[8 * i : 8 * i + 8] for i in range(count // 8)]
    sublane = grid_of((8, LANES), 0)
    pivots = []
    repeat = lambda row: jnp.broadcast_to(row, (8, LANES))
    for k in range(0, count, 2):
        i, s = k // 8, k % 8
        first = [jnp.broadcast_to(g[:, k : k + 1], (8, LANES)) for g in groups[i:]]
        second = [jnp.broadcast_to(g[:, k + 1 : k + 2], (8, LANES)) for g in groups[i:]]
        row0, row1 = repeat(groups[i][s : s + 1]), repeat(groups[i][s + 1 : s + 2])
        a = repeat(first[0][s : s + 1])
        b = repeat(first[0][s + 1 : s + 2])
        c = repeat(second[0][s + 1 : s + 2])
        det = a * c - b * b
        scale = 1.0 / det
        h0, h1, h2 = c * scale, b * scale, a * scale
        w0 = h0 * row0 - h1 * row1
        w1 = h2 * row1 - h1 * row0
        ratio = b / a
        pivots.append((a, c - b * ratio))
        for j in range(i, len(groups)):
            c0, c1 = first[j - i], second[j - i]
            updated = groups[j] - (c0 * w0 + c1 * w1)
            if j == i:
                updated = jnp.where(sublane > s + 1, updated, groups[j])
                updated = jnp.where(sublane == s + 1, row1 - ratio * row0, updated)
            groups[j] = updated
    outs = []
    for i, g in enumerate(groups):
        d = jnp.zeros((8, LANES), F32)
        for s in range(8):
            d = jnp.where(sublane == s, pivots[(8 * i + s) // 2][s % 2], d)
        outs.append(g[:, count : count + width] * lax.rsqrt(d)[:, :width])
    return jnp.concatenate(outs, axis=0)


def start_kernel(modes_ref, rows_ref):
    modes = modes_ref[...]
    rows_ref[...], kept = orthonormal_rows(modes)

    @pl.when(jnp.logical_not(kept >= FLOOR))
    def _():
        rows_ref[...] = careful_rows(modes)


def modes_kernel(parts_ref, rows_ref, new_ref, last_ref, body_ref):
    rows = rows_ref[...]
    days = rows.shape[1]
    cov = unpack_symmetric(parts_ref, body_ref, days)
    same = grid_of((days, days), 1) == grid_of((days, days), 0)
    peak = jnp.max(jnp.where(same, cov, 0.0), keepdims=True)
    cov = cov * (1.0 / peak)
    moved = highest(rows, cov, 1, 0)
    twice = highest(cov, cov, 1, 0)
    new, kept = orthonormal_rows(highest(moved, twice, 1, 0))
    new_ref[...] = new
    last_ref[...] = highest(new, new, 0, 0)

    @pl.when(jnp.logical_not(kept >= FLOOR))
    def _():
        def step(_, held):
            return careful_rows(highest(held, cov, 1, 0))

        again = lax.fori_loop(0, INNER, step, rows)
        new_ref[...] = again
        last_ref[...] = highest(again, again, 0, 0)


def static_kernel(obs_ref, ocean_ref, diff_ref, stat_ref):
    days, rows, cols = obs_ref.shape
    flat = obs_ref.reshape(days * rows, cols)
    for r in range(rows):
        seen = flat[pl.ds(r, days, stride=rows), :]
        ocean = ocean_ref[r : r + 1, :]
        stat_ref[r, :days, :] = ((1 - seen) * ocean).astype(F32)
        rest = jnp.concatenate(
            [
                diff_ref[r : r + 1, :],
                ocean.astype(F32),
                jnp.zeros((EXTRA - 2, cols), F32),
            ],
            axis=0,
        )
        stat_ref[r, days:, :] = rest


def observed_kernel(blocks, offs_ref, *refs):
    piece_refs = refs[:blocks]
    stat_ref, _, seen_ref, head_ref, tail_ref, packed_ref = refs[blocks:]
    rows, days, cols = seen_ref.shape
    each = piece_refs[0].shape[0]
    for r in range(rows):
        ocean = stat_ref[r, days + 1 : days + 2, :]
        for b, piece_ref in enumerate(piece_refs):
            flat = piece_ref.reshape(each * rows, cols)
            start = pl.multiple_of(offs_ref[b], each)
            gap = stat_ref[r, pl.ds(start, each), :]
            value = flat[pl.ds(r, each, stride=rows), :]
            seen_ref[r, pl.ds(start, each), :] = value * (ocean - gap)
    for r in range(HALO):
        head_ref[r] = seen_ref[r]
        tail_ref[r] = seen_ref[rows - HALO + r]
    pack_symmetric(packed_ref, covariance_of(lambda r: seen_ref[r], rows))


def row_source(refs, rows, e):
    north, main, south = refs
    if e < HALO:
        return north[e]
    if e < HALO + rows:
        return main[e - HALO]
    return south[e - HALO - rows]


def strip_rows(sweep, total):
    return range(sweep * PASSES + 1, total - sweep * PASSES - 1)


def strip_place(sweep, e, cols):
    per = cols // (2 * PASSES)
    at = e - sweep * PASSES - 1
    return at // per, at % per * 2 * PASSES


def write_strips(sweep, total, value_of, strip_ref, at):
    _, _, cols = strip_ref.shape
    tiles = {}
    for e in strip_rows(sweep, total):
        value = value_of(e)
        tile, place = strip_place(sweep, e, cols)
        lane = grid_of(value.shape, 1)
        here = (lane >= place) & (lane < place + 2 * PASSES)
        moved = pltpu.roll(value, place + PASSES, 1)
        tiles[tile] = jnp.where(here, moved, tiles.get(tile, 0.0))
    for tile, value in tiles.items():
        strip_ref[tile, at, :] = value


def read_strips(sweep, total, west_ref, east_ref, at):
    _, _, cols = west_ref.shape
    merged = []
    for tile in range(west_ref.shape[0]):
        west, east = west_ref[tile, at, :], east_ref[tile, at, :]
        lane = grid_of(west.shape, 1)
        merged.append(jnp.where(lane % (2 * PASSES) < PASSES, west, east))

    def side(e):
        lane = grid_of(merged[0].shape, 1)
        if e not in strip_rows(sweep, total):
            return jnp.zeros(merged[0].shape, F32)
        tile, place = strip_place(sweep, e, cols)
        moved = pltpu.roll(merged[tile], cols - place - PASSES, 1)
        return jnp.where((lane < PASSES) | (lane >= cols - PASSES), moved, 0.0)

    return side


def first_strip_kernel(*refs):
    seen, stat, strip_ref = refs[0:3], refs[3:6], refs[6]
    rows, days, _ = seen[1].shape
    total = rows + 2 * HALO
    write_strips(0, total, lambda e: row_source(seen, rows, e), strip_ref, slice(0, days))
    write_strips(0, total, lambda e: row_source(stat, rows, e), strip_ref, slice(days, None))


def strip_kernel(sweep, f_ref, strip_ref):
    cols = strip_ref.shape[2]
    total = f_ref.shape[0]
    write_strips(sweep, total, lambda e: f_ref[e, :, :cols], strip_ref, slice(None))


def project_rows(last, row_of, out_ref, seen_ref, gap_ref, low, high):
    p0, p1 = halves(last)
    weights = jnp.concatenate([p0, p0, p1, p1], axis=1)

    for e in range(low, high):
        f0, f1 = halves(row_of(e))
        stack = jnp.concatenate([f0, f1, f0, f1], axis=0)
        recon = jnp.dot(weights, stack, preferred_element_type=F32)
        out_ref[e] = seen_ref[e] + gap_ref[e] * recon


def beside_matrix(width):
    row, col = grid_of((width, width), 0), grid_of((width, width), 1)
    apart = jnp.abs(row - col)
    near = jnp.where((apart == 1) | (apart == width - 1), 1.0, 0.0)
    return jnp.where(apart == 0, -4.0, near).astype(BF16)


def smooth_rows(near, f_ref, out_ref, gap_ref, diff_ref, low, high):
    _, days, width = f_ref.shape
    for e in range(low, high, BATCH):
        value = f_ref[e : e + BATCH].reshape(BATCH * days, width)
        f0, f1 = halves(value)
        lap = jnp.dot(f0, near, preferred_element_type=F32)
        lap = lap + jnp.dot(f1, near, preferred_element_type=F32)
        for k in range(BATCH):
            coef = jnp.broadcast_to(diff_ref[e + k], (CHUNK, width))
            for at in range(0, days, CHUNK):
                part = slice(at, at + CHUNK)
                around = f_ref[e + k - 1, part, :] + f_ref[e + k + 1, part, :]
                around = around + lap[k * days + at : k * days + at + CHUNK]
                out_ref[e + k, part, :] = (
                    f_ref[e + k, part, :] + (gap_ref[e + k, part, :] * coef) * around
                )


def sweep_body(sweep, last, row_of, a_ref, b_ref, seen_ref, gap_ref, diff_ref):
    total = seen_ref.shape[0]
    edge = sweep * PASSES
    project_rows(last, row_of, a_ref, seen_ref, gap_ref, edge, total - edge)
    near = beside_matrix(seen_ref.shape[2])
    now, other = a_ref, b_ref
    for step in range(PASSES):
        edge += 1
        smooth_rows(near, now, other, gap_ref, diff_ref, edge, total - edge)
        now, other = other, now
    return now


def joined(f_ref, side, cols):
    return lambda e: jnp.concatenate([f_ref[e, :, :cols], side(e)], axis=1)


def first_kernel(*refs):
    last_ref = refs[0]
    seen, stat = refs[1:4], refs[4:7]
    west_ref, east_ref = refs[7:9]
    seen_ref, gap_ref, diff_ref, out_ref, packed_ref, a_ref = refs[9:]
    rows, days, cols = seen[1].shape
    total = rows + 2 * HALO
    seen_side = read_strips(0, total, west_ref, east_ref, slice(0, days))
    stat_side = read_strips(0, total, west_ref, east_ref, slice(days, None))
    for e in range(total):
        seen_ref[e, :, :cols] = row_source(seen, rows, e)
        seen_ref[e, :, cols:] = seen_side(e)
        main, side = row_source(stat, rows, e), stat_side(e)
        gap_ref[e, :, :cols] = main[:days]
        gap_ref[e, :, cols:] = side[:days]
        diff_ref[e, :, :cols] = main[days : days + 1]
        diff_ref[e, :, cols:] = side[days : days + 1]
    row_of = lambda e: seen_ref[e]
    now = sweep_body(0, last_ref[...], row_of, a_ref, out_ref, seen_ref, gap_ref, diff_ref)
    assert now is out_ref
    cov = covariance_of(lambda r: out_ref[HALO + r, :, :cols], rows)
    pack_symmetric(packed_ref, cov)


def next_kernel(sweep, *refs):
    last_ref, f_ref, west_ref, east_ref, seen_ref, gap_ref, diff_ref = refs[:7]
    out_ref, packed_ref, a_ref = refs[7:]
    total, cols = seen_ref.shape[0], west_ref.shape[2]
    side = read_strips(sweep, total, west_ref, east_ref, slice(None))
    row_of = joined(f_ref, side, cols)
    now = sweep_body(sweep, last_ref[...], row_of, a_ref, out_ref, seen_ref, gap_ref, diff_ref)
    assert now is out_ref
    cov = covariance_of(lambda r: out_ref[HALO + r, :, :cols], total - 2 * HALO)
    pack_symmetric(packed_ref, cov)


def end_kernel(sweep, *refs):
    last_ref, f_ref, west_ref, east_ref, seen_ref, gap_ref, diff_ref = refs[:7]
    out_ref, a_ref, b_ref = refs[7:]
    days, rows, cols = out_ref.shape
    side = read_strips(sweep, seen_ref.shape[0], west_ref, east_ref, slice(None))
    row_of = joined(f_ref, side, cols)
    now = sweep_body(sweep, last_ref[...], row_of, a_ref, b_ref, seen_ref, gap_ref, diff_ref)
    flat = out_ref.reshape(days * rows, cols)
    for r in range(rows):
        flat[pl.ds(r, days, stride=rows), :] = now[HALO + r, :, :cols]


def call(kernel, name, ins, outs, scratch=(), scalars=0):
    specs = [SMEM] * scalars + [VMEM] * (len(ins) - scalars)
    return pl.pallas_call(
        kernel,
        name=name,
        out_shape=[jax.ShapeDtypeStruct(s, F32) for s in outs],
        in_specs=specs,
        out_specs=[VMEM] * len(outs),
        scratch_shapes=[pltpu.VMEM(s, F32) for s in scratch],
        compiler_params=pltpu.CompilerParams(vmem_limit_bytes=24 * 2**20),
    )(*ins)


def pair_sums(packed):
    count = lax.axis_size("band")
    width = packed.shape[2]
    parity = lax.rem(lax.axis_index("band"), 2)
    mine = lax.dynamic_slice_in_dim(packed, parity, 1, 0)
    other = lax.dynamic_slice_in_dim(packed, 1 - parity, 1, 0)
    got = lax.ppermute(other, "band", [(i, i ^ 1) for i in range(count)])
    everyone = count * lax.axis_size("wide")
    return jnp.broadcast_to(mine + got, (everyone, 1, width))


def trade(copies):
    return lax.all_to_all(copies, ("wide", "band"), 0, 0, tiled=True)


def edges(head, cells, tail):
    count = lax.axis_size("band")
    north = lax.ppermute(tail, "band", [(i, i + 1) for i in range(count - 1)])
    south = lax.ppermute(head, "band", [(i + 1, i) for i in range(count - 1)])
    return [north, cells, south]


def beside(strip):
    count = lax.axis_size("wide")
    from_west = lax.ppermute(strip, "wide", [(i, (i + 1) % count) for i in range(count)])
    from_east = lax.ppermute(strip, "wide", [((i + 1) % count, i) for i in range(count)])
    return [from_west, from_east]


def shards(day_field, obs_mask, ocean_mask, diffusivity, start_modes):
    days, rows, cols = obs_mask.shape
    modes = start_modes.shape[1]
    count = lax.axis_size("wide")
    me = lax.axis_index("wide")
    pieces, offs = [], []
    for k in range(count):
        to = lambda i: i ^ k
        piece = lax.dynamic_slice_in_dim(day_field, to(me) * cols, cols, 2)
        if k:
            piece = lax.ppermute(piece, "wide", [(i, to(i)) for i in range(count)])
        pieces.append(piece)
        offs.append(to(me) * day_field.shape[0])
    offs = jnp.stack(offs).astype(jnp.int32)
    (stat,) = call(
        static_kernel, "static", [obs_mask, ocean_mask, diffusivity], [(rows, days + EXTRA, cols)]
    )
    stats = edges(stat[:HALO], stat, stat[rows - HALO :])
    (basis,) = call(start_kernel, "start", [start_modes.T], [(modes, days)])
    width = (days // 8 + 1) * LANES
    row_strip = (HALO, days, cols)
    seen, head, tail, packed = call(
        functools.partial(observed_kernel, count),
        "observed",
        [offs] + pieces + [stat, basis],
        [(rows, days, cols), row_strip, row_strip, (2, 1, width)],
        scalars=1,
    )
    seens = edges(head, seen, tail)
    total = rows + 2 * HALO
    strip_shape = lambda sweep, depth: (
        pl.cdiv(len(strip_rows(sweep, total)), cols // (2 * PASSES)),
        depth,
        cols,
    )
    wide_map, wide_row = (total, days, 2 * cols), (total, 1, 2 * cols)
    parts = trade(pair_sums(packed))
    (strip,) = call(
        first_strip_kernel, "strips0", seens + stats, [strip_shape(0, 2 * days + EXTRA)]
    )
    sides = beside(strip)
    for sweep in range(OUTER):
        basis, last = call(
            modes_kernel,
            "modes",
            [parts, basis],
            [(modes, days), (days, days)],
            [(days // 4, LANES)],
        )
        if sweep == 0:
            seen_w, gap_w, diff_w, filled, packed = call(
                first_kernel,
                "sweep0",
                [last] + seens + stats + sides,
                [wide_map, wide_map, wide_row, wide_map, (2, 1, width)],
                [wide_map],
            )
        elif sweep < OUTER - 1:
            filled, packed = call(
                functools.partial(next_kernel, sweep),
                f"sweep{sweep}",
                [last, filled] + sides + [seen_w, gap_w, diff_w],
                [wide_map, (2, 1, width)],
                [wide_map],
            )
        else:
            (out,) = call(
                functools.partial(end_kernel, sweep),
                f"sweep{sweep}",
                [last, filled] + sides + [seen_w, gap_w, diff_w],
                [(days, rows, cols)],
                [wide_map, wide_map],
            )
            return (out, basis.T)
        copies, held = lax.optimization_barrier((pair_sums(packed), filled))
        parts = trade(copies)
        (strip,) = call(
            functools.partial(strip_kernel, sweep + 1),
            f"strips{sweep + 1}",
            [held],
            [strip_shape(sweep + 1, days)],
        )
        sides = beside(strip)


def solution(mesh):
    placed = (
        P("wide", "band", None),
        P(None, "band", "wide"),
        P("band", "wide"),
        P("band", "wide"),
        P(),
    )
    return jax.shard_map(
        shards,
        mesh=mesh,
        in_specs=placed,
        out_specs=(P(None, "band", "wide"), P()),
        check_vma=False,
    )
```

time: 93.1 us -> 107 us (1.15); the launches traced: 92.6 us -> 108 us
  blocking collectives: 21.9 us -> 0 us
  local copies, waits for them, and re-layouts: 6.08 us -> 26.1 us
  starting transfers between devices: 23.7 us -> 38.7 us
  waiting for transfers between devices: 8.84 us -> 15.8 us
  Pallas kernels: 31.1 us -> 26.2 us
    all_to_all x2 -> x0, blocking collectives: 21.9 us -> none  [sum_parts(): return lax.all_to_all(copies, ('wide', 'band'), 0, 0, tiled=True)]
    unnamed x9 -> x46, local copies, waits for them, and re-layouts: 2.52 us -> 21.8 us
    all_to_all x1 -> x3, waiting for transfers between devices: 0.01 us -> 9.77 us  [trade(): return lax.all_to_all(copies, ('wide', 'band'), 0, 0, tiled=True)]
    all_to_all x1 -> x3, starting transfers between devices: 3.97 us -> 12 us  [trade(): return lax.all_to_all(copies, ('wide', 'band'), 0, 0, tiled=True)]
    ppermute x9 -> x13, starting transfers between devices: 13.9 us -> 21 us  [the longest x3 11 us: beside(): lax.ppermute(strip, 'wide', [((i + 1) % count, i) for i in range(count)])]
    pallas_call x10 -> x12, Pallas kernels: 31.1 us -> 26.2 us  [call(): pl.pallas_call(kernel, name=name, out_shape=[jax.ShapeDtypeStruct(s, F32)...]
    ppermute x3, waiting for transfers between devices: 3.29 us -> 0.01 us  [shards(): piece = lax.ppermute(piece, 'wide', [(i, to(i)) for i in range(count)])]
    broadcast_in_dim x3, local copies, waits for them, and re-layouts: 0.88 us -> 2.21 us  [pair_sums(): return jnp.broadcast_to(mine + got, (everyone, 1, width))]
  transfers between devices with their start and end apart: 13 -> 19, of which waited for: 5 -> 8; matrix products, arithmetic and copies ran while one was open for 2% -> 2% of each run, Pallas kernels for 12% -> 15%
where the time goes in v3:
time: 107 us; the launch traced here: 108 us
  starting transfers between devices  38.7 us (36%)
  Pallas kernels  26.2 us (24%)
  local copies, waits for them, and re-layouts  26.1 us (24%)
  waiting for transfers between devices  15.8 us (15%)
    pallas_call x12, Pallas kernels, call(): pl.pallas_call(kernel, name=name, out_shape=[jax.ShapeDtypeStruct(s, F32)...  26.2 us
    unnamed x46, local copies, waits for them, and re-layouts  21.8 us
    all_to_all x3, starting transfers between devices, trade(): return lax.all_to_all(copies, ('wide', 'band'), 0, 0, tiled=True)  12 us
    ppermute x3, starting transfers between devices, beside(): lax.ppermute(strip, 'wide', [((i + 1) % count, i) for i in range(count)])  11 us
    all_to_all x3, waiting for transfers between devices, trade(): return lax.all_to_all(copies, ('wide', 'band'), 0, 0, tiled=True)  9.77 us
    ppermute x2, starting transfers between devices, edges(): north = lax.ppermute(tail, 'band', [(i, i + 1) for i in range(count - 1)])  6.21 us
    ppermute x3, starting transfers between devices, shards(): piece = lax.ppermute(piece, 'wide', [(i, to(i)) for i in range(count)])  5.78 us
    ppermute x3, waiting for transfers between devices, pair_sums(): got = lax.ppermute(other, 'band', [(i, i ^ 1) for i in range(count)])  3.3 us
  transfers between devices with their start and end apart: 19, of which 8 were waited for; matrix products, arithmetic and copies ran while one was open for 2% of the time, Pallas kernels for 15%

profile of v3, /device:TPU:0, one launch (start us, length us, event | category | flops | bytes accessed | tf_op | source)
XLA Modules:
  0.0 107.9 jit_solution(14803137980230884460)
XLA Ops:
  0.7 1.1 %constant_dynamic-slice_fusion.3 = (f32[16,16,128]{2,1,0:T(8,128)S(1)}, f32[16,16,128]{2,1,0:T(8,128)S(1)}, f32[16,16,128]{2,1,0:T(8,128)S(1)}, f32[16,16,128]{2,1,0:T(8,128)S(1)}) fusion(f32[16,16,512]{2,1,0:T(8,128)} %param.5, s32[]{:T(128)S(6)} %select_n.25, s32[]{:T(128)S(6)} %select_n.23, s32[]{:T(128)S(6)} %select_n.22, s32[]{:T(128)S(6)} %select_n.24), kind=kLoop, calls=%fused_computation.6 | loop fusion | bytes 1048592 | tf_op jit(solution)/shard_map/dynamic_slice | solution.py:507
  1.8 5.1 %collective-permute-start.2 = (f32[16,16,128]{2,1,0:T(8,128)S(1)}, f32[16,16,128]{2,1,0:T(8,128)S(1)}, u32[]{:S(2)}, u32[]{:S(2)}) collective-permute-start(f32[16,16,128]{2,1,0:T(8,128)S(1)} %get-tuple-element.46), channel_id=1, source_target_pairs={{0,24},{8,16},{16,8},{24,0},{1,25},{9,17},{17,9},{25,1},{2,26},{10... | collective-permute-start | bytes 393224 | tf_op jit(solution)/shard_map/ppermute | solution.py:509
  7.0 0.0 collective-permute-start
  7.0 0.6 collective-permute-start.1
  7.6 1.0 copy-done.17
  8.6 0.7 copy-done.21
  9.3 0.7 copy-done.22
  10.0 0.2 static.1.refs_4_.refs_5_
  10.2 0.9 fusion
  11.1 1.3 %collective-permute-start.7 = (f32[9,72,128]{2,1,0:T(8,128)}, f32[9,72,128]{2,1,0:T(8,128)S(1)}, u32[]{:S(2)}, u32[]{:S(2)}) collective-permute-start(f32[9,72,128]{2,1,0:T(8,128)} %get-tuple-element.44), channel_id=1, source_target_pairs={{1,0},{2,1},{3,2},{4,3},{5,4},{6,5},{7,6},{9,8},{10,9},{11,10},{12... | collective-permute-start | bytes 995336 | tf_op jit(solution)/shard_map/ppermute | solution.py:488
  12.4 3.0 %collective-permute-start.6 = (f32[9,72,128]{2,1,0:T(8,128)}, f32[9,72,128]{2,1,0:T(8,128)S(1)}, u32[]{:S(2)}, u32[]{:S(2)}) collective-permute-start(f32[9,72,128]{2,1,0:T(8,128)} %get-tuple-element.45), channel_id=1, source_target_pairs={{0,1},{1,2},{2,3},{3,4},{4,5},{5,6},{6,7},{8,9},{9,10},{10,11},{11... | collective-permute-start | bytes 995336 | tf_op jit(solution)/shard_map/ppermute | solution.py:487
  15.5 4.8 %start.1.refs_5_.rows_ref = f32[48,64]{1,0:T(8,128)S(1)} custom-call(f32[48,64]{1,0:T(8,128)S(1)} %bitcast.6), custom_call_target="tpu_custom_call" | custom-call | tf_op jit(solution)/shard_map/start/pallas_call | solution.py:459
  20.3 0.1 pad_add_fusion.offs_ref
  20.3 0.0 collective-permute-done.1.refs_2_
  20.4 1.5 %observed.1 = (f32[16,64,128]{2,1,0:T(8,128)S(1)}, f32[9,64,128]{2,1,0:T(8,128)S(1)}, f32[9,64,128]{2,1,0:T(8,128)S(1)}, f32[2,1,1152]{2,1,0:T(1,128)S(1)}) custom-call(s32[4]{0:T(128)S(1)} %pad_add_fusion.offs_ref, f32[16,16,128]{2,1,0:T(8,128)S(1)} %get-tuple-element.48.refs_0_, f32[16,16,128]{2,1,0:T(8,128)S(1)} %collective-permute-done.refs_1_, ...), custom_call_target="tpu_custom_call" | custom-call | tf_op jit(solution)/shard_map/observed/pallas_call | solution.py:459
  21.9 3.2 %collective-permute-start.4 = (f32[9,64,128]{2,1,0:T(8,128)S(1)}, f32[9,64,128]{2,1,0:T(8,128)S(1)}, u32[]{:S(2)}, u32[]{:S(2)}) collective-permute-start(f32[9,64,128]{2,1,0:T(8,128)S(1)} %get-tuple-element.25), channel_id=1, source_target_pairs={{0,1},{1,2},{2,3},{3,4},{4,5},{5,6},{6,7},{8,9},{9,10},{10,11},{11... | collective-permute-start | bytes 884744 | tf_op jit(solution)/shard_map/ppermute | solution.py:487
  25.0 1.3 %collective-permute-start.5 = (f32[9,64,128]{2,1,0:T(8,128)S(1)}, f32[9,64,128]{2,1,0:T(8,128)S(1)}, u32[]{:S(2)}, u32[]{:S(2)}) collective-permute-start(f32[9,64,128]{2,1,0:T(8,128)S(1)} %get-tuple-element.27), channel_id=1, source_target_pairs={{1,0},{2,1},{3,2},{4,3},{5,4},{6,5},{7,6},{9,8},{10,9},{11,10},{12... | collective-permute-start | bytes 884744 | tf_op jit(solution)/shard_map/ppermute | solution.py:488
  26.4 1.2 %collective-permute-start.3 = (f32[1,1,1152]{2,1,0:T(1,128)S(1)}, f32[1,1,1152]{2,1,0:T(1,128)S(1)}, u32[]{:S(2)}, u32[]{:S(2)}) collective-permute-start(f32[1,1,1152]{2,1,0:T(1,128)S(1)} %constant_dynamic-slice_fusion.2), channel_id=1, source_target_pairs={{0,1},{1,0},{2,3},{3,2},{4,5},{5,4},{6,7},{7,6},{8,9},{9,8},{10,11... | collective-permute-start | bytes 13832 | tf_op jit(solution)/shard_map/ppermute | solution.py:476
  27.6 1.0 collective-permute-done.3
  28.5 0.7 broadcast_in_dim.22
  29.3 6.2 %all-to-all-start = ((f32[32,1,1152]{2,1,0:T(1,128)}), f32[32,1,1152]{2,1,0:T(1,128)S(1)}, u32[]{:S(2)}, u32[]{:S(2)}) async-start(f32[32,1,1152]{2,1,0:T(1,128)} %broadcast_in_dim.22), calls=%async_computation | async-start | bytes 294912 | tf_op jit(solution)/shard_map/all_to_all | solution.py:482
  35.5 0.0 collective-permute-done.7.refs_5_.refs_6_
  35.5 0.0 collective-permute-done.6.refs_3_.refs_4_
  35.5 0.0 copy-start.11
  35.5 0.0 collective-permute-done.4.refs_0_.refs_1_
  35.5 0.0 collective-permute-done.5.refs_2_.refs_3_
  35.5 0.7 strips0.1
  36.2 3.7 %collective-permute-start.9 = (f32[2,136,128]{2,1,0:T(8,128)S(1)}, f32[2,136,128]{2,1,0:T(8,128)S(1)}, u32[]{:S(2)}, u32[]{:S(2)}) collective-permute-start(f32[2,136,128]{2,1,0:T(8,128)S(1)} %strips0.1), channel_id=1, source_target_pairs={{8,0},{16,8},{24,16},{0,24},{9,1},{17,9},{25,17},{1,25},{10,2},{18... | collective-permute-start | bytes 417800 | tf_op jit(solution)/shard_map/ppermute | solution.py:495
  39.9 4.1 %all-to-all-done.parts_ref = f32[32,1,1152]{2,1,0:T(1,128)S(1)} async-done(((f32[32,1,1152]{2,1,0:T(1,128)}), f32[32,1,1152]{2,1,0:T(1,128)S(1)}, u32[]{:S(2)}, u32[]{:S(2)}) %all-to-all-start) | async-done | bytes 147488 | tf_op jit(solution)/shard_map/all_to_all | solution.py:482
  44.0 2.4 %modes.3 = (f32[48,64]{1,0:T(8,128)S(1)}, f32[64,64]{1,0:T(8,128)S(1)}) custom-call(f32[32,1,1152]{2,1,0:T(1,128)S(1)} %all-to-all-done.parts_ref, f32[48,64]{1,0:T(8,128)S(1)} %start.1.refs_5_.rows_ref), custom_call_target="tpu_custom_call" | custom-call | tf_op jit(solution)/shard_map/modes/pallas_call | solution.py:459
  46.4 2.1 %collective-permute-done.8.refs_7_ = f32[2,136,128]{2,1,0:T(8,128)S(1)} collective-permute-done((f32[2,136,128]{2,1,0:T(8,128)S(1)}, f32[2,136,128]{2,1,0:T(8,128)S(1)}, u32[]{:S(2)}, u32[]{:S(2)}) %collective-permute-start.8) | collective-permute-done | bytes 139296 | tf_op jit(solution)/shard_map/ppermute | solution.py:494
  48.5 0.6 copy-done.18
  49.2 1.0 copy-done.10
  50.1 1.0 copy-done.12
  51.1 1.0 copy-done.14
  52.1 1.0 copy-done.16
  53.0 0.9 copy-done.19
  53.9 4.3 %sweep0.1 = (f32[34,64,256]{2,1,0:T(8,128)S(1)}, f32[34,64,256]{2,1,0:T(8,128)S(1)}, f32[34,1,256]{2,1,0:T(1,128)S(1)}, f32[34,64,256]{2,1,0:T(8,128)S(1)}, f32[2,1,1152]{2,1,0:T(1,128)S(1)}) custom-call(f32[64,64]{1,0:T(8,128)S(1)} %get-tuple-element.24.refs_0_, f32[9,64,128]{2,1,0:T(8,128)S(1)} %copy-done.14, ...), custom_call_target="tpu_custom_call" | custom-call | tf_op jit(solution)/shard_map/sweep0/pallas_call | solution.py:459
  58.2 1.4 %copy-done = f32[34,64,256]{2,1,0:T(8,128)} copy-done((f32[34,64,256]{2,1,0:T(8,128)}, f32[34,64,256]{2,1,0:T(8,128)S(1)}, u32[]{:S(2)}) %copy-start) | copy-done | bytes 2228248
  59.6 1.4 %copy-done.3 = f32[34,64,256]{2,1,0:T(8,128)} copy-done((f32[34,64,256]{2,1,0:T(8,128)}, f32[34,64,256]{2,1,0:T(8,128)S(1)}, u32[]{:S(2)}) %copy-start.3) | copy-done | bytes 2228248
  61.0 1.2 %collective-permute-done.10 = f32[1,1,1152]{2,1,0:T(1,128)S(1)} collective-permute-done((f32[1,1,1152]{2,1,0:T(1,128)S(1)}, f32[1,1,1152]{2,1,0:T(1,128)S(1)}, u32[]{:S(2)}, u32[]{:S(2)}) %collective-permute-start.10) | collective-permute-done | bytes 4640 | tf_op jit(solution)/shard_map/ppermute | solution.py:476
  62.2 0.7 broadcast_in_dim.24
  63.0 3.0 %all-to-all-start.1 = ((f32[32,1,1152]{2,1,0:T(1,128)}), f32[32,1,1152]{2,1,0:T(1,128)S(1)}, u32[]{:S(2)}, u32[]{:S(2)}) async-start(f32[32,1,1152]{2,1,0:T(1,128)} %broadcast_in_dim.24), calls=%async_computation.1 | async-start | bytes 294912 | tf_op jit(solution)/shard_map/all_to_all | solution.py:482
  66.0 1.6 %copy-done.4 = f32[34,64,256]{2,1,0:T(8,128)S(1)} copy-done((f32[34,64,256]{2,1,0:T(8,128)S(1)}, f32[34,64,256]{2,1,0:T(8,128)}, u32[]{:S(2)}) %copy-start.4) | copy-done | bytes 2228248
  67.6 0.3 strips1.1
  67.9 3.7 %collective-permute-start.12 = (f32[2,64,128]{2,1,0:T(8,128)S(1)}, f32[2,64,128]{2,1,0:T(8,128)S(1)}, u32[]{:S(2)}, u32[]{:S(2)}) collective-permute-start(f32[2,64,128]{2,1,0:T(8,128)S(1)} %strips1.1), channel_id=1, source_target_pairs={{8,0},{16,8},{24,16},{0,24},{9,1},{17,9},{25,17},{1,25},{10,2},{18... | collective-permute-start | bytes 196616 | tf_op jit(solution)/shard_map/ppermute | solution.py:495
  71.6 2.8 %all-to-all-done.1.parts_ref = f32[32,1,1152]{2,1,0:T(1,128)S(1)} async-done(((f32[32,1,1152]{2,1,0:T(1,128)}), f32[32,1,1152]{2,1,0:T(1,128)S(1)}, u32[]{:S(2)}, u32[]{:S(2)}) %all-to-all-start.1) | async-done | bytes 147488 | tf_op jit(solution)/shard_map/all_to_all | solution.py:482
  74.4 2.6 %modes.4 = (f32[48,64]{1,0:T(8,128)S(1)}, f32[64,64]{1,0:T(8,128)S(1)}) custom-call(f32[32,1,1152]{2,1,0:T(1,128)S(1)} %all-to-all-done.1.parts_ref, f32[48,64]{1,0:T(8,128)S(1)} %get-tuple-element.31.rows_ref), custom_call_target="tpu_custom_call" | custom-call | tf_op jit(solution)/shard_map/modes/pallas_call | solution.py:459
  77.0 0.6 collective-permute-done.11.refs_2_
  77.6 1.6 %copy-done.1 = f32[34,64,256]{2,1,0:T(8,128)S(1)} copy-done((f32[34,64,256]{2,1,0:T(8,128)S(1)}, f32[34,64,256]{2,1,0:T(8,128)}, u32[]{:S(2)}) %copy-start.1) | copy-done | bytes 2228248
  79.3 1.6 %copy-done.5 = f32[34,64,256]{2,1,0:T(8,128)S(1)} copy-done((f32[34,64,256]{2,1,0:T(8,128)S(1)}, f32[34,64,256]{2,1,0:T(8,128)}, u32[]{:S(2)}) %copy-start.5) | copy-done | bytes 2228248
  80.9 3.3 %sweep1.1 = (f32[34,64,256]{2,1,0:T(8,128)S(1)}, f32[2,1,1152]{2,1,0:T(1,128)S(1)}) custom-call(f32[64,64]{1,0:T(8,128)S(1)} %get-tuple-element.32.refs_0_, f32[34,64,256]{2,1,0:T(8,128)S(1)} %copy-done.5, f32[2,64,128]{2,1,0:T(8,128)S(1)} %collective-permute-done.11.refs_2_, f32[2,64,128]{2,1,0:T(8,128)S(1)} %collective-permute-done.12.refs_3_, ...), custom_call_target="tpu_custom_call" | custom-call | tf_op jit(solution)/shard_map/sweep1/pallas_call | solution.py:459
  84.2 1.4 %copy-done.6 = f32[34,64,256]{2,1,0:T(8,128)} copy-done((f32[34,64,256]{2,1,0:T(8,128)}, f32[34,64,256]{2,1,0:T(8,128)S(1)}, u32[]{:S(2)}) %copy-start.6) | copy-done | bytes 2228248
  85.6 1.2 %collective-permute-done.13 = f32[1,1,1152]{2,1,0:T(1,128)S(1)} collective-permute-done((f32[1,1,1152]{2,1,0:T(1,128)S(1)}, f32[1,1,1152]{2,1,0:T(1,128)S(1)}, u32[]{:S(2)}, u32[]{:S(2)}) %collective-permute-start.13) | collective-permute-done | bytes 4640 | tf_op jit(solution)/shard_map/ppermute | solution.py:476
  86.8 0.7 broadcast_in_dim.26
  87.6 2.8 %all-to-all-start.2 = ((f32[32,1,1152]{2,1,0:T(1,128)}), f32[32,1,1152]{2,1,0:T(1,128)S(1)}, u32[]{:S(2)}, u32[]{:S(2)}) async-start(f32[32,1,1152]{2,1,0:T(1,128)} %broadcast_in_dim.26), calls=%async_computation.2 | async-start | bytes 294912 | tf_op jit(solution)/shard_map/all_to_all | solution.py:482
  90.4 1.6 %copy-done.7 = f32[34,64,256]{2,1,0:T(8,128)S(1)} copy-done((f32[34,64,256]{2,1,0:T(8,128)S(1)}, f32[34,64,256]{2,1,0:T(8,128)}, u32[]{:S(2)}) %copy-start.7) | copy-done | bytes 2228248
  92.0 0.2 strips2.1
  92.2 3.7 %collective-permute-start.15 = (f32[1,64,128]{2,1,0:T(8,128)S(1)}, f32[1,64,128]{2,1,0:T(8,128)S(1)}, u32[]{:S(2)}, u32[]{:S(2)}) collective-permute-start(f32[1,64,128]{2,1,0:T(8,128)S(1)} %strips2.1), channel_id=1, source_target_pairs={{8,0},{16,8},{24,16},{0,24},{9,1},{17,9},{25,17},{1,25},{10,2},{18... | collective-permute-start | bytes 98312 | tf_op jit(solution)/shard_map/ppermute | solution.py:495
  95.9 2.9 %all-to-all-done.2.parts_ref = f32[32,1,1152]{2,1,0:T(1,128)S(1)} async-done(((f32[32,1,1152]{2,1,0:T(1,128)}), f32[32,1,1152]{2,1,0:T(1,128)S(1)}, u32[]{:S(2)}, u32[]{:S(2)}) %all-to-all-start.2) | async-done | bytes 147488 | tf_op jit(solution)/shard_map/all_to_all | solution.py:482
  98.8 3.0 %modes.5 = (f32[48,64]{1,0:T(8,128)}, f32[64,64]{1,0:T(8,128)S(1)}) custom-call(f32[32,1,1152]{2,1,0:T(1,128)S(1)} %all-to-all-done.2.parts_ref, f32[48,64]{1,0:T(8,128)S(1)} %get-tuple-element.40.rows_ref), custom_call_target="tpu_custom_call" | custom-call | tf_op jit(solution)/shard_map/modes/pallas_call | solution.py:459
  101.8 1.6 %copy-done.2 = f32[34,64,256]{2,1,0:T(8,128)S(1)} copy-done((f32[34,64,256]{2,1,0:T(8,128)S(1)}, f32[34,64,256]{2,1,0:T(8,128)}, u32[]{:S(2)}) %copy-start.2) | copy-done | bytes 2228248
  103.4 1.6 %copy-done.8 = f32[34,64,256]{2,1,0:T(8,128)S(1)} copy-done((f32[34,64,256]{2,1,0:T(8,128)S(1)}, f32[34,64,256]{2,1,0:T(8,128)}, u32[]{:S(2)}) %copy-start.8) | copy-done | bytes 2228248
  105.1 2.9 %sweep2.1 = f32[64,16,128]{2,1,0:T(8,128)} custom-call(f32[64,64]{1,0:T(8,128)S(1)} %get-tuple-element.41.refs_0_, f32[34,64,256]{2,1,0:T(8,128)S(1)} %copy-done.8, f32[1,64,128]{2,1,0:T(8,128)S(1)} %collective-permute-done.14.refs_2_, f32[1,64,128]{2,1,0:T(8,128)S(1)} %collective-permute-done.15.refs_3_, f32[34,64,256]{2,1,0:T(8,128)S(1)} %get-tuple-element.34.refs_4_, ...), custom_call_target="tpu_custom_call" | custom-call | tf_op jit(solution)/shard_map/sweep2/pallas_call | solution.py:459
  (44 shorter events, 0.2 us)
Async XLA Ops:
  0.6 14.9 %copy-start.20 = (f32[64,48]{0,1:T(8,128)S(1)}, f32[64,48]{0,1:T(8,128)}, u32[]{:S(2)}) copy-start(f32[64,48]{0,1:T(8,128)} %param.9) | copy-start | bytes 36868
  1.8 18.5 %collective-permute-start.2 = (f32[16,16,128]{2,1,0:T(8,128)S(1)}, f32[16,16,128]{2,1,0:T(8,128)S(1)}, u32[]{:S(2)}, u32[]{:S(2)}) collective-permute-start(f32[16,16,128]{2,1,0:T(8,128)S(1)} %get-tuple-element.46), channel_id=1, source_target_pairs={{0,24},{8,16},{16,8},{24,0},{1,25},{9,17},{17,9},{25,1},{2,26},{10... | collective-permute-start | bytes 393224 | tf_op jit(solution)/shard_map/ppermute | solution.py:509
  7.0 13.4 %collective-permute-start = (f32[16,16,128]{2,1,0:T(8,128)S(1)}, f32[16,16,128]{2,1,0:T(8,128)S(1)}, u32[]{:S(2)}, u32[]{:S(2)}) collective-permute-start(f32[16,16,128]{2,1,0:T(8,128)S(1)} %get-tuple-element.47), channel_id=1, source_target_pairs={{0,8},{8,0},{16,24},{24,16},{1,9},{9,1},{17,25},{25,17},{2,10},{10... | collective-permute-start | bytes 393224 | tf_op jit(solution)/shard_map/ppermute | solution.py:509
  7.0 13.4 %collective-permute-start.1 = (f32[16,16,128]{2,1,0:T(8,128)S(1)}, f32[16,16,128]{2,1,0:T(8,128)S(1)}, u32[]{:S(2)}, u32[]{:S(2)}) collective-permute-start(f32[16,16,128]{2,1,0:T(8,128)S(1)} %get-tuple-element.49), channel_id=1, source_target_pairs={{0,16},{8,24},{16,0},{24,8},{1,17},{9,25},{17,1},{25,9},{2,18},{10... | collective-permute-start | bytes 393224 | tf_op jit(solution)/shard_map/ppermute | solution.py:509
  7.6 1.0 copy-start.17
  8.6 0.7 copy-start.21
  9.3 0.7 copy-start.22
  11.1 24.3 %collective-permute-start.7 = (f32[9,72,128]{2,1,0:T(8,128)}, f32[9,72,128]{2,1,0:T(8,128)S(1)}, u32[]{:S(2)}, u32[]{:S(2)}) collective-permute-start(f32[9,72,128]{2,1,0:T(8,128)} %get-tuple-element.44), channel_id=1, source_target_pairs={{1,0},{2,1},{3,2},{4,3},{5,4},{6,5},{7,6},{9,8},{10,9},{11,10},{12... | collective-permute-start | bytes 995336 | tf_op jit(solution)/shard_map/ppermute | solution.py:488
  12.4 23.1 %collective-permute-start.6 = (f32[9,72,128]{2,1,0:T(8,128)}, f32[9,72,128]{2,1,0:T(8,128)S(1)}, u32[]{:S(2)}, u32[]{:S(2)}) collective-permute-start(f32[9,72,128]{2,1,0:T(8,128)} %get-tuple-element.45), channel_id=1, source_target_pairs={{0,1},{1,2},{2,3},{3,4},{4,5},{5,6},{6,7},{8,9},{9,10},{10,11},{11... | collective-permute-start | bytes 995336 | tf_op jit(solution)/shard_map/ppermute | solution.py:487
  21.9 13.6 %collective-permute-start.4 = (f32[9,64,128]{2,1,0:T(8,128)S(1)}, f32[9,64,128]{2,1,0:T(8,128)S(1)}, u32[]{:S(2)}, u32[]{:S(2)}) collective-permute-start(f32[9,64,128]{2,1,0:T(8,128)S(1)} %get-tuple-element.25), channel_id=1, source_target_pairs={{0,1},{1,2},{2,3},{3,4},{4,5},{5,6},{6,7},{8,9},{9,10},{10,11},{11... | collective-permute-start | bytes 884744 | tf_op jit(solution)/shard_map/ppermute | solution.py:487
  25.0 10.5 %collective-permute-start.5 = (f32[9,64,128]{2,1,0:T(8,128)S(1)}, f32[9,64,128]{2,1,0:T(8,128)S(1)}, u32[]{:S(2)}, u32[]{:S(2)}) collective-permute-start(f32[9,64,128]{2,1,0:T(8,128)S(1)} %get-tuple-element.27), channel_id=1, source_target_pairs={{1,0},{2,1},{3,2},{4,3},{5,4},{6,5},{7,6},{9,8},{10,9},{11,10},{12... | collective-permute-start | bytes 884744 | tf_op jit(solution)/shard_map/ppermute | solution.py:488
  26.4 2.2 %collective-permute-start.3 = (f32[1,1,1152]{2,1,0:T(1,128)S(1)}, f32[1,1,1152]{2,1,0:T(1,128)S(1)}, u32[]{:S(2)}, u32[]{:S(2)}) collective-permute-start(f32[1,1,1152]{2,1,0:T(1,128)S(1)} %constant_dynamic-slice_fusion.2), channel_id=1, source_target_pairs={{0,1},{1,0},{2,3},{3,2},{4,5},{5,4},{6,7},{7,6},{8,9},{9,8},{10,11... | collective-permute-start | bytes 13832 | tf_op jit(solution)/shard_map/ppermute | solution.py:476
  29.3 14.7 %all-to-all-start = ((f32[32,1,1152]{2,1,0:T(1,128)}), f32[32,1,1152]{2,1,0:T(1,128)S(1)}, u32[]{:S(2)}, u32[]{:S(2)}) async-start(f32[32,1,1152]{2,1,0:T(1,128)} %broadcast_in_dim.22), calls=%async_computation | async-start | bytes 294912 | tf_op jit(solution)/shard_map/all_to_all | solution.py:482
  35.5 13.0 %copy-start.9 = (f32[9,72,128]{2,1,0:T(8,128)}, f32[9,72,128]{2,1,0:T(8,128)S(1)}, u32[]{:S(2)}) copy-start(f32[9,72,128]{2,1,0:T(8,128)S(1)} %collective-permute-done.7.refs_5_.refs_6_) | copy-start | bytes 995332
  35.5 13.0 %copy-start.11 = (f32[9,72,128]{2,1,0:T(8,128)}, f32[9,72,128]{2,1,0:T(8,128)S(1)}, u32[]{:S(2)}) copy-start(f32[9,72,128]{2,1,0:T(8,128)S(1)} %collective-permute-done.6.refs_3_.refs_4_) | copy-start | bytes 995332
  35.5 13.0 %copy-start.13 = (f32[9,64,128]{2,1,0:T(8,128)}, f32[9,64,128]{2,1,0:T(8,128)S(1)}, u32[]{:S(2)}) copy-start(f32[9,64,128]{2,1,0:T(8,128)S(1)} %collective-permute-done.4.refs_0_.refs_1_) | copy-start | bytes 884740
  35.5 13.0 %copy-start.15 = (f32[9,64,128]{2,1,0:T(8,128)}, f32[9,64,128]{2,1,0:T(8,128)S(1)}, u32[]{:S(2)}) copy-start(f32[9,64,128]{2,1,0:T(8,128)S(1)} %collective-permute-done.5.refs_2_.refs_3_) | copy-start | bytes 884740
  36.2 10.2 %collective-permute-start.9 = (f32[2,136,128]{2,1,0:T(8,128)S(1)}, f32[2,136,128]{2,1,0:T(8,128)S(1)}, u32[]{:S(2)}, u32[]{:S(2)}) collective-permute-start(f32[2,136,128]{2,1,0:T(8,128)S(1)} %strips0.1), channel_id=1, source_target_pairs={{8,0},{16,8},{24,16},{0,24},{9,1},{17,9},{25,17},{1,25},{10,2},{18... | collective-permute-start | bytes 417800 | tf_op jit(solution)/shard_map/ppermute | solution.py:495
  39.9 8.6 %collective-permute-start.8 = (f32[2,136,128]{2,1,0:T(8,128)S(1)}, f32[2,136,128]{2,1,0:T(8,128)S(1)}, u32[]{:S(2)}, u32[]{:S(2)}) collective-permute-start(f32[2,136,128]{2,1,0:T(8,128)S(1)} %strips0.1), channel_id=1, source_target_pairs={{0,8},{8,16},{16,24},{24,0},{1,9},{9,17},{17,25},{25,1},{2,10},{10... | collective-permute-start | bytes 417800 | tf_op jit(solution)/shard_map/ppermute | solution.py:494
  48.5 0.7 copy-start.18
  49.2 1.0 copy-start.10
  50.1 1.0 copy-start.12
  51.1 1.0 copy-start.14
  52.1 1.0 copy-start.16
  53.0 0.9 copy-start.19
  58.2 1.4 %copy-start = (f32[34,64,256]{2,1,0:T(8,128)}, f32[34,64,256]{2,1,0:T(8,128)S(1)}, u32[]{:S(2)}) copy-start(f32[34,64,256]{2,1,0:T(8,128)S(1)} %get-tuple-element.35.refs_5_) | copy-start | bytes 6684676
  59.6 1.4 %copy-start.3 = (f32[34,64,256]{2,1,0:T(8,128)}, f32[34,64,256]{2,1,0:T(8,128)S(1)}, u32[]{:S(2)}) copy-start(f32[34,64,256]{2,1,0:T(8,128)S(1)} %get-tuple-element.33.f_ref.refs_1_) | copy-start | bytes 6684676
  61.0 1.2 %collective-permute-start.10 = (f32[1,1,1152]{2,1,0:T(1,128)S(1)}, f32[1,1,1152]{2,1,0:T(1,128)S(1)}, u32[]{:S(2)}, u32[]{:S(2)}) collective-permute-start(f32[1,1,1152]{2,1,0:T(1,128)S(1)} %constant_dynamic-slice_fusion.1), channel_id=1, source_target_pairs={{0,1},{1,0},{2,3},{3,2},{4,5},{5,4},{6,7},{7,6},{8,9},{9,8},{10,11... | collective-permute-start | bytes 13832 | tf_op jit(solution)/shard_map/ppermute | solution.py:476
  63.0 11.4 %all-to-all-start.1 = ((f32[32,1,1152]{2,1,0:T(1,128)}), f32[32,1,1152]{2,1,0:T(1,128)S(1)}, u32[]{:S(2)}, u32[]{:S(2)}) async-start(f32[32,1,1152]{2,1,0:T(1,128)} %broadcast_in_dim.24), calls=%async_computation.1 | async-start | bytes 294912 | tf_op jit(solution)/shard_map/all_to_all | solution.py:482
  66.0 1.6 %copy-start.4 = (f32[34,64,256]{2,1,0:T(8,128)S(1)}, f32[34,64,256]{2,1,0:T(8,128)}, u32[]{:S(2)}) copy-start(f32[34,64,256]{2,1,0:T(8,128)} %copy-done.3) | copy-start | bytes 6684676
  67.9 9.1 %collective-permute-start.12 = (f32[2,64,128]{2,1,0:T(8,128)S(1)}, f32[2,64,128]{2,1,0:T(8,128)S(1)}, u32[]{:S(2)}, u32[]{:S(2)}) collective-permute-start(f32[2,64,128]{2,1,0:T(8,128)S(1)} %strips1.1), channel_id=1, source_target_pairs={{8,0},{16,8},{24,16},{0,24},{9,1},{17,9},{25,17},{1,25},{10,2},{18... | collective-permute-start | bytes 196616 | tf_op jit(solution)/shard_map/ppermute | solution.py:495
  71.6 6.1 %collective-permute-start.11 = (f32[2,64,128]{2,1,0:T(8,128)S(1)}, f32[2,64,128]{2,1,0:T(8,128)S(1)}, u32[]{:S(2)}, u32[]{:S(2)}) collective-permute-start(f32[2,64,128]{2,1,0:T(8,128)S(1)} %strips1.1), channel_id=1, source_target_pairs={{0,8},{8,16},{16,24},{24,0},{1,9},{9,17},{17,25},{25,1},{2,10},{10... | collective-permute-start | bytes 196616 | tf_op jit(solution)/shard_map/ppermute | solution.py:494
  77.6 1.6 %copy-start.1 = (f32[34,64,256]{2,1,0:T(8,128)S(1)}, f32[34,64,256]{2,1,0:T(8,128)}, u32[]{:S(2)}) copy-start(f32[34,64,256]{2,1,0:T(8,128)} %copy-done) | copy-start | bytes 6684676
  79.3 1.6 %copy-start.5 = (f32[34,64,256]{2,1,0:T(8,128)S(1)}, f32[34,64,256]{2,1,0:T(8,128)}, u32[]{:S(2)}) copy-start(f32[34,64,256]{2,1,0:T(8,128)} %copy-done.3) | copy-start | bytes 6684676
  84.2 1.4 %copy-start.6 = (f32[34,64,256]{2,1,0:T(8,128)}, f32[34,64,256]{2,1,0:T(8,128)S(1)}, u32[]{:S(2)}) copy-start(f32[34,64,256]{2,1,0:T(8,128)S(1)} %get-tuple-element.42.f_ref.refs_1_) | copy-start | bytes 6684676
  85.6 1.2 %collective-permute-start.13 = (f32[1,1,1152]{2,1,0:T(1,128)S(1)}, f32[1,1,1152]{2,1,0:T(1,128)S(1)}, u32[]{:S(2)}, u32[]{:S(2)}) collective-permute-start(f32[1,1,1152]{2,1,0:T(1,128)S(1)} %constant_dynamic-slice_fusion), channel_id=1, source_target_pairs={{0,1},{1,0},{2,3},{3,2},{4,5},{5,4},{6,7},{7,6},{8,9},{9,8},{10,11... | collective-permute-start | bytes 13832 | tf_op jit(solution)/shard_map/ppermute | solution.py:476
  87.6 11.2 %all-to-all-start.2 = ((f32[32,1,1152]{2,1,0:T(1,128)}), f32[32,1,1152]{2,1,0:T(1,128)S(1)}, u32[]{:S(2)}, u32[]{:S(2)}) async-start(f32[32,1,1152]{2,1,0:T(1,128)} %broadcast_in_dim.26), calls=%async_computation.2 | async-start | bytes 294912 | tf_op jit(solution)/shard_map/all_to_all | solution.py:482
  90.4 1.6 %copy-start.7 = (f32[34,64,256]{2,1,0:T(8,128)S(1)}, f32[34,64,256]{2,1,0:T(8,128)}, u32[]{:S(2)}) copy-start(f32[34,64,256]{2,1,0:T(8,128)} %copy-done.6) | copy-start | bytes 6684676
  92.2 9.6 %collective-permute-start.15 = (f32[1,64,128]{2,1,0:T(8,128)S(1)}, f32[1,64,128]{2,1,0:T(8,128)S(1)}, u32[]{:S(2)}, u32[]{:S(2)}) collective-permute-start(f32[1,64,128]{2,1,0:T(8,128)S(1)} %strips2.1), channel_id=1, source_target_pairs={{8,0},{16,8},{24,16},{0,24},{9,1},{17,9},{25,17},{1,25},{10,2},{18... | collective-permute-start | bytes 98312 | tf_op jit(solution)/shard_map/ppermute | solution.py:495
  95.9 5.9 %collective-permute-start.14 = (f32[1,64,128]{2,1,0:T(8,128)S(1)}, f32[1,64,128]{2,1,0:T(8,128)S(1)}, u32[]{:S(2)}, u32[]{:S(2)}) collective-permute-start(f32[1,64,128]{2,1,0:T(8,128)S(1)} %strips2.1), channel_id=1, source_target_pairs={{0,8},{8,16},{16,24},{24,0},{1,9},{9,17},{17,25},{25,1},{2,10},{10... | collective-permute-start | bytes 98312 | tf_op jit(solution)/shard_map/ppermute | solution.py:494
  101.8 1.6 %copy-start.2 = (f32[34,64,256]{2,1,0:T(8,128)S(1)}, f32[34,64,256]{2,1,0:T(8,128)}, u32[]{:S(2)}) copy-start(f32[34,64,256]{2,1,0:T(8,128)} %copy-done) | copy-start | bytes 6684676
  103.4 1.6 %copy-start.8 = (f32[34,64,256]{2,1,0:T(8,128)S(1)}, f32[34,64,256]{2,1,0:T(8,128)}, u32[]{:S(2)}) copy-start(f32[34,64,256]{2,1,0:T(8,128)} %copy-done.6) | copy-start | bytes 6684676

commit v4 on v3

--- a/solution.py
+++ b/solution.py
@@ -296,61 +296,54 @@
     return south[e - HALO - rows]
 
 
-def strip_rows(sweep, total):
-    return range(sweep * PASSES + 1, total - sweep * PASSES - 1)
-
-
-def strip_place(sweep, e, cols):
-    per = cols // (2 * PASSES)
-    at = e - sweep * PASSES - 1
-    return at // per, at % per * 2 * PASSES
-
-
-def write_strips(sweep, total, value_of, strip_ref, at):
-    _, _, cols = strip_ref.shape
-    tiles = {}
-    for e in strip_rows(sweep, total):
-        value = value_of(e)
-        tile, place = strip_place(sweep, e, cols)
-        lane = grid_of(value.shape, 1)
-        here = (lane >= place) & (lane < place + 2 * PASSES)
-        moved = pltpu.roll(value, place + PASSES, 1)
-        tiles[tile] = jnp.where(here, moved, tiles.get(tile, 0.0))
-    for tile, value in tiles.items():
-        strip_ref[tile, at, :] = value
-
-
-def read_strips(sweep, total, west_ref, east_ref, at):
+def strip_places(rows, cols):
+    reach = {}
+    for e in range(rows + 2 * HALO):
+        reach[e] = HALO - max(0, HALO - e, e - HALO - rows + 1)
+    places, tile, at = {}, 0, 0
+    for e in sorted(reach, key=lambda e: (-reach[e], e)):
+        if not reach[e]:
+            continue
+        if at + reach[e] > cols:
+            tile, at = tile + 1, 0
+        places[e] = (tile, at, reach[e])
+        at += reach[e]
+    return places, tile + 1
+
+
+def strip_kernel(*refs):
+    seen, stat = refs[0:3], refs[3:6]
+    east_ref, west_ref = refs[6:]
+    rows, days, cols = seen[1].shape
+    places, tiles = strip_places(rows, cols)
+    for source, at in ((seen, slice(0, days)), (stat, slice(days, None))):
+        for tile in range(tiles):
+            east = west = 0.0
+            for e, (where, place, reach) in places.items():
+                if where != tile:
+                    continue
+                value = row_source(source, rows, e)
+                lane = grid_of(value.shape, 1)
+                here = (lane >= place) & (lane < place + reach)
+                to_west = pltpu.roll(value, place, 1) if place else value
+                west = jnp.where(here, to_west, west)
+                east = jnp.where(here, pltpu.roll(value, place + reach, 1), east)
+            east_ref[tile, at, :] = east
+            west_ref[tile, at, :] = west
+
+
+def strip_side(rows, west_ref, east_ref, at, e):
     _, _, cols = west_ref.shape
-    merged = []
-    for tile in range(west_ref.shape[0]):
-        west, east = west_ref[tile, at, :], east_ref[tile, at, :]
-        lane = grid_of(west.shape, 1)
-        merged.append(jnp.where(lane % (2 * PASSES) < PASSES, west, east))
-
-    def side(e):
-        lane = grid_of(merged[0].shape, 1)
-        if e not in strip_rows(sweep, total):
-            return jnp.zeros(merged[0].shape, F32)
-        tile, place = strip_place(sweep, e, cols)
-        moved = pltpu.roll(merged[tile], cols - place - PASSES, 1)
-        return jnp.where((lane < PASSES) | (lane >= cols - PASSES), moved, 0.0)
-
-    return side
-
-
-def first_strip_kernel(*refs):
-    seen, stat, strip_ref = refs[0:3], refs[3:6], refs[6]
-    rows, days, _ = seen[1].shape
-    total = rows + 2 * HALO
-    write_strips(0, total, lambda e: row_source(seen, rows, e), strip_ref, slice(0, days))
-    write_strips(0, total, lambda e: row_source(stat, rows, e), strip_ref, slice(days, None))
-
-
-def strip_kernel(sweep, f_ref, strip_ref):
-    cols = strip_ref.shape[2]
-    total = f_ref.shape[0]
-    write_strips(sweep, total, lambda e: f_ref[e, :, :cols], strip_ref, slice(None))
+    places, _ = strip_places(rows, cols)
+    if e not in places:
+        return jnp.zeros(west_ref[0, at, :].shape, F32)
+    tile, place, reach = places[e]
+    west, east = west_ref[tile, at, :], east_ref[tile, at, :]
+    lane = grid_of(west.shape, 1)
+    east = pltpu.roll(east, cols - place, 1) if place else east
+    west = pltpu.roll(west, cols - reach - place, 1)
+    value = jnp.where(lane >= cols - reach, west, 0.0)
+    return jnp.where(lane < reach, east, value)
 
 
 def project_rows(last, row_of, out_ref, seen_ref, gap_ref, low, high):
@@ -402,10 +395,6 @@
     return now
 
 
-def joined(f_ref, side, cols):
-    return lambda e: jnp.concatenate([f_ref[e, :, :cols], side(e)], axis=1)
-
-
 def first_kernel(*refs):
     last_ref = refs[0]
     seen, stat = refs[1:4], refs[4:7]
@@ -413,12 +402,11 @@
     seen_ref, gap_ref, diff_ref, out_ref, packed_ref, a_ref = refs[9:]
     rows, days, cols = seen[1].shape
     total = rows + 2 * HALO
-    seen_side = read_strips(0, total, west_ref, east_ref, slice(0, days))
-    stat_side = read_strips(0, total, west_ref, east_ref, slice(days, None))
+    side_of = lambda at, e: strip_side(rows, west_ref, east_ref, at, e)
     for e in range(total):
         seen_ref[e, :, :cols] = row_source(seen, rows, e)
-        seen_ref[e, :, cols:] = seen_side(e)
-        main, side = row_source(stat, rows, e), stat_side(e)
+        seen_ref[e, :, cols:] = side_of(slice(0, days), e)
+        main, side = row_source(stat, rows, e), side_of(slice(days, None), e)
         gap_ref[e, :, :cols] = main[:days]
         gap_ref[e, :, cols:] = side[:days]
         diff_ref[e, :, :cols] = main[days : days + 1]
@@ -430,25 +418,18 @@
     pack_symmetric(packed_ref, cov)
 
 
-def next_kernel(sweep, *refs):
-    last_ref, f_ref, west_ref, east_ref, seen_ref, gap_ref, diff_ref = refs[:7]
-    out_ref, packed_ref, a_ref = refs[7:]
-    total, cols = seen_ref.shape[0], west_ref.shape[2]
-    side = read_strips(sweep, total, west_ref, east_ref, slice(None))
-    row_of = joined(f_ref, side, cols)
+def next_kernel(sweep, last_ref, f_ref, seen_ref, gap_ref, diff_ref, out_ref, packed_ref, a_ref):
+    row_of = lambda e: f_ref[e]
     now = sweep_body(sweep, last_ref[...], row_of, a_ref, out_ref, seen_ref, gap_ref, diff_ref)
     assert now is out_ref
-    cov = covariance_of(lambda r: out_ref[HALO + r, :, :cols], total - 2 * HALO)
-    pack_symmetric(packed_ref, cov)
-
-
-def end_kernel(sweep, *refs):
-    last_ref, f_ref, west_ref, east_ref, seen_ref, gap_ref, diff_ref = refs[:7]
-    out_ref, a_ref, b_ref = refs[7:]
+    rows, cols = out_ref.shape[0] - 2 * HALO, out_ref.shape[2] // 2
+    pack_symmetric(packed_ref, covariance_of(lambda r: out_ref[HALO + r, :, :cols], rows))
+
+
+def end_kernel(sweep, last_ref, f_ref, seen_ref, gap_ref, diff_ref, out_ref, a_ref, b_ref):
+    row_of = lambda e: f_ref[e]
+    now = sweep_body(sweep, last_ref[...], row_of, a_ref, b_ref, seen_ref, gap_ref, diff_ref)
     days, rows, cols = out_ref.shape
-    side = read_strips(sweep, seen_ref.shape[0], west_ref, east_ref, slice(None))
-    row_of = joined(f_ref, side, cols)
-    now = sweep_body(sweep, last_ref[...], row_of, a_ref, b_ref, seen_ref, gap_ref, diff_ref)
     flat = out_ref.reshape(days * rows, cols)
     for r in range(rows):
         flat[pl.ds(r, days, stride=rows), :] = now[HALO + r, :, :cols]
@@ -489,10 +470,10 @@
     return [north, cells, south]
 
 
-def beside(strip):
+def beside(east, west):
     count = lax.axis_size("wide")
-    from_west = lax.ppermute(strip, "wide", [(i, (i + 1) % count) for i in range(count)])
-    from_east = lax.ppermute(strip, "wide", [((i + 1) % count, i) for i in range(count)])
+    from_west = lax.ppermute(east, "wide", [(i, (i + 1) % count) for i in range(count)])
+    from_east = lax.ppermute(west, "wide", [((i + 1) % count, i) for i in range(count)])
     return [from_west, from_east]
 
 
@@ -526,17 +507,11 @@
     )
     seens = edges(head, seen, tail)
     total = rows + 2 * HALO
-    strip_shape = lambda sweep, depth: (
-        pl.cdiv(len(strip_rows(sweep, total)), cols // (2 * PASSES)),
-        depth,
-        cols,
-    )
+    strip = (strip_places(rows, cols)[1], 2 * days + EXTRA, cols)
     wide_map, wide_row = (total, days, 2 * cols), (total, 1, 2 * cols)
     parts = trade(pair_sums(packed))
-    (strip,) = call(
-        first_strip_kernel, "strips0", seens + stats, [strip_shape(0, 2 * days + EXTRA)]
-    )
-    sides = beside(strip)
+    east, west = call(strip_kernel, "strips", seens + stats, [strip, strip])
+    sides = beside(east, west)
     for sweep in range(OUTER):
         basis, last = call(
             modes_kernel,
@@ -557,7 +532,7 @@
             filled, packed = call(
                 functools.partial(next_kernel, sweep),
                 f"sweep{sweep}",
-                [last, filled] + sides + [seen_w, gap_w, diff_w],
+                [last, filled, seen_w, gap_w, diff_w],
                 [wide_map, (2, 1, width)],
                 [wide_map],
             )
@@ -565,20 +540,12 @@
             (out,) = call(
                 functools.partial(end_kernel, sweep),
                 f"sweep{sweep}",
-                [last, filled] + sides + [seen_w, gap_w, diff_w],
+                [last, filled, seen_w, gap_w, diff_w],
                 [(days, rows, cols)],
                 [wide_map, wide_map],
             )
             return (out, basis.T)
-        copies, held = lax.optimization_barrier((pair_sums(packed), filled))
-        parts = trade(copies)
-        (strip,) = call(
-            functools.partial(strip_kernel, sweep + 1),
-            f"strips{sweep + 1}",
-            [held],
-            [strip_shape(sweep + 1, days)],
-        )
-        sides = beside(strip)
+        parts = trade(pair_sums(packed))
 
 
 def solution(mesh):

time: 107 us -> 88.8 us (0.83)
  blocking collectives: 0 us -> 22.5 us
  local copies, waits for them, and re-layouts: 26.1 us -> 5.29 us
  starting transfers between devices: 38.7 us -> 26.2 us
  waiting for transfers between devices: 15.8 us -> 7.66 us
  Pallas kernels: 26.2 us -> 27.3 us
    all_to_all x0 -> x2, blocking collectives: none -> 22.5 us  [trade(): return lax.all_to_all(copies, ('wide', 'band'), 0, 0, tiled=True)]
    unnamed x46 -> x8, local copies, waits for them, and re-layouts: 21.8 us -> 2.44 us
    ppermute x6 -> x2, starting transfers between devices: 11 us -> 3.88 us  [the longest x1 2.05 us: beside(): lax.ppermute(west, 'wide', [((i + 1) % count, i) for i in range(count)])]
    all_to_all x3 -> x1, waiting for transfers between devices: 9.77 us -> 3.36 us  [trade(): return lax.all_to_all(copies, ('wide', 'band'), 0, 0, tiled=True)]
    all_to_all x3 -> x1, starting transfers between devices: 12 us -> 6.18 us  [trade(): return lax.all_to_all(copies, ('wide', 'band'), 0, 0, tiled=True)]
    ppermute x6 -> x2, waiting for transfers between devices: 2.74 us -> 1.25 us  [the longest x1 1.25 us: beside(): lax.ppermute(west, 'wide', [((i + 1) % count, i) for i in range(count)])]
    broadcast_in_dim x3, local copies, waits for them, and re-layouts: 2.21 us -> 0.9 us  [pair_sums(): return jnp.broadcast_to(mine + got, (everyone, 1, width))]
    pallas_call x12 -> x10, Pallas kernels: 26.2 us -> 27.3 us  [call(): pl.pallas_call(kernel, name=name, out_shape=[jax.ShapeDtypeStruct(s, F32)...]
  transfers between devices with their start and end apart: 19 -> 13, of which waited for: 8 -> 5; matrix products, arithmetic and copies ran while one was open for 2% -> 2% of each run, Pallas kernels for 15% -> 11%
where the time goes in v4:
time: 88.8 us; the launch traced here: 90 us
  Pallas kernels  27.3 us (31%)
  starting transfers between devices  26.2 us (30%)
  blocking collectives  22.5 us (25%)
  waiting for transfers between devices  7.66 us (9%)
  local copies, waits for them, and re-layouts  5.29 us (6%)
  between operations  0.89 us (1%)
    pallas_call x10, Pallas kernels, call(): pl.pallas_call(kernel, name=name, out_shape=[jax.ShapeDtypeStruct(s, F32)...  27.3 us
    all_to_all x2, blocking collectives, trade(): return lax.all_to_all(copies, ('wide', 'band'), 0, 0, tiled=True)  22.5 us
    ppermute x2, starting transfers between devices, edges(): north = lax.ppermute(tail, 'band', [(i, i + 1) for i in range(count - 1)])  6.21 us
    all_to_all x1, starting transfers between devices, trade(): return lax.all_to_all(copies, ('wide', 'band'), 0, 0, tiled=True)  6.18 us
    ppermute x3, starting transfers between devices, shards(): piece = lax.ppermute(piece, 'wide', [(i, to(i)) for i in range(count)])  5.78 us
    all_to_all x1, waiting for transfers between devices, trade(): return lax.all_to_all(copies, ('wide', 'band'), 0, 0, tiled=True)  3.36 us
    ppermute x3, waiting for transfers between devices, pair_sums(): got = lax.ppermute(other, 'band', [(i, i ^ 1) for i in range(count)])  3.03 us
    ppermute x2, starting transfers between devices, edges(): south = lax.ppermute(head, 'band', [(i + 1, i) for i in range(count - 1)])  2.57 us
  transfers between devices with their start and end apart: 13, of which 5 were waited for; matrix products, arithmetic and copies ran while one was open for 2% of the time, Pallas kernels for 11%

profile of v4, /device:TPU:0, one launch (start us, length us, event | category | flops | bytes accessed | tf_op | source)
XLA Modules:
  0.0 90.0 jit_solution(1298080206482881890)
XLA Ops:
  0.6 0.0 copy-start.1
  0.7 1.1 %constant_dynamic-slice_fusion.3 = (f32[16,16,128]{2,1,0:T(8,128)S(1)}, f32[16,16,128]{2,1,0:T(8,128)S(1)}, f32[16,16,128]{2,1,0:T(8,128)S(1)}, f32[16,16,128]{2,1,0:T(8,128)S(1)}) fusion(f32[16,16,512]{2,1,0:T(8,128)} %param.5, s32[]{:T(128)S(6)} %select_n.25, s32[]{:T(128)S(6)} %select_n.23, s32[]{:T(128)S(6)} %select_n.22, s32[]{:T(128)S(6)} %select_n.24), kind=kLoop, calls=%fused_computation.6 | loop fusion | bytes 1048592 | tf_op jit(solution)/shard_map/dynamic_slice | solution.py:488
  1.8 5.1 %collective-permute-start.2 = (f32[16,16,128]{2,1,0:T(8,128)S(1)}, f32[16,16,128]{2,1,0:T(8,128)S(1)}, u32[]{:S(2)}, u32[]{:S(2)}) collective-permute-start(f32[16,16,128]{2,1,0:T(8,128)S(1)} %get-tuple-element.42), channel_id=1, source_target_pairs={{0,24},{8,16},{16,8},{24,0},{1,25},{9,17},{17,9},{25,1},{2,26},{10... | collective-permute-start | bytes 393224 | tf_op jit(solution)/shard_map/ppermute | solution.py:490
  7.0 0.0 collective-permute-start
  7.0 0.6 collective-permute-start.1
  7.6 0.0 copy-start
  7.6 1.0 %copy-done = s32[64,16,128]{2,1,0:T(8,128)S(1)} copy-done((s32[64,16,128]{2,1,0:T(8,128)S(1)}, s32[64,16,128]{2,1,0:T(8,128)}, u32[]{:S(2)}) %copy-start) | copy-done | bytes 524312
  8.6 0.0 copy-start.2
  8.6 0.7 copy-done.2
  9.3 0.0 copy-start.3
  9.3 0.7 copy-done.3
  10.0 0.2 static.1.refs_4_.refs_5_
  10.2 0.8 fusion
  11.0 1.3 %collective-permute-start.7 = (f32[9,72,128]{2,1,0:T(8,128)}, f32[9,72,128]{2,1,0:T(8,128)S(1)}, u32[]{:S(2)}, u32[]{:S(2)}) collective-permute-start(f32[9,72,128]{2,1,0:T(8,128)} %get-tuple-element.40), channel_id=1, source_target_pairs={{1,0},{2,1},{3,2},{4,3},{5,4},{6,5},{7,6},{9,8},{10,9},{11,10},{12... | collective-permute-start | bytes 995336 | tf_op jit(solution)/shard_map/ppermute | solution.py:469
  12.3 3.1 %collective-permute-start.6 = (f32[9,72,128]{2,1,0:T(8,128)S(1)}, f32[9,72,128]{2,1,0:T(8,128)S(1)}, u32[]{:S(2)}, u32[]{:S(2)}) collective-permute-start(f32[9,72,128]{2,1,0:T(8,128)S(1)} %get-tuple-element.41), channel_id=1, source_target_pairs={{0,1},{1,2},{2,3},{3,4},{4,5},{5,6},{6,7},{8,9},{9,10},{10,11},{11... | collective-permute-start | bytes 995336 | tf_op jit(solution)/shard_map/ppermute | solution.py:468
  15.4 0.0 copy-done.1
  15.4 4.8 %start.1.refs_5_.rows_ref = f32[48,64]{1,0:T(8,128)S(1)} custom-call(f32[48,64]{1,0:T(8,128)S(1)} %bitcast.6), custom_call_target="tpu_custom_call" | custom-call | tf_op jit(solution)/shard_map/start/pallas_call | solution.py:440
  20.1 0.1 pad_add_fusion.offs_ref
  20.2 0.0 collective-permute-done.2.refs_3_
  20.2 0.0 collective-permute-done.refs_1_
  20.2 0.0 collective-permute-done.1.refs_2_
  20.2 1.5 %observed.1 = (f32[16,64,128]{2,1,0:T(8,128)S(1)}, f32[9,64,128]{2,1,0:T(8,128)S(1)}, f32[9,64,128]{2,1,0:T(8,128)S(1)}, f32[2,1,1152]{2,1,0:T(1,128)S(1)}) custom-call(s32[4]{0:T(128)S(1)} %pad_add_fusion.offs_ref, f32[16,16,128]{2,1,0:T(8,128)S(1)} %get-tuple-element.44.refs_0_, f32[16,16,128]{2,1,0:T(8,128)S(1)} %collective-permute-done.refs_1_, ...), custom_call_target="tpu_custom_call" | custom-call | tf_op jit(solution)/shard_map/observed/pallas_call | solution.py:440
  21.8 3.2 %collective-permute-start.4 = (f32[9,64,128]{2,1,0:T(8,128)S(1)}, f32[9,64,128]{2,1,0:T(8,128)S(1)}, u32[]{:S(2)}, u32[]{:S(2)}) collective-permute-start(f32[9,64,128]{2,1,0:T(8,128)S(1)} %get-tuple-element.23), channel_id=1, source_target_pairs={{0,1},{1,2},{2,3},{3,4},{4,5},{5,6},{6,7},{8,9},{9,10},{10,11},{11... | collective-permute-start | bytes 884744 | tf_op jit(solution)/shard_map/ppermute | solution.py:468
  24.9 1.3 %collective-permute-start.5 = (f32[9,64,128]{2,1,0:T(8,128)S(1)}, f32[9,64,128]{2,1,0:T(8,128)S(1)}, u32[]{:S(2)}, u32[]{:S(2)}) collective-permute-start(f32[9,64,128]{2,1,0:T(8,128)S(1)} %get-tuple-element.25), channel_id=1, source_target_pairs={{1,0},{2,1},{3,2},{4,3},{5,4},{6,5},{7,6},{9,8},{10,9},{11,10},{12... | collective-permute-start | bytes 884744 | tf_op jit(solution)/shard_map/ppermute | solution.py:469
  26.2 1.2 %collective-permute-start.3 = (f32[1,1,1152]{2,1,0:T(1,128)S(1)}, f32[1,1,1152]{2,1,0:T(1,128)S(1)}, u32[]{:S(2)}, u32[]{:S(2)}) collective-permute-start(f32[1,1,1152]{2,1,0:T(1,128)S(1)} %constant_dynamic-slice_fusion.2), channel_id=1, source_target_pairs={{0,1},{1,0},{2,3},{3,2},{4,5},{5,4},{6,7},{7,6},{8,9},{9,8},{10,11... | collective-permute-start | bytes 13832 | tf_op jit(solution)/shard_map/ppermute | solution.py:457
  27.4 1.0 %collective-permute-done.3 = f32[1,1,1152]{2,1,0:T(1,128)S(1)} collective-permute-done((f32[1,1,1152]{2,1,0:T(1,128)S(1)}, f32[1,1,1152]{2,1,0:T(1,128)S(1)}, u32[]{:S(2)}, u32[]{:S(2)}) %collective-permute-start.3) | collective-permute-done | bytes 4640 | tf_op jit(solution)/shard_map/ppermute | solution.py:457
  28.4 0.7 broadcast_in_dim.22
  29.2 6.2 %all-to-all-start = ((f32[32,1,1152]{2,1,0:T(1,128)}), f32[32,1,1152]{2,1,0:T(1,128)S(1)}, u32[]{:S(2)}, u32[]{:S(2)}) async-start(f32[32,1,1152]{2,1,0:T(1,128)} %broadcast_in_dim.22), calls=%async_computation | async-start | bytes 294912 | tf_op jit(solution)/shard_map/all_to_all | solution.py:463
  35.4 0.0 collective-permute-done.7.refs_5_.refs_6_
  35.4 0.0 collective-permute-done.6.refs_3_.refs_4_
  35.4 0.0 collective-permute-done.4.refs_0_.refs_1_
  35.4 0.0 collective-permute-done.5.refs_2_.refs_3_
  35.4 1.2 %strips.1 = (f32[2,136,128]{2,1,0:T(8,128)S(1)}, f32[2,136,128]{2,1,0:T(8,128)S(1)}) custom-call(f32[9,64,128]{2,1,0:T(8,128)S(1)} %collective-permute-done.4.refs_0_.refs_1_, f32[16,64,128]{2,1,0:T(8,128)S(1)} %get-tuple-element.24.refs_1_.refs_2_, f32[9,64,128]{2,1,0:T(8,128)S(1)} %collective-permute-done.5.refs_2_.refs_3_, ...), custom_call_target="tpu_custom_call" | custom-call | tf_op jit(solution)/shard_map/strips/pallas_call | solution.py:440
  36.6 1.8 %collective-permute-start.8 = (f32[2,136,128]{2,1,0:T(8,128)S(1)}, f32[2,136,128]{2,1,0:T(8,128)S(1)}, u32[]{:S(2)}, u32[]{:S(2)}) collective-permute-start(f32[2,136,128]{2,1,0:T(8,128)S(1)} %get-tuple-element.26), channel_id=1, source_target_pairs={{0,8},{8,16},{16,24},{24,0},{1,9},{9,17},{17,25},{25,1},{2,10},{10... | collective-permute-start | bytes 417800 | tf_op jit(solution)/shard_map/ppermute | solution.py:475
  38.4 2.1 %collective-permute-start.9 = (f32[2,136,128]{2,1,0:T(8,128)S(1)}, f32[2,136,128]{2,1,0:T(8,128)S(1)}, u32[]{:S(2)}, u32[]{:S(2)}) collective-permute-start(f32[2,136,128]{2,1,0:T(8,128)S(1)} %get-tuple-element.27), channel_id=1, source_target_pairs={{8,0},{16,8},{24,16},{0,24},{9,1},{17,9},{25,17},{1,25},{10,2},{18... | collective-permute-start | bytes 417800 | tf_op jit(solution)/shard_map/ppermute | solution.py:476
  40.5 3.4 %all-to-all-done.parts_ref = f32[32,1,1152]{2,1,0:T(1,128)S(1)} async-done(((f32[32,1,1152]{2,1,0:T(1,128)}), f32[32,1,1152]{2,1,0:T(1,128)S(1)}, u32[]{:S(2)}, u32[]{:S(2)}) %all-to-all-start) | async-done | bytes 147488 | tf_op jit(solution)/shard_map/all_to_all | solution.py:463
  43.9 2.4 %modes.3 = (f32[48,64]{1,0:T(8,128)S(1)}, f32[64,64]{1,0:T(8,128)S(1)}) custom-call(f32[32,1,1152]{2,1,0:T(1,128)S(1)} %all-to-all-done.parts_ref, f32[48,64]{1,0:T(8,128)S(1)} %start.1.refs_5_.rows_ref), custom_call_target="tpu_custom_call" | custom-call | tf_op jit(solution)/shard_map/modes/pallas_call | solution.py:440
  46.3 0.0 collective-permute-done.8.refs_7_
  46.3 1.2 %collective-permute-done.9.refs_8_ = f32[2,136,128]{2,1,0:T(8,128)S(1)} collective-permute-done((f32[2,136,128]{2,1,0:T(8,128)S(1)}, f32[2,136,128]{2,1,0:T(8,128)S(1)}, u32[]{:S(2)}, u32[]{:S(2)}) %collective-permute-start.9) | collective-permute-done | bytes 139296 | tf_op jit(solution)/shard_map/ppermute | solution.py:476
  47.5 4.6 %sweep0.1 = (f32[34,64,256]{2,1,0:T(8,128)S(1)}, f32[34,64,256]{2,1,0:T(8,128)S(1)}, f32[34,1,256]{2,1,0:T(1,128)S(1)}, f32[34,64,256]{2,1,0:T(8,128)S(1)}, f32[2,1,1152]{2,1,0:T(1,128)S(1)}) custom-call(f32[64,64]{1,0:T(8,128)S(1)} %get-tuple-element.22.refs_0_, f32[9,64,128]{2,1,0:T(8,128)S(1)} %collective-permute-done.4.refs_0_.refs_1_, ...), custom_call_target="tpu_custom_call" | custom-call | tf_op jit(solution)/shard_map/sweep0/pallas_call | solution.py:440
  52.2 0.1 collective-permute-start.10
  52.3 1.2 %collective-permute-done.10 = f32[1,1,1152]{2,1,0:T(1,128)S(1)} collective-permute-done((f32[1,1,1152]{2,1,0:T(1,128)S(1)}, f32[1,1,1152]{2,1,0:T(1,128)S(1)}, u32[]{:S(2)}, u32[]{:S(2)}) %collective-permute-start.10) | collective-permute-done | bytes 4640 | tf_op jit(solution)/shard_map/ppermute | solution.py:457
  53.5 0.1 broadcast_in_dim.24
  53.5 12.2 %all_to_all.15.parts_ref = f32[32,1,1152]{2,1,0:T(1,128)S(1)} all-to-all(f32[32,1,1152]{2,1,0:T(1,128)S(1)} %broadcast_in_dim.24), channel_id=1, replica_groups=mesh['wide'=4,'band'=8] {'wide','band'}, dimensions={0} | all-to-all | bytes 294912 | tf_op jit(solution)/shard_map/all_to_all | solution.py:463
  65.7 2.6 %modes.4 = (f32[48,64]{1,0:T(8,128)S(1)}, f32[64,64]{1,0:T(8,128)S(1)}) custom-call(f32[32,1,1152]{2,1,0:T(1,128)S(1)} %all_to_all.15.parts_ref, f32[48,64]{1,0:T(8,128)S(1)} %get-tuple-element.29.rows_ref), custom_call_target="tpu_custom_call" | custom-call | tf_op jit(solution)/shard_map/modes/pallas_call | solution.py:440
  68.3 3.9 %sweep1.1 = (f32[34,64,256]{2,1,0:T(8,128)S(1)}, f32[2,1,1152]{2,1,0:T(1,128)S(1)}) custom-call(f32[64,64]{1,0:T(8,128)S(1)} %get-tuple-element.30.last_ref, f32[34,64,256]{2,1,0:T(8,128)S(1)} %get-tuple-element.31.f_ref, f32[34,64,256]{2,1,0:T(8,128)S(1)} %get-tuple-element.32.seen_ref, f32[34,64,256]{2,1,0:T(8,128)S(1)} %get-tuple-element.33.gap_ref, ...), custom_call_target="tpu_custom_call" | custom-call | tf_op jit(solution)/shard_map/sweep1/pallas_call | solution.py:440
  72.2 0.3 collective-permute-start.11
  72.6 0.9 %collective-permute-done.11 = f32[1,1,1152]{2,1,0:T(1,128)S(1)} collective-permute-done((f32[1,1,1152]{2,1,0:T(1,128)S(1)}, f32[1,1,1152]{2,1,0:T(1,128)S(1)}, u32[]{:S(2)}, u32[]{:S(2)}) %collective-permute-start.11) | collective-permute-done | bytes 4640 | tf_op jit(solution)/shard_map/ppermute | solution.py:457
  73.5 0.1 broadcast_in_dim.26
  73.6 10.3 %all_to_all.16.parts_ref = f32[32,1,1152]{2,1,0:T(1,128)S(1)} all-to-all(f32[32,1,1152]{2,1,0:T(1,128)S(1)} %broadcast_in_dim.26), channel_id=1, replica_groups=mesh['wide'=4,'band'=8] {'wide','band'}, dimensions={0} | all-to-all | bytes 294912 | tf_op jit(solution)/shard_map/all_to_all | solution.py:463
  83.9 3.0 %modes.5 = (f32[48,64]{1,0:T(8,128)}, f32[64,64]{1,0:T(8,128)S(1)}) custom-call(f32[32,1,1152]{2,1,0:T(1,128)S(1)} %all_to_all.16.parts_ref, f32[48,64]{1,0:T(8,128)S(1)} %get-tuple-element.36.rows_ref), custom_call_target="tpu_custom_call" | custom-call | tf_op jit(solution)/shard_map/modes/pallas_call | solution.py:440
  86.9 3.1 %sweep2.1 = f32[64,16,128]{2,1,0:T(8,128)} custom-call(f32[64,64]{1,0:T(8,128)S(1)} %get-tuple-element.37.last_ref, f32[34,64,256]{2,1,0:T(8,128)S(1)} %get-tuple-element.38.f_ref, f32[34,64,256]{2,1,0:T(8,128)S(1)} %get-tuple-element.32.seen_ref, f32[34,64,256]{2,1,0:T(8,128)S(1)} %get-tuple-element.33.gap_ref, f32[34,1,256]{2,1,0:T(1,128)S(1)} %get-tuple-element.34.diff_ref), custom_call_target="tpu_custom_call" | custom-call | tf_op jit(solution)/shard_map/sweep2/pallas_call | solution.py:440
  (6 shorter events, 0.1 us)
Async XLA Ops:
  0.6 14.7 %copy-start.1 = (f32[64,48]{0,1:T(8,128)S(1)}, f32[64,48]{0,1:T(8,128)}, u32[]{:S(2)}) copy-start(f32[64,48]{0,1:T(8,128)} %param.9) | copy-start | bytes 36868
  1.8 18.4 %collective-permute-start.2 = (f32[16,16,128]{2,1,0:T(8,128)S(1)}, f32[16,16,128]{2,1,0:T(8,128)S(1)}, u32[]{:S(2)}, u32[]{:S(2)}) collective-permute-start(f32[16,16,128]{2,1,0:T(8,128)S(1)} %get-tuple-element.42), channel_id=1, source_target_pairs={{0,24},{8,16},{16,8},{24,0},{1,25},{9,17},{17,9},{25,1},{2,26},{10... | collective-permute-start | bytes 393224 | tf_op jit(solution)/shard_map/ppermute | solution.py:490
  7.0 13.3 %collective-permute-start = (f32[16,16,128]{2,1,0:T(8,128)S(1)}, f32[16,16,128]{2,1,0:T(8,128)S(1)}, u32[]{:S(2)}, u32[]{:S(2)}) collective-permute-start(f32[16,16,128]{2,1,0:T(8,128)S(1)} %get-tuple-element.43), channel_id=1, source_target_pairs={{0,8},{8,0},{16,24},{24,16},{1,9},{9,1},{17,25},{25,17},{2,10},{10... | collective-permute-start | bytes 393224 | tf_op jit(solution)/shard_map/ppermute | solution.py:490
  7.0 13.3 %collective-permute-start.1 = (f32[16,16,128]{2,1,0:T(8,128)S(1)}, f32[16,16,128]{2,1,0:T(8,128)S(1)}, u32[]{:S(2)}, u32[]{:S(2)}) collective-permute-start(f32[16,16,128]{2,1,0:T(8,128)S(1)} %get-tuple-element.45), channel_id=1, source_target_pairs={{0,16},{8,24},{16,0},{24,8},{1,17},{9,25},{17,1},{25,9},{2,18},{10... | collective-permute-start | bytes 393224 | tf_op jit(solution)/shard_map/ppermute | solution.py:490
  7.6 1.0 %copy-start = (s32[64,16,128]{2,1,0:T(8,128)S(1)}, s32[64,16,128]{2,1,0:T(8,128)}, u32[]{:S(2)}) copy-start(s32[64,16,128]{2,1,0:T(8,128)} %obs_ref.1) | copy-start | bytes 1572868
  8.6 0.7 copy-start.2
  9.3 0.7 copy-start.3
  11.0 24.4 %collective-permute-start.7 = (f32[9,72,128]{2,1,0:T(8,128)}, f32[9,72,128]{2,1,0:T(8,128)S(1)}, u32[]{:S(2)}, u32[]{:S(2)}) collective-permute-start(f32[9,72,128]{2,1,0:T(8,128)} %get-tuple-element.40), channel_id=1, source_target_pairs={{1,0},{2,1},{3,2},{4,3},{5,4},{6,5},{7,6},{9,8},{10,9},{11,10},{12... | collective-permute-start | bytes 995336 | tf_op jit(solution)/shard_map/ppermute | solution.py:469
  12.3 23.1 %collective-permute-start.6 = (f32[9,72,128]{2,1,0:T(8,128)S(1)}, f32[9,72,128]{2,1,0:T(8,128)S(1)}, u32[]{:S(2)}, u32[]{:S(2)}) collective-permute-start(f32[9,72,128]{2,1,0:T(8,128)S(1)} %get-tuple-element.41), channel_id=1, source_target_pairs={{0,1},{1,2},{2,3},{3,4},{4,5},{5,6},{6,7},{8,9},{9,10},{10,11},{11... | collective-permute-start | bytes 995336 | tf_op jit(solution)/shard_map/ppermute | solution.py:468
  21.8 13.6 %collective-permute-start.4 = (f32[9,64,128]{2,1,0:T(8,128)S(1)}, f32[9,64,128]{2,1,0:T(8,128)S(1)}, u32[]{:S(2)}, u32[]{:S(2)}) collective-permute-start(f32[9,64,128]{2,1,0:T(8,128)S(1)} %get-tuple-element.23), channel_id=1, source_target_pairs={{0,1},{1,2},{2,3},{3,4},{4,5},{5,6},{6,7},{8,9},{9,10},{10,11},{11... | collective-permute-start | bytes 884744 | tf_op jit(solution)/shard_map/ppermute | solution.py:468
  24.9 10.5 %collective-permute-start.5 = (f32[9,64,128]{2,1,0:T(8,128)S(1)}, f32[9,64,128]{2,1,0:T(8,128)S(1)}, u32[]{:S(2)}, u32[]{:S(2)}) collective-permute-start(f32[9,64,128]{2,1,0:T(8,128)S(1)} %get-tuple-element.25), channel_id=1, source_target_pairs={{1,0},{2,1},{3,2},{4,3},{5,4},{6,5},{7,6},{9,8},{10,9},{11,10},{12... | collective-permute-start | bytes 884744 | tf_op jit(solution)/shard_map/ppermute | solution.py:469
  26.2 2.2 %collective-permute-start.3 = (f32[1,1,1152]{2,1,0:T(1,128)S(1)}, f32[1,1,1152]{2,1,0:T(1,128)S(1)}, u32[]{:S(2)}, u32[]{:S(2)}) collective-permute-start(f32[1,1,1152]{2,1,0:T(1,128)S(1)} %constant_dynamic-slice_fusion.2), channel_id=1, source_target_pairs={{0,1},{1,0},{2,3},{3,2},{4,5},{5,4},{6,7},{7,6},{8,9},{9,8},{10,11... | collective-permute-start | bytes 13832 | tf_op jit(solution)/shard_map/ppermute | solution.py:457
  29.2 14.7 %all-to-all-start = ((f32[32,1,1152]{2,1,0:T(1,128)}), f32[32,1,1152]{2,1,0:T(1,128)S(1)}, u32[]{:S(2)}, u32[]{:S(2)}) async-start(f32[32,1,1152]{2,1,0:T(1,128)} %broadcast_in_dim.22), calls=%async_computation | async-start | bytes 294912 | tf_op jit(solution)/shard_map/all_to_all | solution.py:463
  36.6 9.7 %collective-permute-start.8 = (f32[2,136,128]{2,1,0:T(8,128)S(1)}, f32[2,136,128]{2,1,0:T(8,128)S(1)}, u32[]{:S(2)}, u32[]{:S(2)}) collective-permute-start(f32[2,136,128]{2,1,0:T(8,128)S(1)} %get-tuple-element.26), channel_id=1, source_target_pairs={{0,8},{8,16},{16,24},{24,0},{1,9},{9,17},{17,25},{25,1},{2,10},{10... | collective-permute-start | bytes 417800 | tf_op jit(solution)/shard_map/ppermute | solution.py:475
  38.4 9.1 %collective-permute-start.9 = (f32[2,136,128]{2,1,0:T(8,128)S(1)}, f32[2,136,128]{2,1,0:T(8,128)S(1)}, u32[]{:S(2)}, u32[]{:S(2)}) collective-permute-start(f32[2,136,128]{2,1,0:T(8,128)S(1)} %get-tuple-element.27), channel_id=1, source_target_pairs={{8,0},{16,8},{24,16},{0,24},{9,1},{17,9},{25,17},{1,25},{10,2},{18... | collective-permute-start | bytes 417800 | tf_op jit(solution)/shard_map/ppermute | solution.py:476
  52.2 1.2 %collective-permute-start.10 = (f32[1,1,1152]{2,1,0:T(1,128)S(1)}, f32[1,1,1152]{2,1,0:T(1,128)S(1)}, u32[]{:S(2)}, u32[]{:S(2)}) collective-permute-start(f32[1,1,1152]{2,1,0:T(1,128)S(1)} %constant_dynamic-slice_fusion.1), channel_id=1, source_target_pairs={{0,1},{1,0},{2,3},{3,2},{4,5},{5,4},{6,7},{7,6},{8,9},{9,8},{10,11... | collective-permute-start | bytes 13832 | tf_op jit(solution)/shard_map/ppermute | solution.py:457
  72.2 1.2 %collective-permute-start.11 = (f32[1,1,1152]{2,1,0:T(1,128)S(1)}, f32[1,1,1152]{2,1,0:T(1,128)S(1)}, u32[]{:S(2)}, u32[]{:S(2)}) collective-permute-start(f32[1,1,1152]{2,1,0:T(1,128)S(1)} %constant_dynamic-slice_fusion), channel_id=1, source_target_pairs={{0,1},{1,0},{2,3},{3,2},{4,5},{5,4},{6,7},{7,6},{8,9},{9,8},{10,11... | collective-permute-start | bytes 13832 | tf_op jit(solution)/shard_map/ppermute | solution.py:457
